TPU v7x, 32 devices: a whole 2x2x4 slice. The times are simulated.
32 devices in a mesh: seq: 4 (over y, core), head: 8 (over z, x).
Axes of the slice: x: 2, y: 2, z: 4, core: 2. Of those that a mesh axis runs over, the one named last changes fastest.
Arguments:
- queries: bfloat16 [1024, 512], P('seq', 'head'), may hold values from -6 to 6
- key_rows: bfloat16 [1024, 512], P('seq', 'head'), may hold values from -6 to 6
- values: bfloat16 [1024, 1024], P('seq', 'head'), may hold values from -6 to 6
- log_decay: float32 [8, 1024], P('head', 'seq'), may hold values from -0.8 to 0, as said below
- beta_rate: float32 [8, 1024], P('head', 'seq'), may hold values from 0 to 0.95, as said below
- start_states: float32 [4, 8, 128, 128], P('seq', 'head'), may hold values from -4 to 4
- output_grad: bfloat16 [1024, 1024], P('seq', 'head'), may hold values from -6 to 6
Outputs:
- query_grad: float32 [1024, 512], P('seq', 'head')
- key_grad: float32 [1024, 512], P('seq', 'head')
- value_grad: float32 [1024, 1024], P('seq', 'head')
- rate_grad: float32 [8, 1024], P('head', 'seq')
Inputs may be any that keep to these rules, and one draw needn't show every extreme that they name: `log_decay`: every entry is at most zero. `beta_rate`: every entry is positive.
All inputs are finite; a program needn't handle non-finite values.
Results may differ from a plain program's by a relative error of at most 0.00035.
Values may be sent and summed in bfloat16 or wider, within the bound.
No kernel may reach another device: no remote copies, remote signals or barrier semaphores. Data moves between devices by JAX's collectives and lax.ppermute only.
A program may use at most 64 MiB of HBM per device.

v0:
```python
import jax
import jax.numpy as jnp
from jax import lax
from jax.sharding import PartitionSpec as P

SPAN = 64


PRECISE = lax.Precision.HIGHEST


def partner(x, axis, apart):
    return lax.ppermute(x, axis, [(i, i ^ 1 << apart) for i in range(lax.axis_size(axis))])


def from_behind(block, axis, distance):
    devices = range(lax.axis_size(axis))
    route = [(i - distance, i) for i in devices if i - distance in devices]
    return lax.ppermute(block, axis, route)


def unit_rows(rows, factor):
    return rows * (factor / jnp.sqrt(jnp.sum(rows * rows, -1, keepdims=True) + 1e-06))


def product(left, right):
    return jnp.dot(left, right, precision=PRECISE)


def compose_chain(operators):
    while operators.shape[0] > 1:
        paired_count = operators.shape[0] // 2 * 2
        joined = jnp.einsum(
            "nij,njk->nik",
            operators[0:paired_count:2],
            operators[1:paired_count:2],
            precision=PRECISE,
        )
        if operators.shape[0] > paired_count:
            joined = jnp.concatenate([joined, operators[paired_count:]], 0)
        operators = joined
    return operators[0]


def block_forward(state, query_in, key_in, value_in, rate_in, decay, width):
    length, key_width = key_in.shape
    block_count = length // width
    query_norm = unit_rows(query_in, key_width ** (-0.5)).reshape(block_count, width, key_width)
    key_norm = unit_rows(key_in, 1.0).reshape(block_count, width, key_width)
    value_blocks = value_in.reshape(block_count, width, -1)
    rates = rate_in.reshape(block_count, width)
    cumulated = jnp.cumsum(decay.reshape(block_count, width), axis=1)
    spread = cumulated[:, :, None] - cumulated[:, None, :]
    row_ids = lax.broadcasted_iota(jnp.int32, (width, width), 0)
    col_ids = lax.broadcasted_iota(jnp.int32, (width, width), 1)
    strict = jnp.exp(jnp.where(col_ids < row_ids, spread, -1e30))
    causal = jnp.exp(jnp.where(col_ids <= row_ids, spread, -1e30))
    inner_keys = jnp.einsum("nid,njd->nij", key_norm, key_norm, precision=PRECISE)
    nilpotent = -(rates[:, :, None] * inner_keys * strict)
    eye_block = jnp.eye(width, dtype=jnp.float32)
    inverse = eye_block + nilpotent
    power = nilpotent
    reach = 2
    while reach < width:
        power = jnp.einsum("nij,njk->nik", power, power, precision=PRECISE)
        inverse = jnp.einsum("nij,njk->nik", inverse, eye_block + power, precision=PRECISE)
        reach = reach * 2
    growth = jnp.exp(cumulated)
    tail = jnp.exp(cumulated[:, -1:] - cumulated)
    right_side = jnp.concatenate(
        [(rates * growth)[:, :, None] * key_norm, rates[:, :, None] * value_blocks], -1
    )
    solved = jnp.einsum("nij,njd->nid", inverse, right_side, precision=PRECISE)
    w_part = solved[:, :, :key_width]
    u_base = solved[:, :, key_width:]
    key_tail = tail[:, :, None] * key_norm
    ends = jnp.exp(cumulated[:, -1])
    block_ops = ends[:, None, None] * jnp.eye(key_width, dtype=jnp.float32) - jnp.einsum(
        "nci,ncj->nij", w_part, key_tail, precision=PRECISE
    )
    block_adds = jnp.einsum("ncv,nck->nvk", u_base, key_tail, precision=PRECISE)

    def advance(carried, pieces):
        operator, addend = pieces
        return (product(carried, operator) + addend, carried)

    final, starts = lax.scan(advance, state, (block_ops, block_adds))
    updates = u_base - jnp.einsum("nck,nvk->ncv", w_part, starts, precision=PRECISE)
    scores = jnp.einsum("nid,njd->nij", query_norm, key_norm, precision=PRECISE) * causal
    outputs = growth[:, :, None] * jnp.einsum("nck,nvk->ncv", query_norm, starts, precision=PRECISE)
    outputs = outputs + jnp.einsum("nij,njv->niv", scores, updates, precision=PRECISE)
    return ((outputs.reshape(length, -1), final), compose_chain(block_ops))


def per_device(queries, key_rows, values, log_decay, beta_rate, start_states, output_grad):
    parity = lax.axis_index("head") % 2
    is_first = parity == 0
    other_query, other_key = partner((queries, key_rows), "head", 0)
    whole_query = jnp.where(
        is_first,
        jnp.concatenate([queries, other_query], 1),
        jnp.concatenate([other_query, queries], 1),
    ).astype(jnp.float32)
    whole_key = jnp.where(
        is_first,
        jnp.concatenate([key_rows, other_key], 1),
        jnp.concatenate([other_key, key_rows], 1),
    ).astype(jnp.float32)
    half_width = queries.shape[1]
    value_in = values.astype(jnp.float32)
    grad_out = output_grad.astype(jnp.float32)
    decay_row = log_decay[0]
    state = start_states[0, 0]

    def forward_fn(state_arg, query_arg, key_arg, value_arg, rate_arg):
        return block_forward(state_arg, query_arg, key_arg, value_arg, rate_arg, decay_row, SPAN)

    _, pullback, transition = jax.vjp(
        forward_fn, state, whole_query, whole_key, value_in, beta_rate[0], has_aux=True
    )
    zero_state = jnp.zeros_like(state)
    local_part = pullback((grad_out, zero_state))
    own_map = transition.T
    own_shift = local_part[0]

    def pass_back(turn_index, carried):
        return from_behind(product(carried, own_map) + own_shift, "seq", -1)

    incoming = lax.fori_loop(0, lax.axis_size("seq") - 1, pass_back, zero_state)
    far_part = pullback((jnp.zeros_like(grad_out), incoming))
    query_total = local_part[1] + far_part[1]
    key_total = local_part[2] + far_part[2]
    value_grad = local_part[3] + far_part[3]
    rate_grad = (local_part[4] + far_part[4])[None, :]
    own_start = parity * half_width
    other_start = (1 - parity) * half_width
    sent_query = lax.dynamic_slice_in_dim(query_total, other_start, half_width, 1)
    sent_key = lax.dynamic_slice_in_dim(key_total, other_start, half_width, 1)
    partner_query, partner_key = partner((sent_query, sent_key), "head", 0)
    query_grad = lax.dynamic_slice_in_dim(query_total, own_start, half_width, 1) + partner_query
    key_grad = lax.dynamic_slice_in_dim(key_total, own_start, half_width, 1) + partner_key
    return (query_grad, key_grad, value_grad, rate_grad)


def solution(mesh):
    in_specs = (
        P("seq", "head"),
        P("seq", "head"),
        P("seq", "head"),
        P("head", "seq"),
        P("head", "seq"),
        P("seq", "head", None, None),
        P("seq", "head"),
    )
    out_specs = (P("seq", "head"), P("seq", "head"), P("seq", "head"), P("head", "seq"))
    return jax.shard_map(
        per_device, mesh=mesh, in_specs=in_specs, out_specs=out_specs, check_vma=False
    )
```

profile of v0, /device:TPU:1, one launch (start us, length us, event | category | flops | bytes accessed | tf_op | source)
XLA Modules:
  0.0 105.3 jit_solution(16496143836358696040)
XLA Ops:
  0.6 2.1 %collective-permute-start.2 = (bf16[256,64]{0,1:T(8,128)(2,1)}, bf16[256,64]{0,1:T(8,128)(2,1)S(1)}, u32[]{:S(2)}, u32[]{:S(2)}) collective-permute-start(bf16[256,64]{0,1:T(8,128)(2,1)} %param.15), channel_id=1, source_target_pairs={{0,1},{1,0},{2,3},{3,2},{4,5},{5,4},{6,7},{7,6},{8,9},{9,8},{10,11... | collective-permute-start | bytes 98312 | tf_op jit(solution)/shard_map/ppermute | solution.py:13
  17.2 1.6 %while.59 = (s32[]{:T(128)}, f32[128,128]{0,1:T(8,128)S(1)}, f32[4,128,128]{1,2,0:T(8,128)S(1)}, f32[4,128,128]{2,1,0:T(8,128)S(1)}, f32[4,128,128]{1,2,0:T(8,128)S(1)}, /*index=5*/s32[]{:T(128)}) while((s32[]{:T(128)}, f32[128,128]{0,1:T(8,128)S(1)}, f32[4,128,128]{1,2,0:T(8,128)S(1)}, f32[4,128,128]{2,1,0:T(8,128)S(1)}, ...), condition=%wide.region_3.4_spmd, body=%wide.region_2.3_spmd.sunk | while | flops 25182208 | bytes 525393 | solution.py:87
  21.9 1.3 %fusion.84 = (f32[4,64]{1,0:T(4,128)S(1)}, f32[4,64]{1,0:T(4,128)S(1)}, bf16[4,64,128]{2,1,0:T(8,128)(2,1)S(1)}, f32[4,64,128]{2,1,0:T(8,128)}) fusion(f32[4,64,128]{2,1,0:T(8,128)S(1)} %convolution_add_fusion.9, bf16[4,64,64]{2,1,0:T(8,128)(2,1)S(1)} %bitcast.228, bf16[4,64,64]{2,1,0:T(8,128)(2,1)S(1)} %bitcast.229, pred[]{:T(512)S(6)} %eq.31, ...), kind=kOutput, calls=%fused_computation.149 | convolution fusion | flops 50888192 | bytes 855041 | tf_op jit(solution)/shard_map/transpose(jvp(nck,nvk->ncv))/dot_general | solution.py:90
  26.5 1.4 %fusion.51 = f32[4,128,128]{2,1,0:T(8,128)} fusion(bf16[4,64,128]{2,1,0:T(8,128)(2,1)S(1)} %get-tuple-element.473, f32[4,64]{1,0:T(4,128)S(1)} %div.45, f32[4,64]{1,0:T(4,128)S(1)} %get-tuple-element.479), kind=kOutput, calls=%fused_computation.111 | convolution fusion | flops 50397184 | bytes 329728 | tf_op jit(solution)/shard_map/transpose(jvp(nck,nvk->ncv))/dot_general | solution.py:90
  28.6 1.3 %fusion.100 = f32[4,64,128]{2,1,0:T(8,128)} fusion(f32[4,128,128]{1,2,0:T(8,128)S(1)} %get-tuple-element.414, f32[4,64,128]{2,1,0:T(8,128)S(1)} %fusion.217), kind=kOutput, calls=%fused_computation.169 | convolution fusion | flops 50364416 | bytes 524288 | tf_op jit(solution)/shard_map/transpose(jvp(nck,nvk->ncv))/dot_general | solution.py:88
  29.9 1.3 %convolution_add_fusion.2 = f32[4,128,128]{2,1,0:T(8,128)} fusion(f32[4,128,128]{2,1,0:T(8,128)S(1)} %fusion.53, f32[4,64,128]{2,1,0:T(8,128)S(1)} %fusion.217, f32[4,64,256]{2,1,0:T(8,128)S(1)} %fusion.73), kind=kOutput, calls=%fused_computation.40 | convolution fusion | flops 50429952 | bytes 786432 | tf_op jit(solution)/shard_map/transpose(jvp(nck,nvk->ncv))/dot_general | solution.py:88
  31.2 6.1 %while.62 = (s32[]{:T(128)}, f32[128,128]{0,1:T(8,128)S(1)}, f32[4,128,128]{2,1,0:T(8,128)S(1)}, f32[4,128,128]{1,2,0:T(8,128)S(1)}, f32[4,128,128]{2,1,0:T(8,12...) while((s32[]{:T(128)}, f32[128,128]{0,1:T(8,128)S(1)}, ...), condition=%wide.region_8.9_spmd.clone, body=%wide.region_7.8_spmd.clone.sunk | while | flops 50397188 | bytes 984720 | solution.py:87
  37.8 1.3 %fusion.132 = f32[4,64,128]{2,1,0:T(8,128)} fusion(f32[4,128,128]{1,2,0:T(8,128)S(1)} %get-tuple-element.339, f32[4,64,256]{2,1,0:T(8,128)S(1)} %fusion.73), kind=kOutput, calls=%fused_computation.201 | convolution fusion | flops 50331648 | bytes 524288 | tf_op jit(solution)/shard_map/transpose(jvp(ncv,nck->nvk))/dot_general | solution.py:81
  40.1 1.1 %fusion.48 = f32[4,64,256]{2,1,0:T(8,128)} fusion(f32[4,64,64]{2,1,0:T(8,128)S(1)} %fusion.216, f32[4,64,128]{2,1,0:T(8,128)S(1)} %convolution_add_fusion.6, f32[4,64,128]{2,1,0:T(8,128)S(1)} %convolution_add_fusion.7), kind=kOutput, calls=%fused_computation.98 | convolution fusion | flops 50397184 | bytes 589824 | tf_op jit(solution)/shard_map/transpose(jvp(nij,njd->nid))/dot_general | solution.py:73
  42.8 1.3 %fusion.95 = f32[4,64,128]{2,1,0:T(8,128)} fusion(f32[4,128,128]{1,2,0:T(8,128)S(1)} %get-tuple-element.414, f32[4,64,128]{2,1,0:T(8,128)S(1)} %fusion.147), kind=kOutput, calls=%fused_computation.164 | convolution fusion | flops 50364416 | bytes 524288 | tf_op jit(solution)/shard_map/transpose(jvp(nck,nvk->ncv))/dot_general | solution.py:88
  44.1 1.3 %convolution_add_fusion.1 = f32[4,128,128]{2,1,0:T(8,128)} fusion(f32[4,128,128]{2,1,0:T(8,128)S(1)} %copy-done.19, f32[4,64,128]{2,1,0:T(8,128)S(1)} %fusion.147, f32[4,64,256]{2,1,0:T(8,128)S(1)} %fusion.73), kind=kOutput, calls=%fused_computation.39 | convolution fusion | flops 50429952 | bytes 786432 | tf_op jit(solution)/shard_map/transpose(jvp(nck,nvk->ncv))/dot_general | solution.py:88
  45.5 18.2 %while.60 = (s32[]{:T(128)}, f32[128,128]{1,0:T(8,128)S(1)}, f32[128,128]{1,0:T(8,128)S(1)}, f32[128,128]{1,0:T(8,128)S(1)}, s32[]{:T(128)}) while((s32[]{:T(128)}, f32[128,128]{1,0:T(8,128)S(1)}, f32[128,128]{1,0:T(8,128)S(1)}, f32[128,128]{1,0:T(8,128)S(1)}, s32[]{:T(128)}) %tuple.133), condition=%wide.region_11.12_spmd, body=%wide.region_10.11_spmd.sunk | while | flops 25182208 | bytes 524389 | solution.py:129
  45.7 2.9 %collective-permute-start = (f32[128,128]{1,0:T(8,128)S(1)}, f32[128,128]{1,0:T(8,128)S(1)}, u32[]{:S(2)}, u32[]{:S(2)}) collective-permute-start(f32[128,128]{1,0:T(8,128)S(1)} %convolution_add_fusion.33), channel_id=1, source_target_pairs={{8,0},{16,8},{24,16},{9,1},{17,9},{25,17},{10,2},{18,10},{26,18},{... | collective-permute-start | bytes 196616 | tf_op jit(solution)/shard_map/while/body/eval_jaxpr/ppermute | solution.py:19
  48.6 3.5 %collective-permute-done = f32[128,128]{1,0:T(8,128)S(1)} collective-permute-done((f32[128,128]{1,0:T(8,128)S(1)}, f32[128,128]{1,0:T(8,128)S(1)}, u32[]{:S(2)}, u32[]{:S(2)}) %collective-permute-start) | collective-permute-done | bytes 65568 | tf_op jit(solution)/shard_map/while/body/eval_jaxpr/ppermute | solution.py:19
  52.3 1.9 %collective-permute-start = (f32[128,128]{1,0:T(8,128)S(1)}, f32[128,128]{1,0:T(8,128)S(1)}, u32[]{:S(2)}, u32[]{:S(2)}) collective-permute-start(f32[128,128]{1,0:T(8,128)S(1)} %convolution_add_fusion.33), channel_id=1, source_target_pairs={{8,0},{16,8},{24,16},{9,1},{17,9},{25,17},{10,2},{18,10},{26,18},{... | collective-permute-start | bytes 196616 | tf_op jit(solution)/shard_map/while/body/eval_jaxpr/ppermute | solution.py:19
  54.2 3.7 %collective-permute-done = f32[128,128]{1,0:T(8,128)S(1)} collective-permute-done((f32[128,128]{1,0:T(8,128)S(1)}, f32[128,128]{1,0:T(8,128)S(1)}, u32[]{:S(2)}, u32[]{:S(2)}) %collective-permute-start) | collective-permute-done | bytes 65568 | tf_op jit(solution)/shard_map/while/body/eval_jaxpr/ppermute | solution.py:19
  58.1 1.9 %collective-permute-start = (f32[128,128]{1,0:T(8,128)S(1)}, f32[128,128]{1,0:T(8,128)S(1)}, u32[]{:S(2)}, u32[]{:S(2)}) collective-permute-start(f32[128,128]{1,0:T(8,128)S(1)} %convolution_add_fusion.33), channel_id=1, source_target_pairs={{8,0},{16,8},{24,16},{9,1},{17,9},{25,17},{10,2},{18,10},{26,18},{... | collective-permute-start | bytes 196616 | tf_op jit(solution)/shard_map/while/body/eval_jaxpr/ppermute | solution.py:19
  60.0 3.7 %collective-permute-done = f32[128,128]{1,0:T(8,128)S(1)} collective-permute-done((f32[128,128]{1,0:T(8,128)S(1)}, f32[128,128]{1,0:T(8,128)S(1)}, u32[]{:S(2)}, u32[]{:S(2)}) %collective-permute-start) | collective-permute-done | bytes 65568 | tf_op jit(solution)/shard_map/while/body/eval_jaxpr/ppermute | solution.py:19
  63.8 6.3 %while.61 = (s32[]{:T(128)}, f32[128,128]{0,1:T(8,128)S(1)}, f32[4,128,128]{2,1,0:T(8,128)S(1)}, f32[4,128,128]{1,2,0:T(8,128)S(1)}, f32[4,128,128]{2,1,0:T(8,12...) while((s32[]{:T(128)}, f32[128,128]{0,1:T(8,128)S(1)}, ...), condition=%wide.region_13.14_spmd, body=%wide.region_12.13_spmd.sunk | while | flops 50348032 | bytes 984181 | solution.py:87
  72.1 1.1 %fusion.50 = f32[4,64,256]{2,1,0:T(8,128)} fusion(f32[4,64,64]{2,1,0:T(8,128)S(1)} %fusion.216, f32[4,64,128]{2,1,0:T(8,128)S(1)} %convolution_add_fusion.3, f32[4,64,128]{2,1,0:T(8,128)S(1)} %convolution_add_fusion.4), kind=kOutput, calls=%fused_computation.100 | convolution fusion | flops 50397184 | bytes 589824 | tf_op jit(solution)/shard_map/transpose(jvp(nij,njd->nid))/dot_general | solution.py:73
  73.2 1.3 %fusion.130 = f32[4,64,128]{2,1,0:T(8,128)} fusion(f32[4,128,128]{1,2,0:T(8,128)S(1)} %get-tuple-element.343, f32[4,64,256]{2,1,0:T(8,128)S(1)} %fusion.73), kind=kOutput, calls=%fused_computation.199 | convolution fusion | flops 50331648 | bytes 524288 | tf_op jit(solution)/shard_map/transpose(jvp(ncv,nck->nvk))/dot_general | solution.py:81
  96.9 1.3 %collective-permute-start.3 = (f32[256,64]{0,1:T(8,128)S(1)}, f32[256,64]{0,1:T(8,128)S(1)}, u32[]{:S(2)}, u32[]{:S(2)}) collective-permute-start(f32[256,64]{0,1:T(8,128)S(1)} %constant_dynamic-slice_fusion.3), channel_id=1, source_target_pairs={{0,1},{1,0},{2,3},{3,2},{4,5},{5,4},{6,7},{7,6},{8,9},{9,8},{10,11... | collective-permute-start | bytes 196616 | tf_op jit(solution)/shard_map/ppermute | solution.py:13
  98.6 1.1 %fusion.79 = (f32[4,64]{1,0:T(4,128)S(1)}, f32[4,64]{1,0:T(4,128)S(1)}, f32[4,64]{1,0:T(4,128)S(1)}, f32[4,64]{1,0:T(4,128)S(1)}, f32[4,64]{1,0:T(4,128)S(1)}, /...) fusion(bf16[4,64,128]{2,1,0:T(8,128)(2,1)S(1)} %get-tuple-element.475, ...), kind=kOutput, calls=%fused_computation.144 | convolution fusion | flops 51182080 | bytes 1980416 | tf_op jit(solution)/shard_map/transpose(jvp(nci,ncj->nij))/dot_general | solution.py:78
  103.0 1.6 %collective-permute-done.4 = f32[256,64]{0,1:T(8,128)S(1)} collective-permute-done((f32[256,64]{0,1:T(8,128)S(1)}, f32[256,64]{0,1:T(8,128)S(1)}, u32[]{:S(2)}, u32[]{:S(2)}) %collective-permute-start.4) | collective-permute-done | bytes 65568 | tf_op jit(solution)/shard_map/ppermute | solution.py:13
  (286 shorter events, 66.2 us)
Async XLA Ops:
  0.6 4.9 %copy-start.37 = (bf16[256,128]{1,0:T(8,128)(2,1)S(1)}, bf16[256,128]{1,0:T(8,128)(2,1)}, u32[]{:S(2)}) copy-start(bf16[256,128]{1,0:T(8,128)(2,1)} %param.17) | copy-start | bytes 196612
  0.6 7.5 %collective-permute-start.2 = (bf16[256,64]{0,1:T(8,128)(2,1)}, bf16[256,64]{0,1:T(8,128)(2,1)S(1)}, u32[]{:S(2)}, u32[]{:S(2)}) collective-permute-start(bf16[256,64]{0,1:T(8,128)(2,1)} %param.15), channel_id=1, source_target_pairs={{0,1},{1,0},{2,3},{3,2},{4,5},{5,4},{6,7},{7,6},{8,9},{9,8},{10,11... | collective-permute-start | bytes 98312 | tf_op jit(solution)/shard_map/ppermute | solution.py:13
  2.7 5.4 %collective-permute-start.1 = (bf16[256,64]{0,1:T(8,128)(2,1)}, bf16[256,64]{0,1:T(8,128)(2,1)S(1)}, u32[]{:S(2)}, u32[]{:S(2)}) collective-permute-start(bf16[256,64]{0,1:T(8,128)(2,1)} %param.16), channel_id=1, source_target_pairs={{0,1},{1,0},{2,3},{3,2},{4,5},{5,4},{6,7},{7,6},{8,9},{9,8},{10,11... | collective-permute-start | bytes 98312 | tf_op jit(solution)/shard_map/ppermute | solution.py:13
  8.1 13.7 %copy-start.35 = (bf16[256,64]{0,1:T(8,128)(2,1)}, bf16[256,64]{0,1:T(8,128)(2,1)S(1)}, u32[]{:S(2)}) copy-start(bf16[256,64]{0,1:T(8,128)(2,1)S(1)} %collective-permute-done.2) | copy-start | bytes 98308
  10.9 1.7 %copy-start.4 = (f32[4,64,64]{1,2,0:T(8,128)}, f32[4,64,64]{1,2,0:T(8,128)S(1)}, u32[]{:S(2)}) copy-start(f32[4,64,64]{1,2,0:T(8,128)S(1)} %copy.104) | copy-start | bytes 196612
  11.0 1.2 %copy-start.2 = (f32[4,64,64]{1,2,0:T(8,128)}, f32[4,64,64]{1,2,0:T(8,128)S(1)}, u32[]{:S(2)}) copy-start(f32[4,64,64]{1,2,0:T(8,128)S(1)} %copy.102) | copy-start | bytes 196612
  11.2 2.0 %copy-start.6 = (f32[4,64,64]{1,2,0:T(8,128)}, f32[4,64,64]{1,2,0:T(8,128)S(1)}, u32[]{:S(2)}) copy-start(f32[4,64,64]{1,2,0:T(8,128)S(1)} %copy.106) | copy-start | bytes 196612
  21.8 1.4 %copy-start.16 = (f32[4,64,128]{2,1,0:T(8,128)}, f32[4,64,128]{2,1,0:T(8,128)S(1)}, u32[]{:S(2)}) copy-start(f32[4,64,128]{2,1,0:T(8,128)S(1)} %convolution_add_fusion.9) | copy-start | bytes 393220
  26.2 17.9 %copy-start.14 = (f32[4,64,128]{2,1,0:T(8,128)}, f32[4,64,128]{2,1,0:T(8,128)S(1)}, u32[]{:S(2)}) copy-start(f32[4,64,128]{2,1,0:T(8,128)S(1)} %fusion.147) | copy-start | bytes 393220
  37.7 1.3 %copy-start.28 = (f32[4,64,128]{2,1,0:T(8,128)S(1)}, f32[4,64,128]{2,1,0:T(8,128)}, u32[]{:S(2)}) copy-start(f32[4,64,128]{2,1,0:T(8,128)} %fusion.100) | copy-start | bytes 393220
  42.8 1.3 %copy-start.19 = (f32[4,128,128]{2,1,0:T(8,128)S(1)}, f32[4,128,128]{2,1,0:T(8,128)}, u32[]{:S(2)}) copy-start(f32[4,128,128]{2,1,0:T(8,128)} %fusion.51) | copy-start | bytes 786436
  45.7 6.4 %collective-permute-start = (f32[128,128]{1,0:T(8,128)S(1)}, f32[128,128]{1,0:T(8,128)S(1)}, u32[]{:S(2)}, u32[]{:S(2)}) collective-permute-start(f32[128,128]{1,0:T(8,128)S(1)} %convolution_add_fusion.33), channel_id=1, source_target_pairs={{8,0},{16,8},{24,16},{9,1},{17,9},{25,17},{10,2},{18,10},{26,18},{... | collective-permute-start | bytes 196616 | tf_op jit(solution)/shard_map/while/body/eval_jaxpr/ppermute | solution.py:19
  52.3 5.6 %collective-permute-start = (f32[128,128]{1,0:T(8,128)S(1)}, f32[128,128]{1,0:T(8,128)S(1)}, u32[]{:S(2)}, u32[]{:S(2)}) collective-permute-start(f32[128,128]{1,0:T(8,128)S(1)} %convolution_add_fusion.33), channel_id=1, source_target_pairs={{8,0},{16,8},{24,16},{9,1},{17,9},{25,17},{10,2},{18,10},{26,18},{... | collective-permute-start | bytes 196616 | tf_op jit(solution)/shard_map/while/body/eval_jaxpr/ppermute | solution.py:19
  58.1 5.6 %collective-permute-start = (f32[128,128]{1,0:T(8,128)S(1)}, f32[128,128]{1,0:T(8,128)S(1)}, u32[]{:S(2)}, u32[]{:S(2)}) collective-permute-start(f32[128,128]{1,0:T(8,128)S(1)} %convolution_add_fusion.33), channel_id=1, source_target_pairs={{8,0},{16,8},{24,16},{9,1},{17,9},{25,17},{10,2},{18,10},{26,18},{... | collective-permute-start | bytes 196616 | tf_op jit(solution)/shard_map/while/body/eval_jaxpr/ppermute | solution.py:19
  63.8 6.3 %copy-start.15 = (f32[4,64,128]{2,1,0:T(8,128)S(1)}, f32[4,64,128]{2,1,0:T(8,128)}, u32[]{:S(2)}) copy-start(f32[4,64,128]{2,1,0:T(8,128)} %copy-done.14) | copy-start | bytes 393220
  96.8 1.4 %copy-start.21 = (f32[4,64,256]{2,1,0:T(8,128)S(1)}, f32[4,64,256]{2,1,0:T(8,128)}, u32[]{:S(2)}) copy-start(f32[4,64,256]{2,1,0:T(8,128)} %fusion.50) | copy-start | bytes 786436
  96.8 1.4 %copy-start.26 = (f32[4,64,128]{2,1,0:T(8,128)S(1)}, f32[4,64,128]{2,1,0:T(8,128)}, u32[]{:S(2)}) copy-start(f32[4,64,128]{2,1,0:T(8,128)} %fusion.130) | copy-start | bytes 393220
  96.8 1.4 %copy-start.24 = (f32[4,64,128]{2,1,0:T(8,128)S(1)}, f32[4,64,128]{2,1,0:T(8,128)}, u32[]{:S(2)}) copy-start(f32[4,64,128]{2,1,0:T(8,128)} %fusion.52) | copy-start | bytes 393220
  96.9 1.7 %copy-start.22 = (f32[4,64,256]{2,1,0:T(8,128)S(1)}, f32[4,64,256]{2,1,0:T(8,128)}, u32[]{:S(2)}) copy-start(f32[4,64,256]{2,1,0:T(8,128)} %fusion.48) | copy-start | bytes 786436
  96.9 1.7 %copy-start.29 = (f32[4,64,128]{2,1,0:T(8,128)S(1)}, f32[4,64,128]{2,1,0:T(8,128)}, u32[]{:S(2)}) copy-start(f32[4,64,128]{2,1,0:T(8,128)} %fusion.54) | copy-start | bytes 393220
  96.9 1.7 %copy-start.30 = (f32[4,64,128]{2,1,0:T(8,128)S(1)}, f32[4,64,128]{2,1,0:T(8,128)}, u32[]{:S(2)}) copy-start(f32[4,64,128]{2,1,0:T(8,128)} %fusion.132) | copy-start | bytes 393220
  96.9 1.7 %copy-start.38 = (bf16[256,128]{1,0:T(8,128)(2,1)S(1)}, bf16[256,128]{1,0:T(8,128)(2,1)}, u32[]{:S(2)}) copy-start(bf16[256,128]{1,0:T(8,128)(2,1)} %param.17) | copy-start | bytes 196612
  96.9 5.5 %collective-permute-start.3 = (f32[256,64]{0,1:T(8,128)S(1)}, f32[256,64]{0,1:T(8,128)S(1)}, u32[]{:S(2)}, u32[]{:S(2)}) collective-permute-start(f32[256,64]{0,1:T(8,128)S(1)} %constant_dynamic-slice_fusion.3), channel_id=1, source_target_pairs={{0,1},{1,0},{2,3},{3,2},{4,5},{5,4},{6,7},{7,6},{8,9},{9,8},{10,11... | collective-permute-start | bytes 196616 | tf_op jit(solution)/shard_map/ppermute | solution.py:13
  101.5 3.2 %collective-permute-start.4 = (f32[256,64]{0,1:T(8,128)S(1)}, f32[256,64]{0,1:T(8,128)S(1)}, u32[]{:S(2)}, u32[]{:S(2)}) collective-permute-start(f32[256,64]{0,1:T(8,128)S(1)} %constant_dynamic-slice_fusion.2), channel_id=1, source_target_pairs={{0,1},{1,0},{2,3},{3,2},{4,5},{5,4},{6,7},{7,6},{8,9},{9,8},{10,11... | collective-permute-start | bytes 196616 | tf_op jit(solution)/shard_map/ppermute | solution.py:13
  (25 other events, 20.2 us)
where the time goes:
time: 106 us; the launch traced here: 105 us
  matrix products  52.3 us (49%)
  local copies, waits for them, and re-layouts  23.1 us (22%)
  waiting for transfers between devices  12.5 us (12%)
  starting transfers between devices  11.1 us (10%)
  other arithmetic  3.51 us (3%)
  between operations  1.78 us (2%)
  loops' own time  1.08 us (1%)
    unnamed x89, local copies, waits for them, and re-layouts  12.6 us
    ppermute x3, waiting for transfers between devices, from_behind(): return lax.ppermute(block, axis, route)  10.8 us
    dot_general x25, matrix products, block_forward(): power = jnp.einsum('nij,njk->nik', power, power, precision=PRECISE)  9.66 us
    dot_general x25, matrix products, block_forward(): jnp.einsum('nij,njk->nik', inverse, eye_block + power, precision=PRECISE)  9.05 us
    dynamic_slice x16, local copies, waits for them, and re-layouts, block_forward(): final, starts = lax.scan(advance, state, (block_ops, block_adds))  7.54 us
    ppermute x3, starting transfers between devices, from_behind(): return lax.ppermute(block, axis, route)  6.7 us
    dot_general x23, matrix products, product(): return jnp.dot(left, right, precision=PRECISE)  5.77 us
    dot_general x5, matrix products, block_forward(): jnp.einsum('nck,nvk->ncv', w_part, starts, precision=PRECISE)  5.49 us
  transfers between devices with their start and end apart: 7, of which 4 were waited for; matrix products, arithmetic and copies ran while one was open for 6% of the time, Pallas kernels for 0%

commit v1 on v0

v1 whole, which is shorter than its diff:
```python
import jax
import jax.numpy as jnp
from jax import lax
from jax.experimental import pallas as pl
from jax.experimental.pallas import tpu as pltpu
from jax.sharding import PartitionSpec as P

F32 = jnp.float32
BF16 = jnp.bfloat16
BASE = 16
NN = (((1,), (0,)), ((), ()))
NT = (((1,), (1,)), ((), ()))


def split(x):
    high = x.astype(BF16)
    return (high, (x - high.astype(F32)).astype(BF16))


def mm(left, right, dims=NN):
    left = left if isinstance(left, tuple) else (left if left.dtype == BF16 else split(left))
    right = right if isinstance(right, tuple) else (right if right.dtype == BF16 else split(right))

    def one(a, b):
        return lax.dot_general(a, b, dims, preferred_element_type=F32)

    if isinstance(left, tuple) and isinstance(right, tuple):
        return one(left[0], right[0]) + (one(left[0], right[1]) + one(left[1], right[0]))
    if isinstance(left, tuple):
        return one(left[0], right) + one(left[1], right)
    if isinstance(right, tuple):
        return one(left, right[0]) + one(left, right[1])
    return one(left, right)


def ids(shape):
    return lax.broadcasted_iota(jnp.int32, shape, 0), lax.broadcasted_iota(jnp.int32, shape, 1)


def to_col(row, eye):
    return jnp.sum(jnp.where(eye, row, 0.0), 1, keepdims=True)


def to_row(col, eye):
    return jnp.sum(jnp.where(eye, col, 0.0), 0, keepdims=True)


def base_inverse(nil, base):
    size = nil.shape[0]
    count = size // base
    row, lane = ids((base, size))
    block = lane // base
    packed = jnp.zeros((base, size), F32)
    for b in range(count):
        packed = jnp.where(block == b, nil[b * base : (b + 1) * base, :], packed)
    solved = jnp.where(row == lane % base, 1.0, 0.0)
    for j in range(base - 1):
        factor = jnp.take_along_axis(packed, block * base + j, axis=1)
        factor = jnp.where(row > j, factor, 0.0)
        solved = solved + factor * solved[j : j + 1, :]
    return jnp.concatenate([jnp.where(block == b, solved, 0.0) for b in range(count)], 0)


def half_inverse(nil):
    size = nil.shape[0]
    row, lane = ids((size, size))
    inv = base_inverse(nil, BASE)
    width = BASE
    while width < size:
        factor = 4 if size >= 4 * width else 2
        wide = width * factor
        off = jnp.where((row // wide == lane // wide) & (row // width != lane // width), nil, 0.0)
        inv_s = split(inv)
        step = split(mm(inv_s, off))
        first = inv + mm(step, inv_s)
        if factor == 4:
            first = first + mm(mm(step, step), first)
        inv = first
        width = wide
    return inv


def inverse(nil):
    size = nil.shape[0]
    half = size // 2
    upper = half_inverse(nil[:half, :half])
    lower = half_inverse(nil[half:, half:])
    corner = mm(mm(lower, nil[half:, :half]), upper)
    top = jnp.concatenate([upper, jnp.zeros((half, half), F32)], 1)
    return jnp.concatenate([top, jnp.concatenate([corner, lower], 1)], 0)


def decays(decay_row, row, lane):
    cum_col = jnp.sum(jnp.where(lane <= row, decay_row, 0.0), 1, keepdims=True)
    return cum_col, to_row(cum_col, row == lane)


def map_kernel(q_ref, k_ref, other_ref, g_ref, decay_ref, rate_ref, map_ref, inv_ref, low_ref, score_ref, rows_ref):
    half, length = q_ref.shape
    q_t = jnp.concatenate([q_ref[...], other_ref[0:half, :]], 0)
    k_t = jnp.concatenate([k_ref[...], other_ref[half:, :]], 0)
    width = q_t.shape[0]
    row, lane = ids((length, length))
    eye = row == lane
    cum_col, cum_row = decays(decay_ref[...], row, lane)
    q_f, k_f = q_t.astype(F32), k_t.astype(F32)
    q_scale = width ** (-0.5) / jnp.sqrt(jnp.sum(q_f * q_f, 0, keepdims=True) + 1e-6)
    k_scale = 1.0 / jnp.sqrt(jnp.sum(k_f * k_f, 0, keepdims=True) + 1e-6)
    rate_row = rate_ref[...]
    k_rows = k_f.T.astype(BF16)
    q_rows = q_f.T.astype(BF16)
    spread = jnp.exp(jnp.where(lane <= row, cum_col - cum_row, -1e30))
    low = jnp.where(lane < row, spread, 0.0) * (mm(k_rows, k_t) * (to_col(k_scale, eye) * k_scale))
    inv = inverse(-(to_col(rate_row, eye) * low))
    score = spread * (mm(q_rows, k_t) * (to_col(q_scale, eye) * k_scale))
    grow = jnp.exp(cum_row)
    last = cum_row[:, length - 1 :]
    tail = jnp.exp(last - cum_row)
    w_t = mm(k_t, inv * (rate_row * grow * k_scale), NT)
    side = q_f * (q_scale * grow) - mm(w_t, score, NT)
    w_row, w_lane = ids((width, width))
    map_ref[0:width, :] = jnp.where(w_row == w_lane, jnp.exp(last), 0.0) - mm(w_t * (tail * k_scale), k_rows)
    map_ref[width:, :] = mm(side, g_ref[...])
    inv_ref[...] = inv
    low_ref[...] = low
    score_ref[...] = score
    rows_ref[...] = jnp.concatenate([cum_row, q_scale, k_scale, tail, grow, rate_row, cum_row, cum_row], 0)


def join_kernel(flag_ref, own_ref, got_ref, total_ref, ahead_ref):
    width = own_ref.shape[1]
    low = flag_ref[0] == 1
    own, got = own_ref[...], got_ref[...]
    first = jnp.where(low, own[0:width, :], got[0:width, :])
    second = jnp.where(low, got[width:, :], own[width:, :])
    third = jnp.where(low, own[width:, :], got[width:, :])
    total_ref[...] = mm(first, second) + third
    row, lane = ids((2 * width, width))
    ahead_ref[...] = jnp.where(low, got, jnp.where(row == lane, 1.0, 0.0))


def local_kernel(
    q_ref, k_ref, other_ref, v_ref, g_ref, start_ref, inv_ref, low_ref, score_ref, rows_ref, flag_ref, after_ref,
    u_ref, ut_ref, y_ref, psi_ref, psit_ref, w_ref, sym_ref, dq_ref, dk_ref, start_t_ref,
):
    half, length = q_ref.shape
    q_t = jnp.concatenate([q_ref[...], other_ref[0:half, :]], 0)
    k_t = jnp.concatenate([k_ref[...], other_ref[half:, :]], 0)
    width = q_t.shape[0]
    row, lane = ids((length, length))
    eye = row == lane
    rows = rows_ref[...]
    cum_row, q_scale, k_scale, tail, grow, rate_row = (rows[i : i + 1, :] for i in range(6))
    cum_col = to_col(cum_row, eye)
    q_f, k_f = q_t.astype(F32), k_t.astype(F32)
    k_rows = k_f.T.astype(BF16)
    start = start_ref[...]
    start = jnp.where(flag_ref[0] == 1, start, pltpu.roll(start, half, 1))
    start_t = start.T
    start_ts = split(start_t)
    value = v_ref[...].astype(F32)
    grad = g_ref[...]
    grad_t = grad.astype(F32).T.astype(BF16)
    inv = inv_ref[...]
    base = value - to_col(grow * k_scale, eye) * mm(k_rows, start, NT)
    u = mm(inv * rate_row, base)
    u_s = split(u)
    u_t = u.T
    u_ts = split(u_t)
    w_ref[...] = base - mm(low_ref[...], u_s)
    inv_s = split(inv)
    y_t = mm(mm(grad_t, score_ref[...]), inv_s)
    psi_t = mm(k_t, inv * to_col(tail * k_scale, eye))
    y = y_t.T
    y_ts = split(y_t)
    y_s = split(y)
    both = jnp.exp(-jnp.abs(cum_col - cum_row))
    rate_col = to_col(rate_row, eye)
    decay_low = jnp.where(lane < row, both * -rate_col, 0.0)
    decay_up = jnp.where(lane > row, both * -rate_row, 0.0)
    sym = decay_low * mm(y_s, u_ts) + decay_up * mm(u_s, y_ts)
    d_score = mm(grad, u_ts) * jnp.where(lane <= row, both, 0.0)
    k_n = k_f * k_scale
    q_n = q_f * q_scale
    dq = mm(k_t, d_score * k_scale, NT) + grow * mm(start_ts, grad_t)
    unit = q_f * (q_scale * width**0.5)
    dq_ref[...] = q_scale * (dq - unit * jnp.sum(unit * dq, 0, keepdims=True))
    dk_ref[...] = mm(k_n, sym) + mm(q_n, d_score) - mm(start_ts, y_t * (grow * rate_row))
    u_ref[...] = u
    ut_ref[...] = u_t
    y_ref[...] = y
    psi_ref[...] = psi_t.T
    psit_ref[...] = psi_t
    sym_ref[...] = decay_low + decay_up
    start_t_ref[...] = start_t


def far_kernel(
    flag_ref, got_ref, ahead_ref, k_ref, other_ref, u_ref, ut_ref, y_ref, psi_ref, psit_ref, w_ref, sym_ref, dq_ref,
    dk_ref, start_t_ref, rows_ref, send_ref, keep_ref, value_ref, rate_out_ref,
):
    half, length = k_ref.shape
    k_t = jnp.concatenate([k_ref[...], other_ref[half:, :]], 0)
    width = k_t.shape[0]
    row, lane = ids((length, length))
    eye = row == lane
    rows = rows_ref[...]
    k_scale, tail, grow, rate_row = (rows[i : i + 1, :] for i in range(2, 6))
    ahead = ahead_ref[...]
    got = jnp.where(flag_ref[1] == 1, got_ref[...], 0.0)
    far_t = split(mm(ahead[0:width, :], got) + ahead[width:, :])
    u_s = split(u_ref[...])
    psi_s = split(psi_ref[...])
    psi_t = psit_ref[...]
    uz_t = mm(far_t, ut_ref[...])
    uz = mm(u_s, far_t, NT)
    sz = mm(start_t_ref[...], far_t, NT)
    y = y_ref[...] + mm(psi_s, far_t)
    sym = sym_ref[...] * jnp.where(lane < row, mm(psi_s, uz_t), mm(uz, psi_t))
    k_n = k_t.astype(F32) * k_scale
    dk = dk_ref[...] + mm(k_n, sym) + tail * uz_t - mm(sz, psi_t * (grow * rate_row))
    dk = k_scale * (dk - k_n * jnp.sum(k_n * dk, 0, keepdims=True))
    dq = dq_ref[...]
    keep_ref[...] = jnp.concatenate([dq[0:half, :], dk[0:half, :]], 0)
    send_ref[...] = jnp.concatenate([dq[half:, :], dk[half:, :]], 0)
    value_ref[...] = to_col(rate_row, eye) * y
    rate_out_ref[...] = to_row(jnp.sum(y * w_ref[...], 1, keepdims=True), eye)


def add_kernel(keep_ref, got_ref, q_ref, k_ref):
    half = q_ref.shape[0]
    q_ref[...] = keep_ref[0:half, :] + got_ref[0:half, :]
    k_ref[...] = keep_ref[half:, :] + got_ref[half:, :]


def call(kernel, outs, *args, smem=()):
    return pl.pallas_call(
        kernel,
        out_shape=tuple(jax.ShapeDtypeStruct(shape, F32) for shape in outs),
        in_specs=[
            pl.BlockSpec(memory_space=pltpu.SMEM if i in smem else pltpu.VMEM) for i in range(len(args))
        ],
        out_specs=tuple(pl.BlockSpec(memory_space=pltpu.VMEM) for _ in outs),
        compiler_params=pltpu.CompilerParams(vmem_limit_bytes=24 << 20),
    )(*args)


def swap(x, axis, apart):
    return lax.ppermute(x, axis, [(i, i ^ 1 << apart) for i in range(lax.axis_size(axis))])


def per_device(queries, key_rows, values, log_decay, beta_rate, start_states, output_grad):
    count = lax.axis_size("seq")
    stages = count.bit_length() - 1
    assert count == 1 << stages and stages >= 2
    place = lax.axis_index("seq")
    parity = lax.axis_index("head") % 2
    q_t, k_t = queries.T, key_rows.T
    half, length = q_t.shape
    width = 2 * half
    depth = values.shape[1]
    start = start_states[0, 0]
    other = swap(jnp.concatenate([q_t, k_t], 0), "head", 0)

    section, inv, low, score, rows = call(
        map_kernel,
        [(2 * width, depth), (length, length), (length, length), (length, length), (8, length)],
        q_t, k_t, other, output_grad, log_decay, beta_rate,
    )

    def flags(bit):
        return jnp.stack([1 - (place >> bit) % 2, parity * 0]).astype(jnp.int32)

    got = swap(section, "seq", 0)
    if stages == 2:
        total, ahead = call(
            join_kernel, [(width, depth), (2 * width, depth)], flags(0), section, got, smem=(0,)
        )
    else:
        precise = lax.Precision.HIGHEST
        dot = lambda a, b: jnp.dot(a, b, precision=precise)
        ahead = jnp.concatenate([jnp.eye(width, dtype=F32), jnp.zeros((width, depth), F32)], 0)
        for bit in range(stages - 1):
            if bit:
                got = swap(section, "seq", bit)
            is_low = (place >> bit) % 2 == 0
            upper = jnp.where(is_low, got, section)
            lower = jnp.where(is_low, section, got)
            ahead_low = jnp.concatenate(
                [dot(ahead[:width], got[:width]), dot(ahead[:width], got[width:]) + ahead[width:]], 0
            )
            ahead = jnp.where(is_low, ahead_low, ahead)
            section = jnp.concatenate(
                [dot(lower[:width], upper[:width]), dot(lower[:width], upper[width:]) + lower[width:]], 0
            )
        total = section[width:]
    arrived = swap(total, "seq", stages - 1)

    head_flags = jnp.stack([1 - parity, 1 - (place >> (stages - 1)) % 2]).astype(jnp.int32)
    u, u_t, y, psi, psi_t, w, sym, dq, dk, start_t = call(
        local_kernel,
        [(length, depth), (depth, length), (length, depth), (length, width), (width, length), (length, depth),
         (length, length), (width, length), (width, length), (width, depth)],
        q_t, k_t, other, values, output_grad, start, inv, low, score, rows, head_flags, total, smem=(10,),
    )
    send, keep, value_grad, rate_grad = call(
        far_kernel,
        [(width, length), (width, length), (length, depth), (1, length)],
        head_flags, arrived, ahead, k_t, other, u, u_t, y, psi, psi_t, w, sym, dq, dk, start_t, rows, smem=(0,),
    )
    query_grad, key_grad = call(add_kernel, [(half, length), (half, length)], keep, swap(send, "head", 0))
    return (query_grad.T, key_grad.T, value_grad, rate_grad)


def solution(mesh):
    in_specs = (
        P("seq", "head"),
        P("seq", "head"),
        P("seq", "head"),
        P("head", "seq"),
        P("head", "seq"),
        P("seq", "head", None, None),
        P("seq", "head"),
    )
    out_specs = (P("seq", "head"), P("seq", "head"), P("seq", "head"), P("head", "seq"))
    return jax.shard_map(
        per_device, mesh=mesh, in_specs=in_specs, out_specs=out_specs, check_vma=False
    )
```

time: 106 us -> 24.6 us (0.23)
  the two profiles are of different devices: /device:TPU:1 before, /device:TPU:0 now
where the time goes in v1:
time: 24.6 us; the launch traced here: 24.5 us
  Pallas kernels  8.8 us (36%)
  waiting for transfers between devices  7.17 us (29%)
  starting transfers between devices  6.73 us (27%)
  other arithmetic  0.97 us (4%)
  between operations  0.76 us (3%)
    pallas_call x5, Pallas kernels, call(): pl.pallas_call(kernel, out_shape=tuple((jax.ShapeDtypeStruct(shape, F32)...  8.8 us
    ppermute x4, waiting for transfers between devices, swap(): lax.ppermute(x, axis, [(i, i ^ 1 << apart) for i in range(lax.axis_size(a...  7.17 us
    ppermute x4, starting transfers between devices, swap(): lax.ppermute(x, axis, [(i, i ^ 1 << apart) for i in range(lax.axis_size(a...  6.73 us
    concatenate x1, other arithmetic, per_device(): other = swap(jnp.concatenate([q_t, k_t], 0), 'head', 0)  0.82 us
  transfers between devices with their start and end apart: 4, of which 3 were waited for; matrix products, arithmetic and copies ran while one was open for 1% of the time, Pallas kernels for 10%

profile of v1, /device:TPU:0, one launch (start us, length us, event | category | flops | bytes accessed | tf_op | source)
XLA Modules:
  0.0 24.5 jit_solution(10071706081794556635)
XLA Ops:
  0.6 0.0 copy-start.6
  0.6 0.0 copy-start.5
  0.7 0.0 copy-start
  0.7 0.0 copy-start.1
  0.7 0.0 copy-start.2
  0.7 0.8 %pad_maximum_fusion = bf16[128,256]{1,0:T(8,128)(2,1)S(1)} fusion(bf16[64,256]{1,0:T(8,128)(2,1)} %bitcast.8, bf16[64,256]{1,0:T(8,128)(2,1)} %bitcast.12), kind=kLoop, calls=%fused_computation | loop fusion | flops 131072 | bytes 131072 | tf_op jit(solution)/shard_map/concatenate | solution.py:263
  1.5 3.0 %collective-permute-start = (bf16[128,256]{1,0:T(8,128)(2,1)S(1)}, bf16[128,256]{1,0:T(8,128)(2,1)S(1)}, u32[]{:S(2)}, u32[]{:S(2)}) collective-permute-start(bf16[128,256]{1,0:T(8,128)(2,1)S(1)} %pad_maximum_fusion), channel_id=1, source_target_pairs={{0,1},{1,0},{2,3},{3,2},{4,5},{5,4},{6,7},{7,6},{8,9},{9,8},{10,11... | collective-permute-start | bytes 196616 | tf_op jit(solution)/shard_map/ppermute | solution.py:249
  4.5 2.2 %collective-permute-done.other_ref = bf16[128,256]{1,0:T(8,128)(2,1)S(1)} collective-permute-done((bf16[128,256]{1,0:T(8,128)(2,1)S(1)}, bf16[128,256]{1,0:T(8,128)(2,1)S(1)}, u32[]{:S(2)}, u32[]{:S(2)}) %collective-permute-start) | collective-permute-done | bytes 65568 | tf_op jit(solution)/shard_map/ppermute | solution.py:249
  6.7 0.0 copy-done.6
  6.7 0.0 copy-done.5
  6.7 2.8 %shard_map.102 = (f32[256,128]{1,0:T(8,128)S(1)}, f32[256,256]{1,0:T(8,128)S(1)}, f32[256,256]{1,0:T(8,128)S(1)}, f32[256,256]{1,0:T(8,128)S(1)}, f32[8,256]{1,0:T(8,128)S(1)}) custom-call(bf16[64,256]{1,0:T(8,128)(2,1)S(1)} %bitcast.13, bf16[64,256]{1,0:T(8,128)(2,1)S(1)} %bitcast.9, bf16[128,256]{1,0:T(8,128)(2,1)S(1)} %collective-permute-done.other_ref, ...), custom_call_target="tpu_custom_call" | custom-call | tf_op jit(solution)/shard_map/pallas_call | solution.py:237
  9.5 0.1 collective-permute-start.1
  9.6 0.1 pad_add_fusion.1.flag_ref
  9.7 1.2 %collective-permute-done.1.got_ref = f32[256,128]{1,0:T(8,128)S(1)} collective-permute-done((f32[256,128]{1,0:T(8,128)S(1)}, f32[256,128]{1,0:T(8,128)S(1)}, u32[]{:S(2)}, u32[]{:S(2)}) %collective-permute-start.1) | collective-permute-done | bytes 131104 | tf_op jit(solution)/shard_map/ppermute | solution.py:249
  10.9 0.7 %shard_map.103 = (f32[128,128]{1,0:T(8,128)S(1)}, f32[256,128]{1,0:T(8,128)S(1)}) custom-call(s32[2]{0:T(128)S(1)} %pad_add_fusion.1.flag_ref, f32[256,128]{1,0:T(8,128)S(1)} %get-tuple-element.27.own_ref, f32[256,128]{1,0:T(8,128)S(1)} %collective-permute-done.1.got_ref), custom_call_target="tpu_custom_call" | custom-call | tf_op jit(solution)/shard_map/pallas_call | solution.py:237
  11.7 2.1 %collective-permute-start.2 = (f32[128,128]{1,0:T(8,128)S(1)}, f32[128,128]{1,0:T(8,128)S(1)}, u32[]{:S(2)}, u32[]{:S(2)}) collective-permute-start(f32[128,128]{1,0:T(8,128)S(1)} %get-tuple-element.28.after_ref), channel_id=1, source_target_pairs={{0,16},{8,24},{16,0},{24,8},{1,17},{9,25},{17,1},{25,9},{2,18},{10... | collective-permute-start | bytes 196616 | tf_op jit(solution)/shard_map/ppermute | solution.py:249
  13.8 0.1 pad_add_fusion.flag_ref
  13.8 0.0 copy-done.3
  13.8 2.5 %shard_map.104 = (f32[256,128]{1,0:T(8,128)S(1)}, f32[128,256]{1,0:T(8,128)S(1)}, f32[256,128]{1,0:T(8,128)S(1)}, f32[256,128]{1,0:T(8,128)S(1)}, f32[128,256]{1...) custom-call(bf16[64,256]{1,0:T(8,128)(2,1)S(1)} %bitcast.14, ...), custom_call_target="tpu_custom_call" | custom-call | tf_op jit(solution)/shard_map/pallas_call | solution.py:237
  16.4 0.0 collective-permute-done.2.got_ref
  16.4 2.1 %shard_map.105 = (f32[128,256]{1,0:T(8,128)S(1)}, f32[128,256]{1,0:T(8,128)S(1)}, f32[256,128]{1,0:T(8,128)}, f32[1,256]{1,0:T(1,128)}) custom-call(s32[2]{0:T(128)S(1)} %pad_add_fusion.flag_ref, f32[128,128]{1,0:T(8,128)S(1)} %collective-permute-done.2.got_ref, f32[256,128]{1,0:T(8,128)S(1)} %get-tuple-element.29.ahead_ref, bf16[64,256]{1,0:T(8,128)(2,1)S(1)} %bitcast.11, ...), custom_call_target="tpu_custom_call" | custom-call | tf_op jit(solution)/shard_map/pallas_call | solution.py:237
  18.5 1.6 %collective-permute-start.3 = (f32[128,256]{1,0:T(8,128)S(1)}, f32[128,256]{1,0:T(8,128)S(1)}, u32[]{:S(2)}, u32[]{:S(2)}) collective-permute-start(f32[128,256]{1,0:T(8,128)S(1)} %get-tuple-element.45), channel_id=1, source_target_pairs={{0,1},{1,0},{2,3},{3,2},{4,5},{5,4},{6,7},{7,6},{8,9},{9,8},{10,11... | collective-permute-start | bytes 393224 | tf_op jit(solution)/shard_map/ppermute | solution.py:249
  20.1 3.7 %collective-permute-done.3.got_ref = f32[128,256]{1,0:T(8,128)S(1)} collective-permute-done((f32[128,256]{1,0:T(8,128)S(1)}, f32[128,256]{1,0:T(8,128)S(1)}, u32[]{:S(2)}, u32[]{:S(2)}) %collective-permute-start.3) | collective-permute-done | bytes 131104 | tf_op jit(solution)/shard_map/ppermute | solution.py:249
  23.8 0.7 %shard_map.106 = (f32[64,256]{1,0:T(8,128)}, f32[64,256]{1,0:T(8,128)}) custom-call(f32[128,256]{1,0:T(8,128)S(1)} %get-tuple-element.44.keep_ref, f32[128,256]{1,0:T(8,128)S(1)} %collective-permute-done.3.got_ref), custom_call_target="tpu_custom_call" | custom-call | tf_op jit(solution)/shard_map/pallas_call | solution.py:237
  (6 shorter events, 0.0 us)
Async XLA Ops:
  0.6 6.1 %copy-start.6 = (f32[1,256]{1,0:T(1,128)S(1)}, f32[1,256]{1,0:T(1,128)}, u32[]{:S(2)}) copy-start(f32[1,256]{1,0:T(1,128)} %rate_ref.1) | copy-start | bytes 3076
  0.6 6.1 %copy-start.5 = (f32[1,256]{1,0:T(1,128)S(1)}, f32[1,256]{1,0:T(1,128)}, u32[]{:S(2)}) copy-start(f32[1,256]{1,0:T(1,128)} %decay_ref.1) | copy-start | bytes 3076
  0.7 6.1 %copy-start = (bf16[256,64]{0,1:T(8,128)(2,1)S(1)}, bf16[256,64]{0,1:T(8,128)(2,1)}, u32[]{:S(2)}) copy-start(bf16[256,64]{0,1:T(8,128)(2,1)} %param.8) | copy-start | bytes 98308
  0.7 6.1 %copy-start.1 = (bf16[256,64]{0,1:T(8,128)(2,1)S(1)}, bf16[256,64]{0,1:T(8,128)(2,1)}, u32[]{:S(2)}) copy-start(bf16[256,64]{0,1:T(8,128)(2,1)} %param.7) | copy-start | bytes 98308
  0.7 6.1 %copy-start.2 = (bf16[256,128]{1,0:T(8,128)(2,1)S(1)}, bf16[256,128]{1,0:T(8,128)(2,1)}, u32[]{:S(2)}) copy-start(bf16[256,128]{1,0:T(8,128)(2,1)} %g_ref.3) | copy-start | bytes 196612
  1.5 5.2 %collective-permute-start = (bf16[128,256]{1,0:T(8,128)(2,1)S(1)}, bf16[128,256]{1,0:T(8,128)(2,1)S(1)}, u32[]{:S(2)}, u32[]{:S(2)}) collective-permute-start(bf16[128,256]{1,0:T(8,128)(2,1)S(1)} %pad_maximum_fusion), channel_id=1, source_target_pairs={{0,1},{1,0},{2,3},{3,2},{4,5},{5,4},{6,7},{7,6},{8,9},{9,8},{10,11... | collective-permute-start | bytes 196616 | tf_op jit(solution)/shard_map/ppermute | solution.py:249
  9.5 1.4 %collective-permute-start.1 = (f32[256,128]{1,0:T(8,128)S(1)}, f32[256,128]{1,0:T(8,128)S(1)}, u32[]{:S(2)}, u32[]{:S(2)}) collective-permute-start(f32[256,128]{1,0:T(8,128)S(1)} %get-tuple-element.27.own_ref), channel_id=1, source_target_pairs={{0,8},{8,0},{16,24},{24,16},{1,9},{9,1},{17,25},{25,17},{2,10},{10... | collective-permute-start | bytes 393224 | tf_op jit(solution)/shard_map/ppermute | solution.py:249
  9.7 4.1 %copy-start.3 = (bf16[256,128]{1,0:T(8,128)(2,1)S(1)}, bf16[256,128]{1,0:T(8,128)(2,1)}, u32[]{:S(2)}) copy-start(bf16[256,128]{1,0:T(8,128)(2,1)} %v_ref.1) | copy-start | bytes 196612
  9.7 4.1 %copy-start.4 = (f32[1,1,128,128]{3,2,1,0:T(8,128)S(1)}, f32[1,1,128,128]{3,2,1,0:T(8,128)}, u32[]{:S(2)}) copy-start(f32[1,1,128,128]{3,2,1,0:T(8,128)} %param.12) | copy-start | bytes 196612
  11.7 4.7 %collective-permute-start.2 = (f32[128,128]{1,0:T(8,128)S(1)}, f32[128,128]{1,0:T(8,128)S(1)}, u32[]{:S(2)}, u32[]{:S(2)}) collective-permute-start(f32[128,128]{1,0:T(8,128)S(1)} %get-tuple-element.28.after_ref), channel_id=1, source_target_pairs={{0,16},{8,24},{16,0},{24,8},{1,17},{9,25},{17,1},{25,9},{2,18},{10... | collective-permute-start | bytes 196616 | tf_op jit(solution)/shard_map/ppermute | solution.py:249
  18.5 5.3 %collective-permute-start.3 = (f32[128,256]{1,0:T(8,128)S(1)}, f32[128,256]{1,0:T(8,128)S(1)}, u32[]{:S(2)}, u32[]{:S(2)}) collective-permute-start(f32[128,256]{1,0:T(8,128)S(1)} %get-tuple-element.45), channel_id=1, source_target_pairs={{0,1},{1,0},{2,3},{3,2},{4,5},{5,4},{6,7},{7,6},{8,9},{9,8},{10,11... | collective-permute-start | bytes 393224 | tf_op jit(solution)/shard_map/ppermute | solution.py:249

commit v2 on v1

v2 whole, which is shorter than its diff:
```python
import jax
import jax.numpy as jnp
from jax import lax
from jax.experimental import pallas as pl
from jax.experimental.pallas import tpu as pltpu
from jax.sharding import PartitionSpec as P

F32 = jnp.float32
BF16 = jnp.bfloat16
BASE = 16
NN = (((1,), (0,)), ((), ()))
NT = (((1,), (1,)), ((), ()))


def split(x):
    high = x.astype(BF16)
    return (high, (x - high.astype(F32)).astype(BF16))


def mm(left, right, dims=NN):
    left = left if isinstance(left, tuple) else (left if left.dtype == BF16 else split(left))
    right = right if isinstance(right, tuple) else (right if right.dtype == BF16 else split(right))

    def one(a, b):
        return lax.dot_general(a, b, dims, preferred_element_type=F32)

    if isinstance(left, tuple) and isinstance(right, tuple):
        return one(left[0], right[0]) + (one(left[0], right[1]) + one(left[1], right[0]))
    if isinstance(left, tuple):
        return one(left[0], right) + one(left[1], right)
    if isinstance(right, tuple):
        return one(left, right[0]) + one(left, right[1])
    return one(left, right)


def ids(shape):
    return lax.broadcasted_iota(jnp.int32, shape, 0), lax.broadcasted_iota(jnp.int32, shape, 1)


def to_col(row, eye):
    return jnp.sum(jnp.where(eye, row, 0.0), 1, keepdims=True)


def to_row(col, eye):
    return jnp.sum(jnp.where(eye, col, 0.0), 0, keepdims=True)


def base_inverse(nil, base):
    size = nil.shape[0]
    count = size // base
    row, lane = ids((base, size))
    block = lane // base
    packed = jnp.zeros((base, size), F32)
    for b in range(count):
        packed = jnp.where(block == b, nil[b * base : (b + 1) * base, :], packed)
    solved = jnp.where(row == lane % base, 1.0, 0.0)
    for j in range(base - 1):
        factor = jnp.take_along_axis(packed, block * base + j, axis=1)
        factor = jnp.where(row > j, factor, 0.0)
        solved = solved + factor * solved[j : j + 1, :]
    return jnp.concatenate([jnp.where(block == b, solved, 0.0) for b in range(count)], 0)


def half_inverse(nil):
    size = nil.shape[0]
    row, lane = ids((size, size))
    inv = base_inverse(nil, BASE)
    width = BASE
    while width < size:
        factor = 4 if size >= 4 * width else 2
        wide = width * factor
        off = jnp.where((row // wide == lane // wide) & (row // width != lane // width), nil, 0.0)
        inv_s = split(inv)
        step = split(mm(inv_s, off))
        first = inv + mm(step, inv_s)
        if factor == 4:
            first = first + mm(mm(step, step), first)
        inv = first
        width = wide
    return inv


def inverse(nil):
    size = nil.shape[0]
    half = size // 2
    upper = half_inverse(nil[:half, :half])
    lower = half_inverse(nil[half:, half:])
    corner = mm(mm(lower, nil[half:, :half]), upper)
    top = jnp.concatenate([upper, jnp.zeros((half, half), F32)], 1)
    return jnp.concatenate([top, jnp.concatenate([corner, lower], 1)], 0)


def decays(decay_row, row, lane):
    cum_col = jnp.sum(jnp.where(lane <= row, decay_row, 0.0), 1, keepdims=True)
    return cum_col, to_row(cum_col, row == lane)


def prep_kernel(
    flag_ref, q_ref, k_ref, decay_ref, rate_ref, spread_ref, damp_ref, kk_ref, qk_ref, rows_ref, mask_ref,
):
    length = q_ref.shape[1]
    row, lane = ids((length, length))
    cum_col, cum_row = decays(decay_ref[...], row, lane)
    rate_row = rate_ref[...]
    spread = jnp.exp(jnp.where(lane <= row, cum_col - cum_row, -1e30))
    spread_ref[...] = spread
    damp_ref[...] = jnp.where(lane < row, spread, 0.0) * -to_col(rate_row, row == lane)
    k_f, q_f = k_ref[...].astype(F32), q_ref[...].astype(F32)
    kk_ref[...] = mm(k_f.T.astype(BF16), k_ref[...])
    qk_ref[...] = mm(q_f.T.astype(BF16), k_ref[...])
    grow = jnp.exp(cum_row)
    tail = jnp.exp(cum_row[:, length - 1 :] - cum_row)
    k_sum = jnp.sum(k_f * k_f, 0, keepdims=True)
    q_sum = jnp.sum(q_f * q_f, 0, keepdims=True)
    rows_ref[...] = jnp.concatenate([cum_row, grow, tail, rate_row, k_sum, q_sum, cum_row, cum_row], 0)
    mask_ref[...] = jnp.concatenate([jnp.full((1, mask_ref.shape[1]), flag_ref[i], F32) for i in range(8)], 0)


def inverse_kernel(k_ref, other_ref, kk_in_ref, damp_ref, rows_ref, inv_ref, w_ref, map_ref, kk_ref, scale_ref):
    other = other_ref[...]
    other_f = other.astype(F32)
    k_t = jnp.concatenate([k_ref[...], other], 0)
    width, length = k_t.shape
    grow, tail, rate_row, k_sum = (rows_ref[i : i + 1, :] for i in range(1, 5))
    square = k_sum + jnp.sum(other_f * other_f, 0, keepdims=True) + 1e-6
    k_scale = 1.0 / jnp.sqrt(square)
    kk = kk_in_ref[...] + mm(other_f.T.astype(BF16), other)
    inv = inverse(damp_ref[...] * (kk * (k_scale * k_scale)))
    w_t = mm(k_t, inv * (rate_row * grow), NT) * k_scale
    w_row, w_lane = ids((width, width))
    map_ref[...] = jnp.where(w_row == w_lane, grow[:, length - 1 :], 0.0) - mm(w_t * (tail * k_scale), k_t, NT)
    inv_ref[...] = inv
    w_ref[...] = w_t
    kk_ref[...] = kk
    scale_ref[...] = jnp.concatenate([k_scale, square * k_scale], 0)


def shift_kernel(
    q_ref, other_ref, k_other_ref, g_ref, qk_ref, spread_ref, rows_ref, scale_ref, w_ref, shift_ref, score_ref, q_scale_ref
):
    other = other_ref[...]
    other_f = other.astype(F32)
    q_f = jnp.concatenate([q_ref[...].astype(F32), other_f], 0)
    width = q_f.shape[0]
    q_sum = rows_ref[5:6, :] + jnp.sum(other_f * other_f, 0, keepdims=True)
    q_scale = width ** (-0.5) / jnp.sqrt(q_sum + 1e-6)
    score = spread_ref[...] * (qk_ref[...] + mm(other_f.T.astype(BF16), k_other_ref[...]))
    side = q_scale * (q_f * rows_ref[1:2, :] - mm(w_ref[...] * scale_ref[0:1, :], score, NT))
    shift_ref[...] = mm(side, g_ref[...])
    score_ref[...] = score
    q_scale_ref[...] = q_scale


def join_kernel(mask_ref, own_map_ref, own_ref, got_map_ref, got_ref, total_ref):
    low = mask_ref[0:1, :] > 0.0
    own, got = own_ref[...], got_ref[...]
    first = jnp.where(low, own_map_ref[...], got_map_ref[...])
    total_ref[...] = mm(first, jnp.where(low, got, own)) + jnp.where(low, own, got)


def update_kernel(
    mask_ref, q_ref, q_other_ref, k_ref, k_other_ref, v_ref, g_ref, start_ref, inv_ref, spread_ref, rows_ref, scale_ref,
    q_scale_ref, u_ref, base_ref, score_grad_ref, start_t_ref, keep_ref, send_ref,
):
    half, length = q_ref.shape
    q_f = jnp.concatenate([q_ref[...], q_other_ref[...]], 0).astype(F32)
    k_t = jnp.concatenate([k_ref[...], k_other_ref[...]], 0)
    width = k_t.shape[0]
    row, lane = ids((length, length))
    eye = row == lane
    grow, rate_row = rows_ref[1:2, :], rows_ref[3:4, :]
    k_scale, k_norm = scale_ref[0:1, :], scale_ref[1:2, :]
    start = start_ref[...]
    start = jnp.where(mask_ref[2:3, :] > 0.0, start, pltpu.roll(start, half, 1))
    start_t = start.T
    grad = g_ref[...]
    grad_t = grad.astype(F32).T.astype(BF16)
    k_rows = k_t.astype(F32).T.astype(BF16)
    base = v_ref[...].astype(F32) - to_col(grow * k_scale, eye) * mm(k_rows, start, NT)
    u = to_col(k_scale, eye) * mm(inv_ref[...], to_col(k_norm * rate_row, eye) * base)
    score_grad = mm(grad, u, NT) * spread_ref[...]
    q_scale = q_scale_ref[...]
    dq = mm(k_t, score_grad * k_scale, NT) + grow * mm(start_t, grad_t)
    unit = q_f * (q_scale * width**0.5)
    dq = q_scale * (dq - unit * jnp.sum(unit * dq, 0, keepdims=True))
    keep_ref[...] = dq[0:half, :]
    send_ref[...] = dq[half:, :]
    u_ref[...] = u
    base_ref[...] = base
    score_grad_ref[...] = score_grad
    start_t_ref[...] = start_t


def local_kernel(
    q_ref, q_other_ref, k_ref, k_other_ref, g_ref, start_t_ref, inv_ref, score_ref, damp_ref, rows_ref, scale_ref,
    q_scale_ref, u_ref, score_grad_ref, after_ref,
    uh_ref, ul_ref, uth_ref, utl_ref, ph_ref, pl_ref, pth_ref, ptl_ref, gh_ref, gl_ref, kh_ref, kl_ref, y_ref, sym_ref, dk_ref,
):
    length = q_ref.shape[1]
    q_f = jnp.concatenate([q_ref[...], q_other_ref[...]], 0).astype(F32)
    k_t = jnp.concatenate([k_ref[...], k_other_ref[...]], 0)
    row, lane = ids((length, length))
    eye = row == lane
    grow, tail, rate_row = (rows_ref[i : i + 1, :] for i in range(1, 4))
    k_scale, k_norm = scale_ref[0:1, :], scale_ref[1:2, :]
    q_scale = q_scale_ref[...]
    grad_t = g_ref[...].astype(F32).T.astype(BF16)
    inv = inv_ref[...]
    u = u_ref[...]
    u_t = u.T
    u_s, u_ts = split(u), split(u_t)
    score = score_ref[...] * (to_col(q_scale, eye) * k_scale)
    y_t = mm(mm(grad_t, score) * k_scale, inv) * k_norm
    psi_t = mm(k_t, inv * to_col(tail * k_scale * k_scale, eye)) * k_norm
    y = y_t.T
    damp = damp_ref[...]
    sym_decay = damp + damp.T
    sym = sym_decay * jnp.where(lane < row, mm(y, u_ts), mm(u_s, y_t))
    k_s = split(k_t.astype(F32) * k_scale)
    dk_ref[...] = (
        mm(k_s, sym) + mm(q_f * q_scale, score_grad_ref[...]) - mm(start_t_ref[...], y_t * (grow * rate_row))
    )
    uh_ref[...], ul_ref[...] = u_s
    uth_ref[...], utl_ref[...] = u_ts
    ph_ref[...], pl_ref[...] = split(psi_t.T)
    pth_ref[...], ptl_ref[...] = split(psi_t)
    gh_ref[...], gl_ref[...] = split(psi_t * (grow * rate_row))
    kh_ref[...], kl_ref[...] = k_s
    y_ref[...] = y
    sym_ref[...] = sym_decay


def far_kernel(
    mask_ref, got_ref, ahead_map_ref, ahead_ref, k_ref, k_other_ref, uh_ref, ul_ref, uth_ref, utl_ref, ph_ref, pl_ref,
    pth_ref, ptl_ref, gh_ref, gl_ref, kh_ref, kl_ref, sym_ref, dk_ref, start_t_ref, rows_ref, scale_ref,
    send_ref, keep_ref, far_ref,
):
    half, length = k_ref.shape
    k_f = jnp.concatenate([k_ref[...], k_other_ref[...]], 0).astype(F32)
    width = k_f.shape[0]
    row, lane = ids((length, length))
    k_scale = scale_ref[0:1, :]
    w_row, w_lane = ids((width, got_ref.shape[1]))
    low = mask_ref[0:1, :] > 0.0
    got = jnp.where(mask_ref[1:2, :] > 0.0, got_ref[...], 0.0)
    ahead_map = jnp.where(low, ahead_map_ref[...], jnp.where(w_row == w_lane, 1.0, 0.0))
    far = mm(ahead_map, got) + jnp.where(low, ahead_ref[...], 0.0)
    far_s = split(far)
    far_ref[...] = far
    uz_t = mm(far_s, (uth_ref[...], utl_ref[...]))
    uz = mm((uh_ref[...], ul_ref[...]), far_s, NT)
    sz = mm(start_t_ref[...], far_s, NT)
    sym = sym_ref[...] * jnp.where(
        lane < row, mm((ph_ref[...], pl_ref[...]), uz_t), mm(uz, (pth_ref[...], ptl_ref[...]))
    )
    dk = dk_ref[...] + rows_ref[2:3, :] * uz_t - mm(sz, (gh_ref[...], gl_ref[...]))
    dk = dk + mm((kh_ref[...], kl_ref[...]), sym)
    unit = k_f * k_scale
    dk = k_scale * (dk - unit * jnp.sum(unit * dk, 0, keepdims=True))
    keep_ref[...] = dk[0:half, :]
    send_ref[...] = dk[half:, :]


def value_kernel(
    far_ref, ph_ref, pl_ref, y_ref, base_ref, kk_ref, spread_ref, scale_ref, rows_ref, uh_ref, ul_ref, keep_ref, got_ref,
    value_ref, rate_out_ref, q_ref,
):
    length = y_ref.shape[0]
    row, lane = ids((length, length))
    eye = row == lane
    k_scale = scale_ref[0:1, :]
    y = y_ref[...] + mm((ph_ref[...], pl_ref[...]), far_ref[...])
    value_ref[...] = to_col(rows_ref[3:4, :], eye) * y
    low = jnp.where(lane < row, spread_ref[...] * kk_ref[...], 0.0) * (to_col(k_scale, eye) * k_scale)
    write = base_ref[...] - mm(low, (uh_ref[...], ul_ref[...]))
    rate_out_ref[...] = to_row(jnp.sum(y * write, 1, keepdims=True), eye)
    q_ref[...] = keep_ref[...] + got_ref[...]


def add_kernel(keep_ref, got_ref, k_ref):
    k_ref[...] = keep_ref[...] + got_ref[...]


def call(kernel, outs, *args, smem=(), cost=1.0):
    shapes = [out if isinstance(out[0], tuple) else (out, F32) for out in outs]
    return pl.pallas_call(
        kernel,
        out_shape=tuple(jax.ShapeDtypeStruct(shape, kind) for shape, kind in shapes),
        in_specs=[
            pl.BlockSpec(memory_space=pltpu.SMEM if i in smem else pltpu.VMEM) for i in range(len(args))
        ],
        out_specs=tuple(pl.BlockSpec(memory_space=pltpu.VMEM) for _ in outs),
        cost_estimate=pl.CostEstimate(flops=int(cost * 1e9), bytes_accessed=1 << 20, transcendentals=0),
        compiler_params=pltpu.CompilerParams(vmem_limit_bytes=24 << 20),
    )(*args)


def swap(x, axis, apart):
    return lax.ppermute(x, axis, [(i, i ^ 1 << apart) for i in range(lax.axis_size(axis))])


def far_scan(section, count, place):
    def dot(left, right):
        return jnp.dot(left, right, precision=lax.Precision.HIGHEST)

    own_map, own = section
    ahead_map, ahead = jnp.eye(own_map.shape[0], dtype=F32), jnp.zeros_like(own)
    for bit in range(count.bit_length() - 2):
        got_map, got = swap(own_map, "seq", bit), swap(own, "seq", bit)
        low = (place >> bit) % 2 == 0
        ahead = jnp.where(low, dot(ahead_map, got) + ahead, ahead)
        ahead_map = jnp.where(low, dot(ahead_map, got_map), ahead_map)
        low_map, high_map = jnp.where(low, own_map, got_map), jnp.where(low, got_map, own_map)
        own = dot(low_map, jnp.where(low, got, own)) + jnp.where(low, own, got)
        own_map = dot(low_map, high_map)
    return own, ahead_map, ahead


def per_device(queries, key_rows, values, log_decay, beta_rate, start_states, output_grad):
    count = lax.axis_size("seq")
    stages = count.bit_length() - 1
    assert count == 1 << stages and stages >= 2
    place = lax.axis_index("seq")
    parity = lax.axis_index("head") % 2
    q_t, k_t = queries.T, key_rows.T
    half, length = q_t.shape
    width = 2 * half
    depth = values.shape[1]
    start = start_states[0, 0]
    square, tall, wide, thin = (length, length), (length, depth), (width, length), (1, length)
    k_other = swap(k_t, "head", 0)
    q_other = swap(q_t, "head", 0)
    low_first = 1 - place % 2 if stages == 2 else place * 0 + 1
    low_last = 1 - (place >> (stages - 1)) % 2
    flags = jnp.stack([low_first, low_last, 1 - parity] + [parity] * 5).astype(F32)
    spread, damp, kk_own, qk_own, rows, mask = call(
        prep_kernel, [square, square, square, square, (8, length), (8, depth)],
        flags, q_t, k_t, log_decay, beta_rate, smem=(0,),
    )
    inv, w_t, own_map, kk, scale = call(
        inverse_kernel, [square, wide, (width, width), square, (2, length)], k_t, k_other, kk_own, damp, rows
    )
    if stages == 2:
        got_map = swap(own_map, "seq", 0)
    own, score, q_scale = call(
        shift_kernel, [(width, depth), square, thin],
        q_t, q_other, k_other, output_grad, qk_own, spread, rows, scale, w_t,
    )
    if stages == 2:
        got = swap(own, "seq", 0)
        (total,) = call(join_kernel, [(width, depth)], mask, own_map, own, got_map, got)
        ahead_map, ahead = got_map, got
    else:
        total, ahead_map, ahead = far_scan((own_map, own), count, place)
    arrived = swap(total, "seq", stages - 1)
    u, base, score_grad, start_t, keep_q, send_q = call(
        update_kernel, [tall, tall, square, (width, depth), (half, length), (half, length)],
        mask, q_t, q_other, k_t, k_other, values, output_grad, start, inv, spread, rows, scale, q_scale,
    )
    got_q = swap(send_q, "head", 0)
    pairs = [(tall, BF16)] * 2 + [((depth, length), BF16)] * 2 + [((length, width), BF16)] * 2 + [(wide, BF16)] * 6
    *packs, y, sym, dk = call(
        local_kernel, pairs + [tall, square, wide],
        q_t, q_other, k_t, k_other, output_grad, start_t, inv, score, damp, rows, scale, q_scale, u, score_grad, total,
    )
    send, keep, far = call(
        far_kernel, [(half, length), (half, length), (width, depth)],
        mask, arrived, ahead_map, ahead, k_t, k_other, *packs, sym, dk, start_t, rows, scale,
    )
    got_k = swap(send, "head", 0)
    value_grad, rate_grad, query_grad = call(
        value_kernel, [tall, thin, (half, length)],
        far, packs[4], packs[5], y, base, kk, spread, scale, rows, packs[0], packs[1], keep_q, got_q,
    )
    (key_grad,) = call(add_kernel, [(half, length)], keep, got_k)
    return (query_grad.T, key_grad.T, value_grad, rate_grad)


def solution(mesh):
    in_specs = (
        P("seq", "head"),
        P("seq", "head"),
        P("seq", "head"),
        P("head", "seq"),
        P("head", "seq"),
        P("seq", "head", None, None),
        P("seq", "head"),
    )
    out_specs = (P("seq", "head"), P("seq", "head"), P("seq", "head"), P("head", "seq"))

    return jax.shard_map(per_device, mesh=mesh, in_specs=in_specs, out_specs=out_specs, check_vma=False)
```

time: 24.6 us -> 23.5 us (0.955)
  waiting for transfers between devices: 7.17 us -> 4.78 us
  starting transfers between devices: 6.73 us -> 7.72 us
  other arithmetic: 0.97 us -> 0.01 us
  local copies, waits for them, and re-layouts: 0.03 us -> 0.8 us
  Pallas kernels: 8.8 us -> 9.24 us
    ppermute x4 -> x7, waiting for transfers between devices: 7.17 us -> 4.78 us  [swap(): lax.ppermute(x, axis, [(i, i ^ 1 << apart) for i in range(lax.axis_size(a...]
    ppermute x4 -> x7, starting transfers between devices: 6.73 us -> 7.72 us  [swap(): lax.ppermute(x, axis, [(i, i ^ 1 << apart) for i in range(lax.axis_size(a...]
    concatenate x1 -> x0, other arithmetic: 0.82 us -> none  [per_device(): other = swap(jnp.concatenate([q_t, k_t], 0), 'head', 0)]
    unnamed x14, local copies, waits for them, and re-layouts: 0.03 us -> 0.72 us
    pallas_call x5 -> x9, Pallas kernels: 8.8 us -> 9.24 us  [call(): pl.pallas_call(kernel, out_shape=tuple((jax.ShapeDtypeStruct(shape, kind)...]
  transfers between devices with their start and end apart: 4 -> 7, of which waited for: 3 -> 3; matrix products, arithmetic and copies ran while one was open for 1% -> 0% of each run, Pallas kernels for 10% -> 34%
where the time goes in v2:
time: 23.5 us; the launch traced here: 23.3 us
  Pallas kernels  9.24 us (39%)
  starting transfers between devices  7.72 us (33%)
  waiting for transfers between devices  4.78 us (20%)
  local copies, waits for them, and re-layouts  0.8 us (3%)
  between operations  0.73 us (3%)
    pallas_call x9, Pallas kernels, call(): pl.pallas_call(kernel, out_shape=tuple((jax.ShapeDtypeStruct(shape, kind)...  9.24 us
    ppermute x7, starting transfers between devices, swap(): lax.ppermute(x, axis, [(i, i ^ 1 << apart) for i in range(lax.axis_size(a...  7.72 us
    ppermute x7, waiting for transfers between devices, swap(): lax.ppermute(x, axis, [(i, i ^ 1 << apart) for i in range(lax.axis_size(a...  4.78 us
    unnamed x14, local copies, waits for them, and re-layouts  0.72 us
  transfers between devices with their start and end apart: 7, of which 3 were waited for; matrix products, arithmetic and copies ran while one was open for 0% of the time, Pallas kernels for 34%

profile of v2, /device:TPU:0, one launch (start us, length us, event | category | flops | bytes accessed | tf_op | source)
XLA Modules:
  0.0 23.3 jit_solution(3270274181468980891)
XLA Ops:
  0.6 3.0 %collective-permute-start = (bf16[64,256]{1,0:T(8,128)(2,1)}, bf16[64,256]{1,0:T(8,128)(2,1)S(1)}, u32[]{:S(2)}, u32[]{:S(2)}) collective-permute-start(bf16[64,256]{1,0:T(8,128)(2,1)} %bitcast.15), channel_id=1, source_target_pairs={{0,1},{1,0},{2,3},{3,2},{4,5},{5,4},{6,7},{7,6},{8,9},{9,8},{10,11... | collective-permute-start | bytes 98312 | tf_op jit(solution)/shard_map/ppermute | solution.py:299
  3.7 0.1 collective-permute-start.1
  3.7 0.1 stack.23
  3.8 0.6 %copy-done.6 = f32[1,256]{1,0:T(1,128)S(1)} copy-done((f32[1,256]{1,0:T(1,128)S(1)}, f32[1,256]{1,0:T(1,128)}, u32[]{:S(2)}) %copy-start.6) | copy-done | bytes 1048
  4.4 0.1 copy-done.4
  4.5 0.0 copy-done.3
  4.5 0.9 %shard_map.102 = (f32[256,256]{1,0:T(8,128)S(1)}, f32[256,256]{1,0:T(8,128)S(1)}, f32[256,256]{1,0:T(8,128)S(1)}, f32[256,256]{1,0:T(8,128)S(1)}, f32[8,256]{1,0:T(8,128)S(1)}, /*index=5*/f32[8,128]{1,0:T(8,128)S(1)}) custom-call(f32[8]{0:T(128)S(1)} %convert_element_type.3.flag_ref, bf16[64,256]{1,0:T(8,128)(2,1)S(1)} %bitcast.11, ...), custom_call_target="tpu_custom_call" | custom-call | flops 1000000000 | bytes 1048576 | tf_op jit(solution)/shard_map/pallas_call | solution.py:286
  5.4 0.4 %collective-permute-done.other_ref.k_other_ref = bf16[64,256]{1,0:T(8,128)(2,1)S(1)} collective-permute-done((bf16[64,256]{1,0:T(8,128)(2,1)}, bf16[64,256]{1,0:T(8,128)(2,1)S(1)}, u32[]{:S(2)}, u32[]{:S(2)}) %collective-permute-start) | collective-permute-done | bytes 32800 | tf_op jit(solution)/shard_map/ppermute | solution.py:299
  5.8 2.5 %shard_map.103 = (f32[256,256]{1,0:T(8,128)S(1)}, f32[128,256]{1,0:T(8,128)S(1)}, f32[128,128]{1,0:T(8,128)S(1)}, f32[256,256]{1,0:T(8,128)S(1)}, f32[2,256]{1,0:T(2,128)S(1)}) custom-call(bf16[64,256]{1,0:T(8,128)(2,1)S(1)} %bitcast.17, bf16[64,256]{1,0:T(8,128)(2,1)S(1)} %collective-permute-done.other_ref.k_other_ref, ...), custom_call_target="tpu_custom_call" | custom-call | flops 1000000000 | bytes 1048576 | tf_op jit(solution)/shard_map/pallas_call | solution.py:286
  8.3 0.0 copy-start
  8.3 0.7 %shard_map.104 = (f32[128,128]{1,0:T(8,128)S(1)}, f32[256,256]{1,0:T(8,128)S(1)}, f32[1,256]{1,0:T(1,128)S(1)}) custom-call(bf16[64,256]{1,0:T(8,128)(2,1)S(1)} %bitcast.12, bf16[64,256]{1,0:T(8,128)(2,1)S(1)} %collective-permute-done.1.other_ref.q_other_ref, bf16[64,256]{1,0:T(8,128)(2,1)S(1)} %collective-permute-done.other_ref.k_other_ref, ...), custom_call_target="tpu_custom_call" | custom-call | flops 1000000000 | bytes 1048576 | tf_op jit(solution)/shard_map/pallas_call | solution.py:286
  9.0 0.1 collective-permute-start.3
  9.1 0.5 %collective-permute-start.2 = (f32[128,128]{1,0:T(8,128)S(1)}, f32[128,128]{1,0:T(8,128)S(1)}, u32[]{:S(2)}, u32[]{:S(2)}) collective-permute-start(f32[128,128]{1,0:T(8,128)S(1)} %get-tuple-element.49.own_map_ref), channel_id=1, source_target_pairs={{0,8},{8,0},{16,24},{24,16},{1,9},{9,1},{17,25},{25,17},{2,10},{10... | collective-permute-start | bytes 196616 | tf_op jit(solution)/shard_map/ppermute | solution.py:299
  9.6 1.1 %shard_map.106 = (f32[256,128]{1,0:T(8,128)S(1)}, f32[256,128]{1,0:T(8,128)S(1)}, f32[256,256]{1,0:T(8,128)S(1)}, f32[128,128]{1,0:T(8,128)S(1)}, f32[64,256]{1,0:T(8,128)S(1)}, /*index=5*/f32[64,256]{1,0:T(8,128)S(1)}) custom-call(f32[8,128]{1,0:T(8,128)S(1)} %get-tuple-element.45.mask_ref, bf16[64,256]{1,0:T(8,128)(2,1)S(1)} %bitcast.13, ...), custom_call_target="tpu_custom_call" | custom-call | flops 1000000000 | bytes 1048576 | tf_op jit(solution)/shard_map/pallas_call | solution.py:286
  10.7 2.1 %collective-permute-start.5 = (f32[64,256]{1,0:T(8,128)S(1)}, f32[64,256]{1,0:T(8,128)S(1)}, u32[]{:S(2)}, u32[]{:S(2)}) collective-permute-start(f32[64,256]{1,0:T(8,128)S(1)} %get-tuple-element.80), channel_id=1, source_target_pairs={{0,1},{1,0},{2,3},{3,2},{4,5},{5,4},{6,7},{7,6},{8,9},{9,8},{10,11... | collective-permute-start | bytes 196616 | tf_op jit(solution)/shard_map/ppermute | solution.py:299
  12.8 0.2 shard_map.105.after_ref
  13.0 1.6 %collective-permute-start.4 = (f32[128,128]{1,0:T(8,128)S(1)}, f32[128,128]{1,0:T(8,128)S(1)}, u32[]{:S(2)}, u32[]{:S(2)}) collective-permute-start(f32[128,128]{1,0:T(8,128)S(1)} %shard_map.105.after_ref), channel_id=1, source_target_pairs={{0,16},{8,24},{16,0},{24,8},{1,17},{9,25},{17,1},{25,9},{2,18},{10... | collective-permute-start | bytes 196616 | tf_op jit(solution)/shard_map/ppermute | solution.py:299
  14.6 1.2 %shard_map.107 = (bf16[256,128]{1,0:T(8,128)(2,1)S(1)}, bf16[256,128]{1,0:T(8,128)(2,1)S(1)}, bf16[128,256]{1,0:T(8,128)(2,1)S(1)}, bf16[128,256]{1,0:T(8,128)(2...) custom-call(bf16[64,256]{1,0:T(8,128)(2,1)S(1)} %bitcast.14, ...), custom_call_target="tpu_custom_call" | custom-call | flops 1000000000 | bytes 1048576 | tf_op jit(solution)/shard_map/pallas_call | solution.py:286
  15.8 1.6 %collective-permute-done.4.got_ref = f32[128,128]{1,0:T(8,128)S(1)} collective-permute-done((f32[128,128]{1,0:T(8,128)S(1)}, f32[128,128]{1,0:T(8,128)S(1)}, u32[]{:S(2)}, u32[]{:S(2)}) %collective-permute-start.4) | collective-permute-done | bytes 65568 | tf_op jit(solution)/shard_map/ppermute | solution.py:299
  17.3 1.0 %shard_map.108 = (f32[64,256]{1,0:T(8,128)S(1)}, f32[64,256]{1,0:T(8,128)S(1)}, f32[128,128]{1,0:T(8,128)S(1)}) custom-call(f32[8,128]{1,0:T(8,128)S(1)} %get-tuple-element.45.mask_ref, f32[128,128]{1,0:T(8,128)S(1)} %collective-permute-done.4.got_ref, f32[128,128]{1,0:T(8,128)S(1)} %collective-permute-done.2.got_map_ref.ahead_map_ref, ...), custom_call_target="tpu_custom_call" | custom-call | flops 1000000000 | bytes 1048576 | tf_op jit(solution)/shard_map/pallas_call | solution.py:286
  18.3 0.4 %collective-permute-start.6 = (f32[64,256]{1,0:T(8,128)S(1)}, f32[64,256]{1,0:T(8,128)S(1)}, u32[]{:S(2)}, u32[]{:S(2)}) collective-permute-start(f32[64,256]{1,0:T(8,128)S(1)} %get-tuple-element.83), channel_id=1, source_target_pairs={{0,1},{1,0},{2,3},{3,2},{4,5},{5,4},{6,7},{7,6},{8,9},{9,8},{10,11... | collective-permute-start | bytes 196616 | tf_op jit(solution)/shard_map/ppermute | solution.py:299
  18.7 1.1 %shard_map.109 = (f32[256,128]{1,0:T(8,128)}, f32[1,256]{1,0:T(1,128)}, f32[64,256]{1,0:T(8,128)}) custom-call(f32[128,128]{1,0:T(8,128)S(1)} %get-tuple-element.75.far_ref, bf16[256,128]{1,0:T(8,128)(2,1)S(1)} %get-tuple-element.65.ph_ref, bf16[256,128]{1,0:T(8,128)(2,1)S(1)} %get-tuple-element.66.pl_ref, f32[256,128]{1,0:T(8,128)S(1)} %get-tuple-element.76.y_ref, ...), custom_call_target="tpu_custom_call" | custom-call | flops 1000000000 | bytes 1048576 | tf_op jit(solution)/shard_map/pallas_call | solution.py:286
  19.8 2.8 %collective-permute-done.6.got_ref = f32[64,256]{1,0:T(8,128)S(1)} collective-permute-done((f32[64,256]{1,0:T(8,128)S(1)}, f32[64,256]{1,0:T(8,128)S(1)}, u32[]{:S(2)}, u32[]{:S(2)}) %collective-permute-start.6) | collective-permute-done | bytes 65568 | tf_op jit(solution)/shard_map/ppermute | solution.py:299
  22.6 0.6 %shard_map.110 = f32[64,256]{1,0:T(8,128)} custom-call(f32[64,256]{1,0:T(8,128)S(1)} %get-tuple-element.82.keep_ref, f32[64,256]{1,0:T(8,128)S(1)} %collective-permute-done.6.got_ref), custom_call_target="tpu_custom_call" | custom-call | flops 1000000000 | bytes 1048576 | tf_op jit(solution)/shard_map/pallas_call | solution.py:286
  (15 shorter events, 0.0 us)
Async XLA Ops:
  0.6 5.1 %collective-permute-start = (bf16[64,256]{1,0:T(8,128)(2,1)}, bf16[64,256]{1,0:T(8,128)(2,1)S(1)}, u32[]{:S(2)}, u32[]{:S(2)}) collective-permute-start(bf16[64,256]{1,0:T(8,128)(2,1)} %bitcast.15), channel_id=1, source_target_pairs={{0,1},{1,0},{2,3},{3,2},{4,5},{5,4},{6,7},{7,6},{8,9},{9,8},{10,11... | collective-permute-start | bytes 98312 | tf_op jit(solution)/shard_map/ppermute | solution.py:299
  3.7 4.6 %collective-permute-start.1 = (bf16[64,256]{1,0:T(8,128)(2,1)}, bf16[64,256]{1,0:T(8,128)(2,1)S(1)}, u32[]{:S(2)}, u32[]{:S(2)}) collective-permute-start(bf16[64,256]{1,0:T(8,128)(2,1)} %bitcast.10), channel_id=1, source_target_pairs={{0,1},{1,0},{2,3},{3,2},{4,5},{5,4},{6,7},{7,6},{8,9},{9,8},{10,11... | collective-permute-start | bytes 98312 | tf_op jit(solution)/shard_map/ppermute | solution.py:299
  3.7 0.7 %copy-start.6 = (f32[1,256]{1,0:T(1,128)S(1)}, f32[1,256]{1,0:T(1,128)}, u32[]{:S(2)}) copy-start(f32[1,256]{1,0:T(1,128)} %rate_ref.1) | copy-start | bytes 3076
  3.7 0.8 %copy-start.4 = (bf16[256,64]{0,1:T(8,128)(2,1)S(1)}, bf16[256,64]{0,1:T(8,128)(2,1)}, u32[]{:S(2)}) copy-start(bf16[256,64]{0,1:T(8,128)(2,1)} %param.8) | copy-start | bytes 98308
  3.7 0.8 %copy-start.3 = (bf16[256,64]{0,1:T(8,128)(2,1)S(1)}, bf16[256,64]{0,1:T(8,128)(2,1)}, u32[]{:S(2)}) copy-start(bf16[256,64]{0,1:T(8,128)(2,1)} %param.7) | copy-start | bytes 98308
  3.8 0.7 %copy-start.5 = (f32[1,256]{1,0:T(1,128)S(1)}, f32[1,256]{1,0:T(1,128)}, u32[]{:S(2)}) copy-start(f32[1,256]{1,0:T(1,128)} %decay_ref.1) | copy-start | bytes 3076
  5.8 2.5 %copy-start.2 = (bf16[256,128]{1,0:T(8,128)(2,1)S(1)}, bf16[256,128]{1,0:T(8,128)(2,1)}, u32[]{:S(2)}) copy-start(bf16[256,128]{1,0:T(8,128)(2,1)} %g_ref.5) | copy-start | bytes 196612
  8.3 1.3 %copy-start = (bf16[256,128]{1,0:T(8,128)(2,1)S(1)}, bf16[256,128]{1,0:T(8,128)(2,1)}, u32[]{:S(2)}) copy-start(bf16[256,128]{1,0:T(8,128)(2,1)} %v_ref.1) | copy-start | bytes 196612
  8.3 1.3 %copy-start.1 = (f32[1,1,128,128]{3,2,1,0:T(8,128)S(1)}, f32[1,1,128,128]{3,2,1,0:T(8,128)}, u32[]{:S(2)}) copy-start(f32[1,1,128,128]{3,2,1,0:T(8,128)} %param.12) | copy-start | bytes 196612
  9.0 3.8 %collective-permute-start.3 = (f32[128,128]{1,0:T(8,128)S(1)}, f32[128,128]{1,0:T(8,128)S(1)}, u32[]{:S(2)}, u32[]{:S(2)}) collective-permute-start(f32[128,128]{1,0:T(8,128)S(1)} %get-tuple-element.54.own_ref), channel_id=1, source_target_pairs={{0,8},{8,0},{16,24},{24,16},{1,9},{9,1},{17,25},{25,17},{2,10},{10... | collective-permute-start | bytes 196616 | tf_op jit(solution)/shard_map/ppermute | solution.py:299
  9.1 3.7 %collective-permute-start.2 = (f32[128,128]{1,0:T(8,128)S(1)}, f32[128,128]{1,0:T(8,128)S(1)}, u32[]{:S(2)}, u32[]{:S(2)}) collective-permute-start(f32[128,128]{1,0:T(8,128)S(1)} %get-tuple-element.49.own_map_ref), channel_id=1, source_target_pairs={{0,8},{8,0},{16,24},{24,16},{1,9},{9,1},{17,25},{25,17},{2,10},{10... | collective-permute-start | bytes 196616 | tf_op jit(solution)/shard_map/ppermute | solution.py:299
  10.7 8.0 %collective-permute-start.5 = (f32[64,256]{1,0:T(8,128)S(1)}, f32[64,256]{1,0:T(8,128)S(1)}, u32[]{:S(2)}, u32[]{:S(2)}) collective-permute-start(f32[64,256]{1,0:T(8,128)S(1)} %get-tuple-element.80), channel_id=1, source_target_pairs={{0,1},{1,0},{2,3},{3,2},{4,5},{5,4},{6,7},{7,6},{8,9},{9,8},{10,11... | collective-permute-start | bytes 196616 | tf_op jit(solution)/shard_map/ppermute | solution.py:299
  13.0 4.3 %collective-permute-start.4 = (f32[128,128]{1,0:T(8,128)S(1)}, f32[128,128]{1,0:T(8,128)S(1)}, u32[]{:S(2)}, u32[]{:S(2)}) collective-permute-start(f32[128,128]{1,0:T(8,128)S(1)} %shard_map.105.after_ref), channel_id=1, source_target_pairs={{0,16},{8,24},{16,0},{24,8},{1,17},{9,25},{17,1},{25,9},{2,18},{10... | collective-permute-start | bytes 196616 | tf_op jit(solution)/shard_map/ppermute | solution.py:299
  18.3 4.3 %collective-permute-start.6 = (f32[64,256]{1,0:T(8,128)S(1)}, f32[64,256]{1,0:T(8,128)S(1)}, u32[]{:S(2)}, u32[]{:S(2)}) collective-permute-start(f32[64,256]{1,0:T(8,128)S(1)} %get-tuple-element.83), channel_id=1, source_target_pairs={{0,1},{1,0},{2,3},{3,2},{4,5},{5,4},{6,7},{7,6},{8,9},{9,8},{10,11... | collective-permute-start | bytes 196616 | tf_op jit(solution)/shard_map/ppermute | solution.py:299

commit v3 on v2

v3 whole, which is shorter than its diff:
```python
import jax
import jax.numpy as jnp
from jax import lax
from jax.experimental import pallas as pl
from jax.experimental.pallas import tpu as pltpu
from jax.sharding import PartitionSpec as P

F32 = jnp.float32
BF16 = jnp.bfloat16
BASE = 32
NN = (((1,), (0,)), ((), ()))
NT = (((1,), (1,)), ((), ()))


def split(x):
    high = x.astype(BF16)
    return (high, (x - high.astype(F32)).astype(BF16))


def mm(left, right, dims=NN):
    left = left if isinstance(left, tuple) else (left if left.dtype == BF16 else split(left))
    right = right if isinstance(right, tuple) else (right if right.dtype == BF16 else split(right))

    def one(a, b):
        return lax.dot_general(a, b, dims, preferred_element_type=F32)

    if isinstance(left, tuple) and isinstance(right, tuple):
        return one(left[0], right[0]) + (one(left[0], right[1]) + one(left[1], right[0]))
    if isinstance(left, tuple):
        return one(left[0], right) + one(left[1], right)
    if isinstance(right, tuple):
        return one(left, right[0]) + one(left, right[1])
    return one(left, right)


def ids(shape):
    return lax.broadcasted_iota(jnp.int32, shape, 0), lax.broadcasted_iota(jnp.int32, shape, 1)


def to_col(row, eye):
    return jnp.sum(jnp.where(eye, row, 0.0), 1, keepdims=True)


def to_row(col, eye):
    return jnp.sum(jnp.where(eye, col, 0.0), 0, keepdims=True)


def base_inverse(nil, base):
    size = nil.shape[0]
    count = size // base
    _, lane = ids((base, size))
    block = lane // base
    packed = jnp.zeros((base, size), F32)
    for b in range(count):
        packed = jnp.where(block == b, nil[b * base : (b + 1) * base, :], packed)
    row, lane = ids((8, size))
    first = lane // base * base
    tiles = range(base // 8)
    parts = [packed[8 * t : 8 * t + 8, :] for t in tiles]
    solved = [jnp.where(row + 8 * t == lane - first, 1.0, 0.0) for t in tiles]
    for j in range(base - 1):
        source = solved[j // 8][j % 8 : j % 8 + 1, :]
        for t in tiles[(j + 1) // 8 :]:
            factor = jnp.take_along_axis(parts[t], first + j, axis=1)
            if t == j // 8:
                factor = jnp.where(row + 8 * t > j, factor, 0.0)
            solved[t] = solved[t] + factor * source
    solved = jnp.concatenate(solved, 0)
    return jnp.concatenate([jnp.where(block == b, solved, 0.0) for b in range(count)], 0)


def inverses(nils):
    size = nils[0].shape[0]
    row, lane = ids((size, size))
    found = [base_inverse(nil, BASE) for nil in nils]
    width = BASE
    while width < size:
        factor = 4 if size >= 4 * width else 2
        wide = width * factor
        off = (row // wide == lane // wide) & (row // width != lane // width)
        known = [split(inv) for inv in found]
        steps = [split(mm(inv, jnp.where(off, nil, 0.0))) for inv, nil in zip(known, nils)]
        found = [inv + mm(step, pair) for inv, step, pair in zip(found, steps, known)]
        if factor == 4:
            steps = [mm(step, step) for step in steps]
            found = [inv + mm(step, inv) for inv, step in zip(found, steps)]
        width = wide
    return found


def inverse(nil):
    half = nil.shape[0] // 2
    upper, lower = inverses([nil[:half, :half], nil[half:, half:]])
    corner = mm(mm(lower, nil[half:, :half]), upper)
    top = jnp.concatenate([upper, jnp.zeros((half, half), F32)], 1)
    return jnp.concatenate([top, jnp.concatenate([corner, lower], 1)], 0)


def decays(decay_row, row, lane):
    cum_col = jnp.sum(jnp.where(lane <= row, decay_row, 0.0), 1, keepdims=True)
    return cum_col, to_row(cum_col, row == lane)


def prep_kernel(
    flag_ref, q_ref, k_ref, decay_ref, rate_ref, spread_ref, damp_ref, kk_ref, qk_ref, rows_ref, mask_ref,
):
    length = q_ref.shape[1]
    row, lane = ids((length, length))
    cum_col, cum_row = decays(decay_ref[...], row, lane)
    rate_row = rate_ref[...]
    spread = jnp.exp(jnp.where(lane <= row, cum_col - cum_row, -1e30))
    spread_ref[...] = spread
    damp_ref[...] = jnp.where(lane < row, spread, 0.0) * -to_col(rate_row, row == lane)
    k_f, q_f = k_ref[...].astype(F32), q_ref[...].astype(F32)
    kk_ref[...] = mm(k_f.T.astype(BF16), k_ref[...])
    qk_ref[...] = mm(q_f.T.astype(BF16), k_ref[...])
    grow = jnp.exp(cum_row)
    tail = jnp.exp(cum_row[:, length - 1 :] - cum_row)
    k_sum = jnp.sum(k_f * k_f, 0, keepdims=True)
    q_sum = jnp.sum(q_f * q_f, 0, keepdims=True)
    rows_ref[...] = jnp.concatenate([cum_row, grow, tail, rate_row, k_sum, q_sum, cum_row, cum_row], 0)
    mask_ref[...] = jnp.concatenate([jnp.full((1, mask_ref.shape[1]), flag_ref[i], F32) for i in range(8)], 0)


def inverse_kernel(k_ref, other_ref, kk_in_ref, damp_ref, rows_ref, inv_ref, w_ref, kk_ref, scale_ref):
    other = other_ref[...]
    other_f = other.astype(F32)
    k_t = jnp.concatenate([k_ref[...], other], 0)
    grow, rate_row, k_sum = (rows_ref[i : i + 1, :] for i in (1, 3, 4))
    square = k_sum + jnp.sum(other_f * other_f, 0, keepdims=True) + 1e-6
    k_scale = 1.0 / jnp.sqrt(square)
    kk = kk_in_ref[...] + mm(other_f.T.astype(BF16), other)
    inv = inverse(damp_ref[...] * (kk * (k_scale * k_scale)))
    w_ref[...] = mm(k_t, inv * (rate_row * grow), NT) * k_scale
    inv_ref[...] = inv
    kk_ref[...] = kk
    scale_ref[...] = jnp.concatenate([k_scale, square * k_scale], 0)


def shift_kernel(
    q_ref, other_ref, k_ref, k_other_ref, g_ref, qk_ref, spread_ref, rows_ref, scale_ref, w_ref,
    map_ref, score_ref, q_scale_ref,
):
    other = other_ref[...]
    other_f = other.astype(F32)
    k_t = jnp.concatenate([k_ref[...], k_other_ref[...]], 0)
    q_f = jnp.concatenate([q_ref[...].astype(F32), other_f], 0)
    width, length = k_t.shape
    k_scale, grow, tail = scale_ref[0:1, :], rows_ref[1:2, :], rows_ref[2:3, :]
    score = spread_ref[...] * (qk_ref[...] + mm(other_f.T.astype(BF16), k_other_ref[...]))
    q_sum = rows_ref[5:6, :] + jnp.sum(other_f * other_f, 0, keepdims=True)
    q_scale = width ** (-0.5) / jnp.sqrt(q_sum + 1e-6)
    w_t = w_ref[...] * k_scale
    w_row, w_lane = ids((width, width))
    own_map = jnp.where(w_row == w_lane, grow[:, length - 1 :], 0.0) - mm(w_t * tail, k_t, NT)
    side = q_scale * (q_f * grow - mm(w_t, score, NT))
    map_ref[0:width, :] = own_map
    score_ref[...] = score
    q_scale_ref[...] = q_scale
    map_ref[width:, :] = mm(side, g_ref[...])


def join_kernel(mask_ref, own_ref, got_ref, total_ref):
    width = own_ref.shape[1]
    low = mask_ref[0:1, :] > 0.0
    own, got = own_ref[width:, :], got_ref[width:, :]
    first = jnp.where(low, own_ref[0:width, :], got_ref[0:width, :])
    total_ref[...] = mm(first, jnp.where(low, got, own)) + jnp.where(low, own, got)


def update_kernel(
    mask_ref, q_ref, q_other_ref, k_ref, k_other_ref, v_ref, g_ref, start_ref, inv_ref, spread_ref, rows_ref, scale_ref,
    q_scale_ref, u_ref, base_ref, score_grad_ref, start_t_ref, keep_ref, send_ref,
):
    half, length = q_ref.shape
    q_f = jnp.concatenate([q_ref[...], q_other_ref[...]], 0).astype(F32)
    k_t = jnp.concatenate([k_ref[...], k_other_ref[...]], 0)
    width = k_t.shape[0]
    row, lane = ids((length, length))
    eye = row == lane
    grow, rate_row = rows_ref[1:2, :], rows_ref[3:4, :]
    k_scale, k_norm = scale_ref[0:1, :], scale_ref[1:2, :]
    start = start_ref[...]
    start = jnp.where(mask_ref[2:3, :] > 0.0, start, pltpu.roll(start, half, 1))
    start_t = start.T
    grad = g_ref[...]
    grad_t = grad.astype(F32).T.astype(BF16)
    k_rows = k_t.astype(F32).T.astype(BF16)
    base = v_ref[...].astype(F32) - to_col(grow * k_scale, eye) * mm(k_rows, start, NT)
    u = to_col(k_scale, eye) * mm(inv_ref[...], to_col(k_norm * rate_row, eye) * base)
    score_grad = mm(grad, u, NT) * spread_ref[...]
    q_scale = q_scale_ref[...]
    dq = mm(k_t, score_grad * k_scale, NT) + grow * mm(start_t, grad_t)
    unit = q_f * (q_scale * width**0.5)
    dq = q_scale * (dq - unit * jnp.sum(unit * dq, 0, keepdims=True))
    keep_ref[...] = dq[0:half, :]
    send_ref[...] = dq[half:, :]
    u_ref[...] = u
    base_ref[...] = base
    score_grad_ref[...] = score_grad
    start_t_ref[...] = start_t


def local_kernel(
    mask_ref, q_ref, q_other_ref, k_ref, k_other_ref, g_ref, start_t_ref, inv_ref, score_ref, damp_ref, rows_ref, scale_ref,
    q_scale_ref, u_ref, score_grad_ref, ahead_ref, after_ref,
    uth_ref, utl_ref, ph_ref, pl_ref, gh_ref, gl_ref, kh_ref, kl_ref, sh_ref, sl_ref, ah_ref, al_ref, y_ref, dk_ref,
):
    length = q_ref.shape[1]
    q_f = jnp.concatenate([q_ref[...], q_other_ref[...]], 0).astype(F32)
    k_t = jnp.concatenate([k_ref[...], k_other_ref[...]], 0)
    width = k_t.shape[0]
    eye = jnp.equal(*ids((length, length)))
    grow, tail, rate_row = (rows_ref[i : i + 1, :] for i in range(1, 4))
    k_scale, k_norm = scale_ref[0:1, :], scale_ref[1:2, :]
    low = mask_ref[0:1, :] > 0.0
    ahead_map = jnp.where(low, ahead_ref[0:width, :], jnp.where(jnp.equal(*ids((width, width))), 1.0, 0.0))
    ahead = jnp.where(low, ahead_ref[width:, :], 0.0)
    grad_t = g_ref[...].astype(F32).T.astype(BF16)
    score = score_ref[...] * to_col(q_scale_ref[...], eye)
    u_ts = split(u_ref[...].T)
    inv = inv_ref[...]
    psi_t = mm(k_t, inv * to_col(tail * k_scale * k_scale, eye)) * k_norm
    du_t = mm(grad_t, score) * (k_scale * k_scale)
    psi_s = split(psi_t.T)
    y_t = mm(du_t, inv) * k_norm
    y_t = y_t + mm(ahead.T, psi_t)
    map_s = split(ahead_map)
    psi_far = mm(psi_s, map_s)
    uz_t = mm(ahead, u_ts)
    y = y_t.T
    y_ref[...] = y
    start_s = split(start_t_ref[...])
    inner = damp_ref[...] * mm(y, u_ts)
    k_s = split(k_t.astype(F32) * k_scale)
    dk = mm(q_f * q_scale_ref[...], score_grad_ref[...]) - mm(start_s, y_t * (grow * rate_row)) + tail * uz_t
    ph_ref[...], pl_ref[...] = split(psi_far)
    gh_ref[...], gl_ref[...] = split(psi_far.T * (grow * rate_row))
    inner_s = split(inner)
    dk_ref[...] = dk + (mm(k_s, inner_s) + mm(k_s, inner_s, NT))
    uth_ref[...], utl_ref[...] = u_ts
    kh_ref[...], kl_ref[...] = k_s
    sh_ref[...], sl_ref[...] = start_s
    ah_ref[...], al_ref[...] = map_s


def far_kernel(
    mask_ref, got_ref, k_ref, k_other_ref, damp_ref, rows_ref, scale_ref,
    uth_ref, utl_ref, ph_ref, pl_ref, gh_ref, gl_ref, kh_ref, kl_ref, sh_ref, sl_ref, ah_ref, al_ref, dk_ref,
    send_ref, keep_ref,
):
    half = k_ref.shape[0]
    k_scale = scale_ref[0:1, :]
    got_s = split(jnp.where(mask_ref[1:2, :] > 0.0, got_ref[...], 0.0))
    gu_s = split(mm(got_s, (uth_ref[...], utl_ref[...])))
    sg_s = split(mm((sh_ref[...], sl_ref[...]), got_s, NT))
    inner_s = split(damp_ref[...] * mm((ph_ref[...], pl_ref[...]), gu_s))
    dk = dk_ref[...] + rows_ref[2:3, :] * mm((ah_ref[...], al_ref[...]), gu_s) - mm(sg_s, (gh_ref[...], gl_ref[...]))
    k_s = (kh_ref[...], kl_ref[...])
    dk = dk + (mm(k_s, inner_s) + mm(k_s, inner_s, NT))
    unit = jnp.concatenate([k_ref[...], k_other_ref[...]], 0).astype(F32) * k_scale
    dk = k_scale * (dk - unit * jnp.sum(unit * dk, 0, keepdims=True))
    send_ref[...] = dk[half:, :]
    keep_ref[...] = dk[0:half, :]


def value_kernel(
    mask_ref, got_ref, ph_ref, pl_ref, y_ref, base_ref, kk_ref, spread_ref, scale_ref, rows_ref, u_ref, keep_ref, got_q_ref,
    value_ref, rate_out_ref, q_ref,
):
    length = y_ref.shape[0]
    row, lane = ids((length, length))
    eye = row == lane
    k_scale = scale_ref[0:1, :]
    got = jnp.where(mask_ref[1:2, :] > 0.0, got_ref[...], 0.0)
    low = jnp.where(lane < row, spread_ref[...] * kk_ref[...], 0.0) * (to_col(k_scale, eye) * k_scale)
    y = y_ref[...] + mm((ph_ref[...], pl_ref[...]), got)
    write = base_ref[...] - mm(low, u_ref[...])
    value_ref[...] = to_col(rows_ref[3:4, :], eye) * y
    rate_out_ref[...] = to_row(jnp.sum(y * write, 1, keepdims=True), eye)
    q_ref[...] = keep_ref[...] + got_q_ref[...]


def add_kernel(keep_ref, got_ref, k_ref):
    k_ref[...] = keep_ref[...] + got_ref[...]


def call(kernel, outs, *args, smem=(), cost=1.0):
    shapes = [out if isinstance(out[0], tuple) else (out, F32) for out in outs]
    return pl.pallas_call(
        kernel,
        out_shape=tuple(jax.ShapeDtypeStruct(shape, kind) for shape, kind in shapes),
        in_specs=[
            pl.BlockSpec(memory_space=pltpu.SMEM if i in smem else pltpu.VMEM) for i in range(len(args))
        ],
        out_specs=tuple(pl.BlockSpec(memory_space=pltpu.VMEM) for _ in outs),
        cost_estimate=pl.CostEstimate(flops=int(cost * 1e9), bytes_accessed=1 << 20, transcendentals=0),
        compiler_params=pltpu.CompilerParams(vmem_limit_bytes=24 << 20),
    )(*args)


def swap(x, axis, apart):
    return lax.ppermute(x, axis, [(i, i ^ 1 << apart) for i in range(lax.axis_size(axis))])


def far_scan(section, count, place):
    def dot(left, right):
        return jnp.dot(left, right, precision=lax.Precision.HIGHEST)

    width = section.shape[1]
    own_map, own = section[:width], section[width:]
    ahead_map, ahead = jnp.eye(width, dtype=F32), jnp.zeros_like(own)
    for bit in range(count.bit_length() - 2):
        got = swap(jnp.concatenate([own_map, own], 0), "seq", bit)
        got_map, got = got[:width], got[width:]
        low = (place >> bit) % 2 == 0
        ahead = jnp.where(low, dot(ahead_map, got) + ahead, ahead)
        ahead_map = jnp.where(low, dot(ahead_map, got_map), ahead_map)
        low_map, high_map = jnp.where(low, own_map, got_map), jnp.where(low, got_map, own_map)
        own = dot(low_map, jnp.where(low, got, own)) + jnp.where(low, own, got)
        own_map = dot(low_map, high_map)
    return own, jnp.concatenate([ahead_map, ahead], 0)


def per_device(queries, key_rows, values, log_decay, beta_rate, start_states, output_grad):
    count = lax.axis_size("seq")
    stages = count.bit_length() - 1
    assert count == 1 << stages and stages >= 2
    place = lax.axis_index("seq")
    parity = lax.axis_index("head") % 2
    q_t, k_t = queries.T, key_rows.T
    half, length = q_t.shape
    width = 2 * half
    depth = values.shape[1]
    start = start_states[0, 0]
    square, tall, wide, thin = (length, length), (length, depth), (width, length), (1, length)
    k_other = swap(k_t, "head", 0)
    q_other = swap(q_t, "head", 0)
    low_first = 1 - place % 2 if stages == 2 else place * 0 + 1
    low_last = 1 - (place >> (stages - 1)) % 2
    flags = jnp.stack([low_first, low_last, 1 - parity] + [parity] * 5).astype(F32)
    spread, damp, kk_own, qk_own, rows, mask = call(
        prep_kernel, [square, square, square, square, (8, length), (8, depth)],
        flags, q_t, k_t, log_decay, beta_rate, smem=(0,),
    )
    inv, w_t, kk, scale = call(
        inverse_kernel, [square, wide, square, (2, length)], k_t, k_other, kk_own, damp, rows
    )
    section, score, q_scale = call(
        shift_kernel, [(2 * width, depth), square, thin],
        q_t, q_other, k_t, k_other, output_grad, qk_own, spread, rows, scale, w_t,
    )
    if stages == 2:
        ahead = swap(section, "seq", 0)
        (total,) = call(join_kernel, [(width, depth)], mask, section, ahead)
    else:
        total, ahead = far_scan(section, count, place)
    arrived = swap(total, "seq", stages - 1)
    u, base, score_grad, start_t, keep_q, send_q = call(
        update_kernel, [tall, tall, square, (width, depth), (half, length), (half, length)],
        mask, q_t, q_other, k_t, k_other, values, output_grad, start, inv, spread, rows, scale, q_scale,
    )
    got_q = swap(send_q, "head", 0)
    shapes = [(depth, length), (length, width), wide, wide, (width, depth), (width, width)]
    *packs, y, dk = call(
        local_kernel, [(shape, BF16) for shape in shapes for _ in range(2)] + [tall, wide],
        mask, q_t, q_other, k_t, k_other, output_grad, start_t, inv, score, damp, rows, scale, q_scale, u, score_grad, ahead,
        total,
    )
    send, keep = call(
        far_kernel, [(half, length), (half, length)],
        mask, arrived, k_t, k_other, damp, rows, scale, *packs, dk,
    )
    got_k = swap(send, "head", 0)
    value_grad, rate_grad, query_grad = call(
        value_kernel, [tall, thin, (half, length)],
        mask, arrived, packs[2], packs[3], y, base, kk, spread, scale, rows, u, keep_q, got_q,
    )
    (key_grad,) = call(add_kernel, [(half, length)], keep, got_k)
    return (query_grad.T, key_grad.T, value_grad, rate_grad)


def solution(mesh):
    in_specs = (
        P("seq", "head"),
        P("seq", "head"),
        P("seq", "head"),
        P("head", "seq"),
        P("head", "seq"),
        P("seq", "head", None, None),
        P("seq", "head"),
    )
    out_specs = (P("seq", "head"), P("seq", "head"), P("seq", "head"), P("head", "seq"))

    return jax.shard_map(per_device, mesh=mesh, in_specs=in_specs, out_specs=out_specs, check_vma=False)
```

time: 23.5 us -> 22.4 us (0.953)
  starting transfers between devices: 7.72 us -> 7.3 us
  Pallas kernels: 9.24 us -> 8.84 us
  waiting for transfers between devices: 4.78 us -> 4.53 us
    ppermute x7 -> x6, starting transfers between devices: 7.72 us -> 7.3 us  [swap(): lax.ppermute(x, axis, [(i, i ^ 1 << apart) for i in range(lax.axis_size(a...]
    pallas_call x9, Pallas kernels: 9.24 us -> 8.84 us  [call(): pl.pallas_call(kernel, out_shape=tuple((jax.ShapeDtypeStruct(shape, kind)...]
    ppermute x7 -> x6, waiting for transfers between devices: 4.78 us -> 4.53 us  [swap(): lax.ppermute(x, axis, [(i, i ^ 1 << apart) for i in range(lax.axis_size(a...]
  transfers between devices with their start and end apart: 7 -> 6, of which waited for: 3 -> 4; matrix products, arithmetic and copies ran while one was open for 0% -> 0% of each run, Pallas kernels for 34% -> 34%
where the time goes in v3:
time: 22.4 us; the launch traced here: 22.2 us
  Pallas kernels  8.84 us (39%)
  starting transfers between devices  7.3 us (33%)
  waiting for transfers between devices  4.53 us (20%)
  local copies, waits for them, and re-layouts  0.84 us (4%)
  between operations  0.7 us (3%)
    pallas_call x9, Pallas kernels, call(): pl.pallas_call(kernel, out_shape=tuple((jax.ShapeDtypeStruct(shape, kind)...  8.84 us
    ppermute x6, starting transfers between devices, swap(): lax.ppermute(x, axis, [(i, i ^ 1 << apart) for i in range(lax.axis_size(a...  7.3 us
    ppermute x6, waiting for transfers between devices, swap(): lax.ppermute(x, axis, [(i, i ^ 1 << apart) for i in range(lax.axis_size(a...  4.53 us
    unnamed x14, local copies, waits for them, and re-layouts  0.76 us
  transfers between devices with their start and end apart: 6, of which 4 were waited for; matrix products, arithmetic and copies ran while one was open for 0% of the time, Pallas kernels for 34%

profile of v3, /device:TPU:0, one launch (start us, length us, event | category | flops | bytes accessed | tf_op | source)
XLA Modules:
  0.0 22.2 jit_solution(10181079741773780949)
XLA Ops:
  0.6 3.0 %collective-permute-start.1 = (bf16[64,256]{1,0:T(8,128)(2,1)}, bf16[64,256]{1,0:T(8,128)(2,1)S(1)}, u32[]{:S(2)}, u32[]{:S(2)}) collective-permute-start(bf16[64,256]{1,0:T(8,128)(2,1)} %bitcast.15), channel_id=1, source_target_pairs={{0,1},{1,0},{2,3},{3,2},{4,5},{5,4},{6,7},{7,6},{8,9},{9,8},{10,11... | collective-permute-start | bytes 98312 | tf_op jit(solution)/shard_map/ppermute | solution.py:303
  3.7 0.1 collective-permute-start
  3.7 0.1 stack.23
  3.8 0.6 %copy-done.6 = f32[1,256]{1,0:T(1,128)S(1)} copy-done((f32[1,256]{1,0:T(1,128)S(1)}, f32[1,256]{1,0:T(1,128)}, u32[]{:S(2)}) %copy-start.6) | copy-done | bytes 1048
  4.4 0.1 copy-done.4
  4.5 0.0 copy-done.3
  4.5 0.9 %shard_map.102 = (f32[256,256]{1,0:T(8,128)S(1)}, f32[256,256]{1,0:T(8,128)S(1)}, f32[256,256]{1,0:T(8,128)S(1)}, f32[256,256]{1,0:T(8,128)S(1)}, f32[8,256]{1,0:T(8,128)S(1)}, /*index=5*/f32[8,128]{1,0:T(8,128)S(1)}) custom-call(f32[8]{0:T(128)S(1)} %convert_element_type.3.flag_ref, bf16[64,256]{1,0:T(8,128)(2,1)S(1)} %bitcast.11, ...), custom_call_target="tpu_custom_call" | custom-call | flops 1000000000 | bytes 1048576 | tf_op jit(solution)/shard_map/pallas_call | solution.py:290
  5.4 0.4 %collective-permute-done.1.other_ref.k_other_ref = bf16[64,256]{1,0:T(8,128)(2,1)S(1)} collective-permute-done((bf16[64,256]{1,0:T(8,128)(2,1)}, bf16[64,256]{1,0:T(8,128)(2,1)S(1)}, u32[]{:S(2)}, u32[]{:S(2)}) %collective-permute-start.1) | collective-permute-done | bytes 32800 | tf_op jit(solution)/shard_map/ppermute | solution.py:303
  5.8 1.9 %shard_map.103 = (f32[256,256]{1,0:T(8,128)S(1)}, f32[128,256]{1,0:T(8,128)S(1)}, f32[256,256]{1,0:T(8,128)S(1)}, f32[2,256]{1,0:T(2,128)S(1)}) custom-call(bf16[64,256]{1,0:T(8,128)(2,1)S(1)} %bitcast.17, bf16[64,256]{1,0:T(8,128)(2,1)S(1)} %collective-permute-done.1.other_ref.k_other_ref, f32[256,256]{1,0:T(8,128)S(1)} %get-tuple-element.46.kk_in_ref, ...), custom_call_target="tpu_custom_call" | custom-call | flops 1000000000 | bytes 1048576 | tf_op jit(solution)/shard_map/pallas_call | solution.py:290
  7.6 0.1 collective-permute-done.other_ref.q_other_ref
  7.8 0.7 %shard_map.104 = (f32[256,128]{1,0:T(8,128)S(1)}, f32[256,256]{1,0:T(8,128)S(1)}, f32[1,256]{1,0:T(1,128)S(1)}) custom-call(bf16[64,256]{1,0:T(8,128)(2,1)S(1)} %bitcast.12, bf16[64,256]{1,0:T(8,128)(2,1)S(1)} %collective-permute-done.other_ref.q_other_ref, bf16[64,256]{1,0:T(8,128)(2,1)S(1)} %bitcast.18, ...), custom_call_target="tpu_custom_call" | custom-call | flops 1000000000 | bytes 1048576 | tf_op jit(solution)/shard_map/pallas_call | solution.py:290
  8.5 0.1 collective-permute-start.2
  8.6 0.0 copy-done.1
  8.7 1.1 %shard_map.106 = (f32[256,128]{1,0:T(8,128)S(1)}, f32[256,128]{1,0:T(8,128)S(1)}, f32[256,256]{1,0:T(8,128)S(1)}, f32[128,128]{1,0:T(8,128)S(1)}, f32[64,256]{1,0:T(8,128)S(1)}, /*index=5*/f32[64,256]{1,0:T(8,128)S(1)}) custom-call(f32[8,128]{1,0:T(8,128)S(1)} %get-tuple-element.42.mask_ref, bf16[64,256]{1,0:T(8,128)(2,1)S(1)} %bitcast.13, ...), custom_call_target="tpu_custom_call" | custom-call | flops 1000000000 | bytes 1048576 | tf_op jit(solution)/shard_map/pallas_call | solution.py:290
  9.8 2.0 %collective-permute-start.4 = (f32[64,256]{1,0:T(8,128)S(1)}, f32[64,256]{1,0:T(8,128)S(1)}, u32[]{:S(2)}, u32[]{:S(2)}) collective-permute-start(f32[64,256]{1,0:T(8,128)S(1)} %get-tuple-element.63), channel_id=1, source_target_pairs={{0,1},{1,0},{2,3},{3,2},{4,5},{5,4},{6,7},{7,6},{8,9},{9,8},{10,11... | collective-permute-start | bytes 196616 | tf_op jit(solution)/shard_map/ppermute | solution.py:303
  11.8 0.2 shard_map.105.after_ref
  12.0 1.6 %collective-permute-start.3 = (f32[128,128]{1,0:T(8,128)S(1)}, f32[128,128]{1,0:T(8,128)S(1)}, u32[]{:S(2)}, u32[]{:S(2)}) collective-permute-start(f32[128,128]{1,0:T(8,128)S(1)} %shard_map.105.after_ref), channel_id=1, source_target_pairs={{0,16},{8,24},{16,0},{24,8},{1,17},{9,25},{17,1},{25,9},{2,18},{10... | collective-permute-start | bytes 196616 | tf_op jit(solution)/shard_map/ppermute | solution.py:303
  13.5 1.4 %shard_map.107 = (bf16[128,256]{1,0:T(8,128)(2,1)S(1)}, bf16[128,256]{1,0:T(8,128)(2,1)S(1)}, bf16[256,128]{1,0:T(8,128)(2,1)S(1)}, bf16[256,128]{1,0:T(8,128)(2...) custom-call(f32[8,128]{1,0:T(8,128)S(1)} %get-tuple-element.42.mask_, ...), custom_call_target="tpu_custom_call" | custom-call | flops 1000000000 | bytes 1048576 | tf_op jit(solution)/shard_map/pallas_call | solution.py:290
  14.9 1.4 %collective-permute-done.3.got_ref = f32[128,128]{1,0:T(8,128)S(1)} collective-permute-done((f32[128,128]{1,0:T(8,128)S(1)}, f32[128,128]{1,0:T(8,128)S(1)}, u32[]{:S(2)}, u32[]{:S(2)}) %collective-permute-start.3) | collective-permute-done | bytes 65568 | tf_op jit(solution)/shard_map/ppermute | solution.py:303
  16.3 1.0 %shard_map.109 = (f32[64,256]{1,0:T(8,128)S(1)}, f32[64,256]{1,0:T(8,128)S(1)}) custom-call(f32[8,128]{1,0:T(8,128)S(1)} %get-tuple-element.42.mask_ref, f32[128,128]{1,0:T(8,128)S(1)} %collective-permute-done.3.got_ref, bf16[64,256]{1,0:T(8,128)(2,1)S(1)} %bitcast.21, bf16[64,256]{1,0:T(8,128)(2,1)S(1)} %collective-permute-done.1.other_ref.k_other_ref, ...), custom_call_target="tpu_custom_call" | custom-call | flops 1000000000 | bytes 1048576 | tf_op jit(solution)/shard_map/pallas_call | solution.py:290
  17.2 0.6 %collective-permute-start.5 = (f32[64,256]{1,0:T(8,128)S(1)}, f32[64,256]{1,0:T(8,128)S(1)}, u32[]{:S(2)}, u32[]{:S(2)}) collective-permute-start(f32[64,256]{1,0:T(8,128)S(1)} %get-tuple-element.77), channel_id=1, source_target_pairs={{0,1},{1,0},{2,3},{3,2},{4,5},{5,4},{6,7},{7,6},{8,9},{9,8},{10,11... | collective-permute-start | bytes 196616 | tf_op jit(solution)/shard_map/ppermute | solution.py:303
  17.8 1.1 %shard_map.108 = (f32[256,128]{1,0:T(8,128)}, f32[1,256]{1,0:T(1,128)}, f32[64,256]{1,0:T(8,128)}) custom-call(f32[8,128]{1,0:T(8,128)S(1)} %get-tuple-element.42.mask_ref, f32[128,128]{1,0:T(8,128)S(1)} %collective-permute-done.3.got_ref, bf16[256,128]{1,0:T(8,128)(2,1)S(1)} %get-tuple-element.57.ph_ref, bf16[256,128]{1,0:T(8,128)(2,1)S(1)} %get-tuple-element.58.pl_ref, ...), custom_call_target="tpu_custom_call" | custom-call | flops 1000000000 | bytes 1048576 | tf_op jit(solution)/shard_map/pallas_call | solution.py:290
  19.0 2.6 %collective-permute-done.5.got_ref = f32[64,256]{1,0:T(8,128)S(1)} collective-permute-done((f32[64,256]{1,0:T(8,128)S(1)}, f32[64,256]{1,0:T(8,128)S(1)}, u32[]{:S(2)}, u32[]{:S(2)}) %collective-permute-start.5) | collective-permute-done | bytes 65568 | tf_op jit(solution)/shard_map/ppermute | solution.py:303
  21.6 0.6 %shard_map.110 = f32[64,256]{1,0:T(8,128)} custom-call(f32[64,256]{1,0:T(8,128)S(1)} %get-tuple-element.76.keep_ref, f32[64,256]{1,0:T(8,128)S(1)} %collective-permute-done.5.got_ref), custom_call_target="tpu_custom_call" | custom-call | flops 1000000000 | bytes 1048576 | tf_op jit(solution)/shard_map/pallas_call | solution.py:290
  (13 shorter events, 0.0 us)
Async XLA Ops:
  0.6 5.1 %collective-permute-start.1 = (bf16[64,256]{1,0:T(8,128)(2,1)}, bf16[64,256]{1,0:T(8,128)(2,1)S(1)}, u32[]{:S(2)}, u32[]{:S(2)}) collective-permute-start(bf16[64,256]{1,0:T(8,128)(2,1)} %bitcast.15), channel_id=1, source_target_pairs={{0,1},{1,0},{2,3},{3,2},{4,5},{5,4},{6,7},{7,6},{8,9},{9,8},{10,11... | collective-permute-start | bytes 98312 | tf_op jit(solution)/shard_map/ppermute | solution.py:303
  3.7 4.1 %collective-permute-start = (bf16[64,256]{1,0:T(8,128)(2,1)}, bf16[64,256]{1,0:T(8,128)(2,1)S(1)}, u32[]{:S(2)}, u32[]{:S(2)}) collective-permute-start(bf16[64,256]{1,0:T(8,128)(2,1)} %bitcast.10), channel_id=1, source_target_pairs={{0,1},{1,0},{2,3},{3,2},{4,5},{5,4},{6,7},{7,6},{8,9},{9,8},{10,11... | collective-permute-start | bytes 98312 | tf_op jit(solution)/shard_map/ppermute | solution.py:303
  3.7 0.7 %copy-start.6 = (f32[1,256]{1,0:T(1,128)S(1)}, f32[1,256]{1,0:T(1,128)}, u32[]{:S(2)}) copy-start(f32[1,256]{1,0:T(1,128)} %rate_ref.1) | copy-start | bytes 3076
  3.7 0.8 %copy-start.4 = (bf16[256,64]{0,1:T(8,128)(2,1)S(1)}, bf16[256,64]{0,1:T(8,128)(2,1)}, u32[]{:S(2)}) copy-start(bf16[256,64]{0,1:T(8,128)(2,1)} %param.8) | copy-start | bytes 98308
  3.7 0.8 %copy-start.3 = (bf16[256,64]{0,1:T(8,128)(2,1)S(1)}, bf16[256,64]{0,1:T(8,128)(2,1)}, u32[]{:S(2)}) copy-start(bf16[256,64]{0,1:T(8,128)(2,1)} %param.7) | copy-start | bytes 98308
  3.8 0.7 %copy-start.5 = (f32[1,256]{1,0:T(1,128)S(1)}, f32[1,256]{1,0:T(1,128)}, u32[]{:S(2)}) copy-start(f32[1,256]{1,0:T(1,128)} %decay_ref.1) | copy-start | bytes 3076
  5.8 2.0 %copy-start.2 = (bf16[256,128]{1,0:T(8,128)(2,1)S(1)}, bf16[256,128]{1,0:T(8,128)(2,1)}, u32[]{:S(2)}) copy-start(bf16[256,128]{1,0:T(8,128)(2,1)} %g_ref.5) | copy-start | bytes 196612
  7.8 0.8 %copy-start = (bf16[256,128]{1,0:T(8,128)(2,1)S(1)}, bf16[256,128]{1,0:T(8,128)(2,1)}, u32[]{:S(2)}) copy-start(bf16[256,128]{1,0:T(8,128)(2,1)} %v_ref.1) | copy-start | bytes 196612
  7.8 0.9 %copy-start.1 = (f32[1,1,128,128]{3,2,1,0:T(8,128)S(1)}, f32[1,1,128,128]{3,2,1,0:T(8,128)}, u32[]{:S(2)}) copy-start(f32[1,1,128,128]{3,2,1,0:T(8,128)} %param.12) | copy-start | bytes 196612
  8.5 3.2 %collective-permute-start.2 = (f32[256,128]{1,0:T(8,128)S(1)}, f32[256,128]{1,0:T(8,128)S(1)}, u32[]{:S(2)}, u32[]{:S(2)}) collective-permute-start(f32[256,128]{1,0:T(8,128)S(1)} %get-tuple-element.50.own_ref), channel_id=1, source_target_pairs={{0,8},{8,0},{16,24},{24,16},{1,9},{9,1},{17,25},{25,17},{2,10},{10... | collective-permute-start | bytes 393224 | tf_op jit(solution)/shard_map/ppermute | solution.py:303
  9.8 8.0 %collective-permute-start.4 = (f32[64,256]{1,0:T(8,128)S(1)}, f32[64,256]{1,0:T(8,128)S(1)}, u32[]{:S(2)}, u32[]{:S(2)}) collective-permute-start(f32[64,256]{1,0:T(8,128)S(1)} %get-tuple-element.63), channel_id=1, source_target_pairs={{0,1},{1,0},{2,3},{3,2},{4,5},{5,4},{6,7},{7,6},{8,9},{9,8},{10,11... | collective-permute-start | bytes 196616 | tf_op jit(solution)/shard_map/ppermute | solution.py:303
  12.0 4.3 %collective-permute-start.3 = (f32[128,128]{1,0:T(8,128)S(1)}, f32[128,128]{1,0:T(8,128)S(1)}, u32[]{:S(2)}, u32[]{:S(2)}) collective-permute-start(f32[128,128]{1,0:T(8,128)S(1)} %shard_map.105.after_ref), channel_id=1, source_target_pairs={{0,16},{8,24},{16,0},{24,8},{1,17},{9,25},{17,1},{25,9},{2,18},{10... | collective-permute-start | bytes 196616 | tf_op jit(solution)/shard_map/ppermute | solution.py:303
  17.2 4.3 %collective-permute-start.5 = (f32[64,256]{1,0:T(8,128)S(1)}, f32[64,256]{1,0:T(8,128)S(1)}, u32[]{:S(2)}, u32[]{:S(2)}) collective-permute-start(f32[64,256]{1,0:T(8,128)S(1)} %get-tuple-element.77), channel_id=1, source_target_pairs={{0,1},{1,0},{2,3},{3,2},{4,5},{5,4},{6,7},{7,6},{8,9},{9,8},{10,11... | collective-permute-start | bytes 196616 | tf_op jit(solution)/shard_map/ppermute | solution.py:303

commit v4 on v3

--- a/solution.py
+++ b/solution.py
@@ -8,6 +8,7 @@
 F32 = jnp.float32
 BF16 = jnp.bfloat16
 BASE = 32
+PACK = 128
 NN = (((1,), (0,)), ((), ()))
 NT = (((1,), (1,)), ((), ()))
 
@@ -20,15 +21,39 @@
 def mm(left, right, dims=NN):
     left = left if isinstance(left, tuple) else (left if left.dtype == BF16 else split(left))
     right = right if isinstance(right, tuple) else (right if right.dtype == BF16 else split(right))
+    deep, out = (0, 1) if dims is NN else (1, 0)
 
     def one(a, b):
         return lax.dot_general(a, b, dims, preferred_element_type=F32)
 
-    if isinstance(left, tuple) and isinstance(right, tuple):
-        return one(left[0], right[0]) + (one(left[0], right[1]) + one(left[1], right[0]))
-    if isinstance(left, tuple):
+    def join(parts, axis):
+        return jnp.concatenate(parts, axis)
+
+    pair_left, pair_right = isinstance(left, tuple), isinstance(right, tuple)
+    shape = (right[0] if pair_right else right).shape
+    shallow, thin = shape[deep] == PACK, shape[out] == PACK
+    if pair_left and pair_right:
+        high, low = right
+        if shallow and thin:
+            block = join([join([high, low], out), join([high, jnp.zeros_like(low)], out)], deep)
+            both = one(join(left, 1), block)
+            return both[:, :PACK] + both[:, PACK:]
+        if shallow:
+            return one(join(left, 1), join([high, high], deep)) + one(left[0], low)
+        if thin:
+            both = one(left[0], join(right, out))
+            return both[:, :PACK] + both[:, PACK:] + one(left[1], high)
+        return one(left[0], high) + (one(left[0], low) + one(left[1], high))
+    if pair_left:
+        if shallow:
+            return one(join(left, 1), join([right, right], deep))
         return one(left[0], right) + one(left[1], right)
-    if isinstance(right, tuple):
+    if pair_right:
+        if shallow:
+            return one(join([left, left], 1), join(right, deep))
+        if thin:
+            both = one(left, join(right, out))
+            return both[:, :PACK] + both[:, PACK:]
         return one(left, right[0]) + one(left, right[1])
     return one(left, right)
 
@@ -88,14 +113,6 @@
     return found
 
 
-def inverse(nil):
-    half = nil.shape[0] // 2
-    upper, lower = inverses([nil[:half, :half], nil[half:, half:]])
-    corner = mm(mm(lower, nil[half:, :half]), upper)
-    top = jnp.concatenate([upper, jnp.zeros((half, half), F32)], 1)
-    return jnp.concatenate([top, jnp.concatenate([corner, lower], 1)], 0)
-
-
 def decays(decay_row, row, lane):
     cum_col = jnp.sum(jnp.where(lane <= row, decay_row, 0.0), 1, keepdims=True)
     return cum_col, to_row(cum_col, row == lane)
@@ -126,38 +143,53 @@
     other = other_ref[...]
     other_f = other.astype(F32)
     k_t = jnp.concatenate([k_ref[...], other], 0)
+    mid = k_t.shape[1] // 2
     grow, rate_row, k_sum = (rows_ref[i : i + 1, :] for i in (1, 3, 4))
     square = k_sum + jnp.sum(other_f * other_f, 0, keepdims=True) + 1e-6
     k_scale = 1.0 / jnp.sqrt(square)
     kk = kk_in_ref[...] + mm(other_f.T.astype(BF16), other)
-    inv = inverse(damp_ref[...] * (kk * (k_scale * k_scale)))
-    w_ref[...] = mm(k_t, inv * (rate_row * grow), NT) * k_scale
-    inv_ref[...] = inv
+    nil = damp_ref[...] * (kk * (k_scale * k_scale))
+    upper, lower = inverses([nil[:mid, :mid], nil[mid:, mid:]])
+    keys = k_t.astype(F32) * (rate_row * grow)
+    corner = nil[mid:, :mid]
+    first = mm(keys[:, :mid], upper, NT)
+    second = mm(mm(first, corner, NT) + keys[:, mid:], lower, NT)
+    w_ref[...] = jnp.concatenate([first, second], 1) * k_scale
+    inv_ref[...] = jnp.concatenate(
+        [jnp.concatenate([upper, jnp.zeros_like(upper)], 1), jnp.concatenate([corner, lower], 1)], 0
+    )
     kk_ref[...] = kk
     scale_ref[...] = jnp.concatenate([k_scale, square * k_scale], 0)
 
 
 def shift_kernel(
-    q_ref, other_ref, k_ref, k_other_ref, g_ref, qk_ref, spread_ref, rows_ref, scale_ref, w_ref,
-    map_ref, score_ref, q_scale_ref,
+    q_ref, other_ref, k_ref, k_other_ref, g_ref, qk_ref, spread_ref, rows_ref, scale_ref, w_ref, inv_in_ref,
+    map_ref, score_ref, q_scale_ref, inv_ref,
 ):
     other = other_ref[...]
     other_f = other.astype(F32)
     k_t = jnp.concatenate([k_ref[...], k_other_ref[...]], 0)
     q_f = jnp.concatenate([q_ref[...].astype(F32), other_f], 0)
     width, length = k_t.shape
+    mid = length // 2
     k_scale, grow, tail = scale_ref[0:1, :], rows_ref[1:2, :], rows_ref[2:3, :]
     score = spread_ref[...] * (qk_ref[...] + mm(other_f.T.astype(BF16), k_other_ref[...]))
+    lower = split(inv_in_ref[mid:, mid:])
+    corner = mm(lower, inv_in_ref[mid:, :mid])
+    w_t = w_ref[...] * k_scale
+    w_row, w_lane = ids((width, width))
+    side = mm(w_t, score, NT)
     q_sum = rows_ref[5:6, :] + jnp.sum(other_f * other_f, 0, keepdims=True)
     q_scale = width ** (-0.5) / jnp.sqrt(q_sum + 1e-6)
-    w_t = w_ref[...] * k_scale
-    w_row, w_lane = ids((width, width))
     own_map = jnp.where(w_row == w_lane, grow[:, length - 1 :], 0.0) - mm(w_t * tail, k_t, NT)
-    side = q_scale * (q_f * grow - mm(w_t, score, NT))
+    corner = mm(corner, inv_in_ref[:mid, :mid])
+    side = q_scale * (q_f * grow - side)
+    map_ref[width:, :] = mm(side, g_ref[...])
     map_ref[0:width, :] = own_map
     score_ref[...] = score
     q_scale_ref[...] = q_scale
-    map_ref[width:, :] = mm(side, g_ref[...])
+    inv_ref[0:mid, :] = inv_in_ref[0:mid, :]
+    inv_ref[mid:, :] = jnp.concatenate([corner, inv_in_ref[mid:, mid:]], 1)
 
 
 def join_kernel(mask_ref, own_ref, got_ref, total_ref):
@@ -343,12 +375,12 @@
         prep_kernel, [square, square, square, square, (8, length), (8, depth)],
         flags, q_t, k_t, log_decay, beta_rate, smem=(0,),
     )
-    inv, w_t, kk, scale = call(
+    halves, w_t, kk, scale = call(
         inverse_kernel, [square, wide, square, (2, length)], k_t, k_other, kk_own, damp, rows
     )
-    section, score, q_scale = call(
-        shift_kernel, [(2 * width, depth), square, thin],
-        q_t, q_other, k_t, k_other, output_grad, qk_own, spread, rows, scale, w_t,
+    section, score, q_scale, inv = call(
+        shift_kernel, [(2 * width, depth), square, thin, square],
+        q_t, q_other, k_t, k_other, output_grad, qk_own, spread, rows, scale, w_t, halves,
     )
     if stages == 2:
         ahead = swap(section, "seq", 0)

time: 22.4 us -> 21.9 us (0.978)
  Pallas kernels: 8.84 us -> 8.23 us
  waiting for transfers between devices: 4.53 us -> 4.89 us
  starting transfers between devices: 7.3 us -> 7.03 us
    pallas_call x9, Pallas kernels: 8.84 us -> 8.23 us  [call(): pl.pallas_call(kernel, out_shape=tuple((jax.ShapeDtypeStruct(shape, kind)...]
    ppermute x6, waiting for transfers between devices: 4.53 us -> 4.89 us  [swap(): lax.ppermute(x, axis, [(i, i ^ 1 << apart) for i in range(lax.axis_size(a...]
    ppermute x6, starting transfers between devices: 7.3 us -> 7.03 us  [swap(): lax.ppermute(x, axis, [(i, i ^ 1 << apart) for i in range(lax.axis_size(a...]
  transfers between devices with their start and end apart: 6 -> 6, of which waited for: 4 -> 4; matrix products, arithmetic and copies ran while one was open for 0% -> 0% of each run, Pallas kernels for 34% -> 32%
where the time goes in v4:
time: 21.9 us; the launch traced here: 21.7 us
  Pallas kernels  8.23 us (38%)
  starting transfers between devices  7.03 us (32%)
  waiting for transfers between devices  4.89 us (22%)
  local copies, waits for them, and re-layouts  0.85 us (4%)
  between operations  0.7 us (3%)
    pallas_call x9, Pallas kernels, call(): pl.pallas_call(kernel, out_shape=tuple((jax.ShapeDtypeStruct(shape, kind)...  8.23 us
    ppermute x6, starting transfers between devices, swap(): lax.ppermute(x, axis, [(i, i ^ 1 << apart) for i in range(lax.axis_size(a...  7.03 us
    ppermute x6, waiting for transfers between devices, swap(): lax.ppermute(x, axis, [(i, i ^ 1 << apart) for i in range(lax.axis_size(a...  4.89 us
    unnamed x14, local copies, waits for them, and re-layouts  0.77 us
  transfers between devices with their start and end apart: 6, of which 4 were waited for; matrix products, arithmetic and copies ran while one was open for 0% of the time, Pallas kernels for 32%

profile of v4, /device:TPU:0, one launch (start us, length us, event | category | flops | bytes accessed | tf_op | source)
XLA Modules:
  0.0 21.7 jit_solution(5917755950672801530)
XLA Ops:
  0.6 3.0 %collective-permute-start.1 = (bf16[64,256]{1,0:T(8,128)(2,1)}, bf16[64,256]{1,0:T(8,128)(2,1)S(1)}, u32[]{:S(2)}, u32[]{:S(2)}) collective-permute-start(bf16[64,256]{1,0:T(8,128)(2,1)} %bitcast.15), channel_id=1, source_target_pairs={{0,1},{1,0},{2,3},{3,2},{4,5},{5,4},{6,7},{7,6},{8,9},{9,8},{10,11... | collective-permute-start | bytes 98312 | tf_op jit(solution)/shard_map/ppermute | solution.py:335
  3.7 0.1 collective-permute-start
  3.7 0.1 stack.23
  3.8 0.6 %copy-done.6 = f32[1,256]{1,0:T(1,128)S(1)} copy-done((f32[1,256]{1,0:T(1,128)S(1)}, f32[1,256]{1,0:T(1,128)}, u32[]{:S(2)}) %copy-start.6) | copy-done | bytes 1048
  4.4 0.1 copy-done.4
  4.5 0.9 %shard_map.102 = (f32[256,256]{1,0:T(8,128)S(1)}, f32[256,256]{1,0:T(8,128)S(1)}, f32[256,256]{1,0:T(8,128)S(1)}, f32[256,256]{1,0:T(8,128)S(1)}, f32[8,256]{1,0:T(8,128)S(1)}, /*index=5*/f32[8,128]{1,0:T(8,128)S(1)}) custom-call(f32[8]{0:T(128)S(1)} %convert_element_type.3.flag_ref, bf16[64,256]{1,0:T(8,128)(2,1)S(1)} %bitcast.11, ...), custom_call_target="tpu_custom_call" | custom-call | flops 1000000000 | bytes 1048576 | tf_op jit(solution)/shard_map/pallas_call | solution.py:322
  5.4 0.4 %collective-permute-done.1.other_ref.k_other_ref = bf16[64,256]{1,0:T(8,128)(2,1)S(1)} collective-permute-done((bf16[64,256]{1,0:T(8,128)(2,1)}, bf16[64,256]{1,0:T(8,128)(2,1)S(1)}, u32[]{:S(2)}, u32[]{:S(2)}) %collective-permute-start.1) | collective-permute-done | bytes 32800 | tf_op jit(solution)/shard_map/ppermute | solution.py:335
  5.8 1.6 %shard_map.103 = (f32[256,256]{1,0:T(8,128)S(1)}, f32[128,256]{1,0:T(8,128)S(1)}, f32[256,256]{1,0:T(8,128)S(1)}, f32[2,256]{1,0:T(2,128)S(1)}) custom-call(bf16[64,256]{1,0:T(8,128)(2,1)S(1)} %bitcast.17, bf16[64,256]{1,0:T(8,128)(2,1)S(1)} %collective-permute-done.1.other_ref.k_other_ref, f32[256,256]{1,0:T(8,128)S(1)} %get-tuple-element.47.kk_in_ref, ...), custom_call_target="tpu_custom_call" | custom-call | flops 1000000000 | bytes 1048576 | tf_op jit(solution)/shard_map/pallas_call | solution.py:322
  7.4 0.4 %collective-permute-done.other_ref.q_other_ref = bf16[64,256]{1,0:T(8,128)(2,1)S(1)} collective-permute-done((bf16[64,256]{1,0:T(8,128)(2,1)}, bf16[64,256]{1,0:T(8,128)(2,1)S(1)}, u32[]{:S(2)}, u32[]{:S(2)}) %collective-permute-start) | collective-permute-done | bytes 32800 | tf_op jit(solution)/shard_map/ppermute | solution.py:335
  7.8 0.7 %shard_map.104 = (f32[256,128]{1,0:T(8,128)S(1)}, f32[256,256]{1,0:T(8,128)S(1)}, f32[1,256]{1,0:T(1,128)S(1)}, f32[256,256]{1,0:T(8,128)S(1)}) custom-call(bf16[64,256]{1,0:T(8,128)(2,1)S(1)} %bitcast.12, bf16[64,256]{1,0:T(8,128)(2,1)S(1)} %collective-permute-done.other_ref.q_other_ref, bf16[64,256]{1,0:T(8,128)(2,1)S(1)} %bitcast.18, ...), custom_call_target="tpu_custom_call" | custom-call | flops 1000000000 | bytes 1048576 | tf_op jit(solution)/shard_map/pallas_call | solution.py:322
  8.5 0.1 collective-permute-start.2
  8.6 0.0 copy-done
  8.6 0.0 copy-done.1
  8.7 0.9 %shard_map.106 = (f32[256,128]{1,0:T(8,128)S(1)}, f32[256,128]{1,0:T(8,128)S(1)}, f32[256,256]{1,0:T(8,128)S(1)}, f32[128,128]{1,0:T(8,128)S(1)}, f32[64,256]{1,0:T(8,128)S(1)}, /*index=5*/f32[64,256]{1,0:T(8,128)S(1)}) custom-call(f32[8,128]{1,0:T(8,128)S(1)} %get-tuple-element.43.mask_ref, bf16[64,256]{1,0:T(8,128)(2,1)S(1)} %bitcast.13, ...), custom_call_target="tpu_custom_call" | custom-call | flops 1000000000 | bytes 1048576 | tf_op jit(solution)/shard_map/pallas_call | solution.py:322
  9.6 1.7 %collective-permute-start.4 = (f32[64,256]{1,0:T(8,128)S(1)}, f32[64,256]{1,0:T(8,128)S(1)}, u32[]{:S(2)}, u32[]{:S(2)}) collective-permute-start(f32[64,256]{1,0:T(8,128)S(1)} %get-tuple-element.65), channel_id=1, source_target_pairs={{0,1},{1,0},{2,3},{3,2},{4,5},{5,4},{6,7},{7,6},{8,9},{9,8},{10,11... | collective-permute-start | bytes 196616 | tf_op jit(solution)/shard_map/ppermute | solution.py:335
  11.3 0.2 shard_map.105.after_ref
  11.5 1.6 %collective-permute-start.3 = (f32[128,128]{1,0:T(8,128)S(1)}, f32[128,128]{1,0:T(8,128)S(1)}, u32[]{:S(2)}, u32[]{:S(2)}) collective-permute-start(f32[128,128]{1,0:T(8,128)S(1)} %shard_map.105.after_ref), channel_id=1, source_target_pairs={{0,16},{8,24},{16,0},{24,8},{1,17},{9,25},{17,1},{25,9},{2,18},{10... | collective-permute-start | bytes 196616 | tf_op jit(solution)/shard_map/ppermute | solution.py:335
  13.1 1.3 %shard_map.107 = (bf16[128,256]{1,0:T(8,128)(2,1)S(1)}, bf16[128,256]{1,0:T(8,128)(2,1)S(1)}, bf16[256,128]{1,0:T(8,128)(2,1)S(1)}, bf16[256,128]{1,0:T(8,128)(2...) custom-call(f32[8,128]{1,0:T(8,128)S(1)} %get-tuple-element.43.mask_, ...), custom_call_target="tpu_custom_call" | custom-call | flops 1000000000 | bytes 1048576 | tf_op jit(solution)/shard_map/pallas_call | solution.py:322
  14.4 1.4 %collective-permute-done.3.got_ref = f32[128,128]{1,0:T(8,128)S(1)} collective-permute-done((f32[128,128]{1,0:T(8,128)S(1)}, f32[128,128]{1,0:T(8,128)S(1)}, u32[]{:S(2)}, u32[]{:S(2)}) %collective-permute-start.3) | collective-permute-done | bytes 65568 | tf_op jit(solution)/shard_map/ppermute | solution.py:335
  15.8 0.9 %shard_map.109 = (f32[64,256]{1,0:T(8,128)S(1)}, f32[64,256]{1,0:T(8,128)S(1)}) custom-call(f32[8,128]{1,0:T(8,128)S(1)} %get-tuple-element.43.mask_ref, f32[128,128]{1,0:T(8,128)S(1)} %collective-permute-done.3.got_ref, bf16[64,256]{1,0:T(8,128)(2,1)S(1)} %bitcast.21, bf16[64,256]{1,0:T(8,128)(2,1)S(1)} %collective-permute-done.1.other_ref.k_other_ref, ...), custom_call_target="tpu_custom_call" | custom-call | flops 1000000000 | bytes 1048576 | tf_op jit(solution)/shard_map/pallas_call | solution.py:322
  16.7 0.6 %collective-permute-start.5 = (f32[64,256]{1,0:T(8,128)S(1)}, f32[64,256]{1,0:T(8,128)S(1)}, u32[]{:S(2)}, u32[]{:S(2)}) collective-permute-start(f32[64,256]{1,0:T(8,128)S(1)} %get-tuple-element.79), channel_id=1, source_target_pairs={{0,1},{1,0},{2,3},{3,2},{4,5},{5,4},{6,7},{7,6},{8,9},{9,8},{10,11... | collective-permute-start | bytes 196616 | tf_op jit(solution)/shard_map/ppermute | solution.py:335
  17.3 1.1 %shard_map.108 = (f32[256,128]{1,0:T(8,128)}, f32[1,256]{1,0:T(1,128)}, f32[64,256]{1,0:T(8,128)}) custom-call(f32[8,128]{1,0:T(8,128)S(1)} %get-tuple-element.43.mask_ref, f32[128,128]{1,0:T(8,128)S(1)} %collective-permute-done.3.got_ref, bf16[256,128]{1,0:T(8,128)(2,1)S(1)} %get-tuple-element.59.ph_ref, bf16[256,128]{1,0:T(8,128)(2,1)S(1)} %get-tuple-element.60.pl_ref, ...), custom_call_target="tpu_custom_call" | custom-call | flops 1000000000 | bytes 1048576 | tf_op jit(solution)/shard_map/pallas_call | solution.py:322
  18.4 2.7 %collective-permute-done.5.got_ref = f32[64,256]{1,0:T(8,128)S(1)} collective-permute-done((f32[64,256]{1,0:T(8,128)S(1)}, f32[64,256]{1,0:T(8,128)S(1)}, u32[]{:S(2)}, u32[]{:S(2)}) %collective-permute-start.5) | collective-permute-done | bytes 65568 | tf_op jit(solution)/shard_map/ppermute | solution.py:335
  21.1 0.6 %shard_map.110 = f32[64,256]{1,0:T(8,128)} custom-call(f32[64,256]{1,0:T(8,128)S(1)} %get-tuple-element.78.keep_ref, f32[64,256]{1,0:T(8,128)S(1)} %collective-permute-done.5.got_ref), custom_call_target="tpu_custom_call" | custom-call | flops 1000000000 | bytes 1048576 | tf_op jit(solution)/shard_map/pallas_call | solution.py:322
  (13 shorter events, 0.0 us)
Async XLA Ops:
  0.6 5.1 %collective-permute-start.1 = (bf16[64,256]{1,0:T(8,128)(2,1)}, bf16[64,256]{1,0:T(8,128)(2,1)S(1)}, u32[]{:S(2)}, u32[]{:S(2)}) collective-permute-start(bf16[64,256]{1,0:T(8,128)(2,1)} %bitcast.15), channel_id=1, source_target_pairs={{0,1},{1,0},{2,3},{3,2},{4,5},{5,4},{6,7},{7,6},{8,9},{9,8},{10,11... | collective-permute-start | bytes 98312 | tf_op jit(solution)/shard_map/ppermute | solution.py:335
  3.7 4.1 %collective-permute-start = (bf16[64,256]{1,0:T(8,128)(2,1)}, bf16[64,256]{1,0:T(8,128)(2,1)S(1)}, u32[]{:S(2)}, u32[]{:S(2)}) collective-permute-start(bf16[64,256]{1,0:T(8,128)(2,1)} %bitcast.10), channel_id=1, source_target_pairs={{0,1},{1,0},{2,3},{3,2},{4,5},{5,4},{6,7},{7,6},{8,9},{9,8},{10,11... | collective-permute-start | bytes 98312 | tf_op jit(solution)/shard_map/ppermute | solution.py:335
  3.7 0.7 %copy-start.6 = (f32[1,256]{1,0:T(1,128)S(1)}, f32[1,256]{1,0:T(1,128)}, u32[]{:S(2)}) copy-start(f32[1,256]{1,0:T(1,128)} %rate_ref.1) | copy-start | bytes 3076
  3.7 0.8 %copy-start.4 = (bf16[256,64]{0,1:T(8,128)(2,1)S(1)}, bf16[256,64]{0,1:T(8,128)(2,1)}, u32[]{:S(2)}) copy-start(bf16[256,64]{0,1:T(8,128)(2,1)} %param.8) | copy-start | bytes 98308
  3.7 0.8 %copy-start.3 = (bf16[256,64]{0,1:T(8,128)(2,1)S(1)}, bf16[256,64]{0,1:T(8,128)(2,1)}, u32[]{:S(2)}) copy-start(bf16[256,64]{0,1:T(8,128)(2,1)} %param.7) | copy-start | bytes 98308
  3.8 0.7 %copy-start.5 = (f32[1,256]{1,0:T(1,128)S(1)}, f32[1,256]{1,0:T(1,128)}, u32[]{:S(2)}) copy-start(f32[1,256]{1,0:T(1,128)} %decay_ref.1) | copy-start | bytes 3076
  5.8 2.0 %copy-start.2 = (bf16[256,128]{1,0:T(8,128)(2,1)S(1)}, bf16[256,128]{1,0:T(8,128)(2,1)}, u32[]{:S(2)}) copy-start(bf16[256,128]{1,0:T(8,128)(2,1)} %g_ref.5) | copy-start | bytes 196612
  7.8 0.8 %copy-start = (bf16[256,128]{1,0:T(8,128)(2,1)S(1)}, bf16[256,128]{1,0:T(8,128)(2,1)}, u32[]{:S(2)}) copy-start(bf16[256,128]{1,0:T(8,128)(2,1)} %v_ref.1) | copy-start | bytes 196612
  7.8 0.9 %copy-start.1 = (f32[1,1,128,128]{3,2,1,0:T(8,128)S(1)}, f32[1,1,128,128]{3,2,1,0:T(8,128)}, u32[]{:S(2)}) copy-start(f32[1,1,128,128]{3,2,1,0:T(8,128)} %param.12) | copy-start | bytes 196612
  8.5 2.8 %collective-permute-start.2 = (f32[256,128]{1,0:T(8,128)S(1)}, f32[256,128]{1,0:T(8,128)S(1)}, u32[]{:S(2)}, u32[]{:S(2)}) collective-permute-start(f32[256,128]{1,0:T(8,128)S(1)} %get-tuple-element.52.own_ref), channel_id=1, source_target_pairs={{0,8},{8,0},{16,24},{24,16},{1,9},{9,1},{17,25},{25,17},{2,10},{10... | collective-permute-start | bytes 393224 | tf_op jit(solution)/shard_map/ppermute | solution.py:335
  9.6 7.7 %collective-permute-start.4 = (f32[64,256]{1,0:T(8,128)S(1)}, f32[64,256]{1,0:T(8,128)S(1)}, u32[]{:S(2)}, u32[]{:S(2)}) collective-permute-start(f32[64,256]{1,0:T(8,128)S(1)} %get-tuple-element.65), channel_id=1, source_target_pairs={{0,1},{1,0},{2,3},{3,2},{4,5},{5,4},{6,7},{7,6},{8,9},{9,8},{10,11... | collective-permute-start | bytes 196616 | tf_op jit(solution)/shard_map/ppermute | solution.py:335
  11.5 4.3 %collective-permute-start.3 = (f32[128,128]{1,0:T(8,128)S(1)}, f32[128,128]{1,0:T(8,128)S(1)}, u32[]{:S(2)}, u32[]{:S(2)}) collective-permute-start(f32[128,128]{1,0:T(8,128)S(1)} %shard_map.105.after_ref), channel_id=1, source_target_pairs={{0,16},{8,24},{16,0},{24,8},{1,17},{9,25},{17,1},{25,9},{2,18},{10... | collective-permute-start | bytes 196616 | tf_op jit(solution)/shard_map/ppermute | solution.py:335
  16.7 4.3 %collective-permute-start.5 = (f32[64,256]{1,0:T(8,128)S(1)}, f32[64,256]{1,0:T(8,128)S(1)}, u32[]{:S(2)}, u32[]{:S(2)}) collective-permute-start(f32[64,256]{1,0:T(8,128)S(1)} %get-tuple-element.79), channel_id=1, source_target_pairs={{0,1},{1,0},{2,3},{3,2},{4,5},{5,4},{6,7},{7,6},{8,9},{9,8},{10,11... | collective-permute-start | bytes 196616 | tf_op jit(solution)/shard_map/ppermute | solution.py:335

commit v5 on v4

--- a/solution.py
+++ b/solution.py
@@ -32,6 +32,7 @@
     pair_left, pair_right = isinstance(left, tuple), isinstance(right, tuple)
     shape = (right[0] if pair_right else right).shape
     shallow, thin = shape[deep] == PACK, shape[out] == PACK
+    rows = (left[0] if pair_left else left).shape[0]
     if pair_left and pair_right:
         high, low = right
         if shallow and thin:
@@ -41,13 +42,15 @@
         if shallow:
             return one(join(left, 1), join([high, high], deep)) + one(left[0], low)
         if thin:
-            both = one(left[0], join(right, out))
-            return both[:, :PACK] + both[:, PACK:] + one(left[1], high)
-        return one(left[0], high) + (one(left[0], low) + one(left[1], high))
+            both = one(join(left, 0), join(right, out))
+            return both[:rows, :PACK] + (both[:rows, PACK:] + both[rows:, :PACK])
+        both = one(join(left, 0), high)
+        return both[:rows] + (both[rows:] + one(left[0], low))
     if pair_left:
         if shallow:
             return one(join(left, 1), join([right, right], deep))
-        return one(left[0], right) + one(left[1], right)
+        both = one(join(left, 0), right)
+        return both[:rows] + both[rows:]
     if pair_right:
         if shallow:
             return one(join([left, left], 1), join(right, deep))
@@ -236,7 +239,7 @@
 def local_kernel(
     mask_ref, q_ref, q_other_ref, k_ref, k_other_ref, g_ref, start_t_ref, inv_ref, score_ref, damp_ref, rows_ref, scale_ref,
     q_scale_ref, u_ref, score_grad_ref, ahead_ref, after_ref,
-    uth_ref, utl_ref, ph_ref, pl_ref, gh_ref, gl_ref, kh_ref, kl_ref, sh_ref, sl_ref, ah_ref, al_ref, y_ref, dk_ref,
+    uth_ref, utl_ref, uh_ref, ul_ref, ph_ref, pl_ref, pth_ref, ptl_ref, gh_ref, gl_ref, kh_ref, kl_ref, sym_ref, y_ref, dk_ref,
 ):
     length = q_ref.shape[1]
     q_f = jnp.concatenate([q_ref[...], q_other_ref[...]], 0).astype(F32)
@@ -250,46 +253,56 @@
     ahead = jnp.where(low, ahead_ref[width:, :], 0.0)
     grad_t = g_ref[...].astype(F32).T.astype(BF16)
     score = score_ref[...] * to_col(q_scale_ref[...], eye)
-    u_ts = split(u_ref[...].T)
+    u = u_ref[...]
+    u_ts = split(u.T)
     inv = inv_ref[...]
+    damp = damp_ref[...]
     psi_t = mm(k_t, inv * to_col(tail * k_scale * k_scale, eye)) * k_norm
     du_t = mm(grad_t, score) * (k_scale * k_scale)
     psi_s = split(psi_t.T)
     y_t = mm(du_t, inv) * k_norm
+    sym = damp + damp.T
+    sym_ref[...] = sym
     y_t = y_t + mm(ahead.T, psi_t)
     map_s = split(ahead_map)
     psi_far = mm(psi_s, map_s)
     uz_t = mm(ahead, u_ts)
     y = y_t.T
     y_ref[...] = y
-    start_s = split(start_t_ref[...])
-    inner = damp_ref[...] * mm(y, u_ts)
+    start_t = start_t_ref[...]
+    start_s = split(start_t)
+    inner = damp * mm(y, u_ts)
     k_s = split(k_t.astype(F32) * k_scale)
     dk = mm(q_f * q_scale_ref[...], score_grad_ref[...]) - mm(start_s, y_t * (grow * rate_row)) + tail * uz_t
-    ph_ref[...], pl_ref[...] = split(psi_far)
-    gh_ref[...], gl_ref[...] = split(psi_far.T * (grow * rate_row))
-    inner_s = split(inner)
-    dk_ref[...] = dk + (mm(k_s, inner_s) + mm(k_s, inner_s, NT))
+    psi_far_s = split(psi_far)
+    psi_far_t = psi_far.T
+    ph_ref[0:length, :], pl_ref[0:length, :] = psi_far_s
+    ph_ref[length:, :], pl_ref[length:, :] = map_s
+    pth_ref[...], ptl_ref[...] = split(psi_far_t)
+    gh_ref[...], gl_ref[...] = split(psi_far_t * (grow * rate_row))
+    dk_ref[...] = dk + mm(k_s, inner + inner.T)
     uth_ref[...], utl_ref[...] = u_ts
+    uh_ref[0:length, :], ul_ref[0:length, :] = split(u)
+    uh_ref[length:, :], ul_ref[length:, :] = start_s
     kh_ref[...], kl_ref[...] = k_s
-    sh_ref[...], sl_ref[...] = start_s
-    ah_ref[...], al_ref[...] = map_s
 
 
 def far_kernel(
-    mask_ref, got_ref, k_ref, k_other_ref, damp_ref, rows_ref, scale_ref,
-    uth_ref, utl_ref, ph_ref, pl_ref, gh_ref, gl_ref, kh_ref, kl_ref, sh_ref, sl_ref, ah_ref, al_ref, dk_ref,
+    mask_ref, got_ref, k_ref, k_other_ref, rows_ref, scale_ref,
+    uth_ref, utl_ref, uh_ref, ul_ref, ph_ref, pl_ref, pth_ref, ptl_ref, gh_ref, gl_ref, kh_ref, kl_ref, sym_ref, dk_ref,
     send_ref, keep_ref,
 ):
-    half = k_ref.shape[0]
+    half, length = k_ref.shape
     k_scale = scale_ref[0:1, :]
+    row, lane = ids((length, length))
     got_s = split(jnp.where(mask_ref[1:2, :] > 0.0, got_ref[...], 0.0))
     gu_s = split(mm(got_s, (uth_ref[...], utl_ref[...])))
-    sg_s = split(mm((sh_ref[...], sl_ref[...]), got_s, NT))
-    inner_s = split(damp_ref[...] * mm((ph_ref[...], pl_ref[...]), gu_s))
-    dk = dk_ref[...] + rows_ref[2:3, :] * mm((ah_ref[...], al_ref[...]), gu_s) - mm(sg_s, (gh_ref[...], gl_ref[...]))
-    k_s = (kh_ref[...], kl_ref[...])
-    dk = dk + (mm(k_s, inner_s) + mm(k_s, inner_s, NT))
+    right = mm((uh_ref[...], ul_ref[...]), got_s, NT)
+    upper = mm(right[0:length, :], (pth_ref[...], ptl_ref[...]))
+    left = mm((ph_ref[...], pl_ref[...]), gu_s)
+    inner = sym_ref[...] * jnp.where(lane < row, left[0:length, :], upper)
+    dk = dk_ref[...] + rows_ref[2:3, :] * left[length:, :] - mm(right[length:, :], (gh_ref[...], gl_ref[...]))
+    dk = dk + mm((kh_ref[...], kl_ref[...]), inner)
     unit = jnp.concatenate([k_ref[...], k_other_ref[...]], 0).astype(F32) * k_scale
     dk = k_scale * (dk - unit * jnp.sum(unit * dk, 0, keepdims=True))
     send_ref[...] = dk[half:, :]
@@ -306,7 +319,7 @@
     k_scale = scale_ref[0:1, :]
     got = jnp.where(mask_ref[1:2, :] > 0.0, got_ref[...], 0.0)
     low = jnp.where(lane < row, spread_ref[...] * kk_ref[...], 0.0) * (to_col(k_scale, eye) * k_scale)
-    y = y_ref[...] + mm((ph_ref[...], pl_ref[...]), got)
+    y = y_ref[...] + mm((ph_ref[0:length, :], pl_ref[0:length, :]), got)
     write = base_ref[...] - mm(low, u_ref[...])
     value_ref[...] = to_col(rows_ref[3:4, :], eye) * y
     rate_out_ref[...] = to_row(jnp.sum(y * write, 1, keepdims=True), eye)
@@ -393,20 +406,20 @@
         mask, q_t, q_other, k_t, k_other, values, output_grad, start, inv, spread, rows, scale, q_scale,
     )
     got_q = swap(send_q, "head", 0)
-    shapes = [(depth, length), (length, width), wide, wide, (width, depth), (width, width)]
-    *packs, y, dk = call(
-        local_kernel, [(shape, BF16) for shape in shapes for _ in range(2)] + [tall, wide],
+    shapes = [(depth, length), (length + width, depth), (length + width, width), wide, wide, wide]
+    *packs, sym, y, dk = call(
+        local_kernel, [(shape, BF16) for shape in shapes for _ in range(2)] + [square, tall, wide],
         mask, q_t, q_other, k_t, k_other, output_grad, start_t, inv, score, damp, rows, scale, q_scale, u, score_grad, ahead,
         total,
     )
     send, keep = call(
         far_kernel, [(half, length), (half, length)],
-        mask, arrived, k_t, k_other, damp, rows, scale, *packs, dk,
+        mask, arrived, k_t, k_other, rows, scale, *packs, sym, dk,
     )
     got_k = swap(send, "head", 0)
     value_grad, rate_grad, query_grad = call(
         value_kernel, [tall, thin, (half, length)],
-        mask, arrived, packs[2], packs[3], y, base, kk, spread, scale, rows, u, keep_q, got_q,
+        mask, arrived, packs[4], packs[5], y, base, kk, spread, scale, rows, u, keep_q, got_q,
     )
     (key_grad,) = call(add_kernel, [(half, length)], keep, got_k)
     return (query_grad.T, key_grad.T, value_grad, rate_grad)

time: 21.9 us -> 21.8 us (level)
  Pallas kernels: 8.23 us -> 7.88 us
    pallas_call x9, Pallas kernels: 8.23 us -> 7.88 us  [call(): pl.pallas_call(kernel, out_shape=tuple((jax.ShapeDtypeStruct(shape, kind)...]
  transfers between devices with their start and end apart: 6 -> 6, of which waited for: 4 -> 4; matrix products, arithmetic and copies ran while one was open for 0% -> 0% of each run, Pallas kernels for 32% -> 31%
where the time goes in v5:
time: 21.8 us; the launch traced here: 21.6 us
  Pallas kernels  7.88 us (36%)
  starting transfers between devices  6.95 us (32%)
  waiting for transfers between devices  5.1 us (23%)
  local copies, waits for them, and re-layouts  0.93 us (4%)
  between operations  0.7 us (3%)
    pallas_call x9, Pallas kernels, call(): pl.pallas_call(kernel, out_shape=tuple((jax.ShapeDtypeStruct(shape, kind)...  7.88 us
    ppermute x6, starting transfers between devices, swap(): lax.ppermute(x, axis, [(i, i ^ 1 << apart) for i in range(lax.axis_size(a...  6.95 us
    ppermute x6, waiting for transfers between devices, swap(): lax.ppermute(x, axis, [(i, i ^ 1 << apart) for i in range(lax.axis_size(a...  5.1 us
    unnamed x14, local copies, waits for them, and re-layouts  0.84 us
  transfers between devices with their start and end apart: 6, of which 4 were waited for; matrix products, arithmetic and copies ran while one was open for 0% of the time, Pallas kernels for 31%

profile of v5, /device:TPU:0, one launch (start us, length us, event | category | flops | bytes accessed | tf_op | source)
XLA Modules:
  0.0 21.6 jit_solution(13181524201905188304)
XLA Ops:
  0.6 3.0 %collective-permute-start.1 = (bf16[64,256]{1,0:T(8,128)(2,1)}, bf16[64,256]{1,0:T(8,128)(2,1)S(1)}, u32[]{:S(2)}, u32[]{:S(2)}) collective-permute-start(bf16[64,256]{1,0:T(8,128)(2,1)} %bitcast.15), channel_id=1, source_target_pairs={{0,1},{1,0},{2,3},{3,2},{4,5},{5,4},{6,7},{7,6},{8,9},{9,8},{10,11... | collective-permute-start | bytes 98312 | tf_op jit(solution)/shard_map/ppermute | solution.py:348
  3.7 0.1 collective-permute-start
  3.7 0.1 stack.23
  3.8 0.6 %copy-done.6 = f32[1,256]{1,0:T(1,128)S(1)} copy-done((f32[1,256]{1,0:T(1,128)S(1)}, f32[1,256]{1,0:T(1,128)}, u32[]{:S(2)}) %copy-start.6) | copy-done | bytes 1048
  4.4 0.1 copy-done.4
  4.5 0.9 %shard_map.102 = (f32[256,256]{1,0:T(8,128)S(1)}, f32[256,256]{1,0:T(8,128)S(1)}, f32[256,256]{1,0:T(8,128)S(1)}, f32[256,256]{1,0:T(8,128)S(1)}, f32[8,256]{1,0:T(8,128)S(1)}, /*index=5*/f32[8,128]{1,0:T(8,128)S(1)}) custom-call(f32[8]{0:T(128)S(1)} %convert_element_type.3.flag_ref, bf16[64,256]{1,0:T(8,128)(2,1)S(1)} %bitcast.11, ...), custom_call_target="tpu_custom_call" | custom-call | flops 1000000000 | bytes 1048576 | tf_op jit(solution)/shard_map/pallas_call | solution.py:335
  5.4 0.4 %collective-permute-done.1.other_ref.k_other_ref = bf16[64,256]{1,0:T(8,128)(2,1)S(1)} collective-permute-done((bf16[64,256]{1,0:T(8,128)(2,1)}, bf16[64,256]{1,0:T(8,128)(2,1)S(1)}, u32[]{:S(2)}, u32[]{:S(2)}) %collective-permute-start.1) | collective-permute-done | bytes 32800 | tf_op jit(solution)/shard_map/ppermute | solution.py:348
  5.8 1.6 %shard_map.103 = (f32[256,256]{1,0:T(8,128)S(1)}, f32[128,256]{1,0:T(8,128)S(1)}, f32[256,256]{1,0:T(8,128)S(1)}, f32[2,256]{1,0:T(2,128)S(1)}) custom-call(bf16[64,256]{1,0:T(8,128)(2,1)S(1)} %bitcast.17, bf16[64,256]{1,0:T(8,128)(2,1)S(1)} %collective-permute-done.1.other_ref.k_other_ref, f32[256,256]{1,0:T(8,128)S(1)} %get-tuple-element.48.kk_in_ref, ...), custom_call_target="tpu_custom_call" | custom-call | flops 1000000000 | bytes 1048576 | tf_op jit(solution)/shard_map/pallas_call | solution.py:335
  7.4 0.4 %collective-permute-done.other_ref.q_other_ref = bf16[64,256]{1,0:T(8,128)(2,1)S(1)} collective-permute-done((bf16[64,256]{1,0:T(8,128)(2,1)}, bf16[64,256]{1,0:T(8,128)(2,1)S(1)}, u32[]{:S(2)}, u32[]{:S(2)}) %collective-permute-start) | collective-permute-done | bytes 32800 | tf_op jit(solution)/shard_map/ppermute | solution.py:348
  7.8 0.6 %shard_map.104 = (f32[256,128]{1,0:T(8,128)S(1)}, f32[256,256]{1,0:T(8,128)S(1)}, f32[1,256]{1,0:T(1,128)S(1)}, f32[256,256]{1,0:T(8,128)S(1)}) custom-call(bf16[64,256]{1,0:T(8,128)(2,1)S(1)} %bitcast.12, bf16[64,256]{1,0:T(8,128)(2,1)S(1)} %collective-permute-done.other_ref.q_other_ref, bf16[64,256]{1,0:T(8,128)(2,1)S(1)} %bitcast.18, ...), custom_call_target="tpu_custom_call" | custom-call | flops 1000000000 | bytes 1048576 | tf_op jit(solution)/shard_map/pallas_call | solution.py:335
  8.4 0.1 collective-permute-start.2
  8.5 0.1 copy-done
  8.6 0.0 copy-done.1
  8.7 1.0 %shard_map.106 = (f32[256,128]{1,0:T(8,128)S(1)}, f32[256,128]{1,0:T(8,128)S(1)}, f32[256,256]{1,0:T(8,128)S(1)}, f32[128,128]{1,0:T(8,128)S(1)}, f32[64,256]{1,0:T(8,128)S(1)}, /*index=5*/f32[64,256]{1,0:T(8,128)S(1)}) custom-call(f32[8,128]{1,0:T(8,128)S(1)} %get-tuple-element.44.mask_ref, bf16[64,256]{1,0:T(8,128)(2,1)S(1)} %bitcast.13, ...), custom_call_target="tpu_custom_call" | custom-call | flops 1000000000 | bytes 1048576 | tf_op jit(solution)/shard_map/pallas_call | solution.py:335
  9.6 1.7 %collective-permute-start.4 = (f32[64,256]{1,0:T(8,128)S(1)}, f32[64,256]{1,0:T(8,128)S(1)}, u32[]{:S(2)}, u32[]{:S(2)}) collective-permute-start(f32[64,256]{1,0:T(8,128)S(1)} %get-tuple-element.66), channel_id=1, source_target_pairs={{0,1},{1,0},{2,3},{3,2},{4,5},{5,4},{6,7},{7,6},{8,9},{9,8},{10,11... | collective-permute-start | bytes 196616 | tf_op jit(solution)/shard_map/ppermute | solution.py:348
  11.3 0.2 shard_map.105.after_ref
  11.5 1.6 %collective-permute-start.3 = (f32[128,128]{1,0:T(8,128)S(1)}, f32[128,128]{1,0:T(8,128)S(1)}, u32[]{:S(2)}, u32[]{:S(2)}) collective-permute-start(f32[128,128]{1,0:T(8,128)S(1)} %shard_map.105.after_ref), channel_id=1, source_target_pairs={{0,16},{8,24},{16,0},{24,8},{1,17},{9,25},{17,1},{25,9},{2,18},{10... | collective-permute-start | bytes 196616 | tf_op jit(solution)/shard_map/ppermute | solution.py:348
  13.1 1.2 %shard_map.107 = (bf16[128,256]{1,0:T(8,128)(2,1)S(1)}, bf16[128,256]{1,0:T(8,128)(2,1)S(1)}, bf16[384,128]{1,0:T(8,128)(2,1)S(1)}, bf16[384,128]{1,0:T(8,128)(2...) custom-call(f32[8,128]{1,0:T(8,128)S(1)} %get-tuple-element.44.mask_, ...), custom_call_target="tpu_custom_call" | custom-call | flops 1000000000 | bytes 1048576 | tf_op jit(solution)/shard_map/pallas_call | solution.py:335
  14.3 1.6 %collective-permute-done.3.got_ref = f32[128,128]{1,0:T(8,128)S(1)} collective-permute-done((f32[128,128]{1,0:T(8,128)S(1)}, f32[128,128]{1,0:T(8,128)S(1)}, u32[]{:S(2)}, u32[]{:S(2)}) %collective-permute-start.3) | collective-permute-done | bytes 65568 | tf_op jit(solution)/shard_map/ppermute | solution.py:348
  15.8 0.7 %shard_map.109 = (f32[64,256]{1,0:T(8,128)S(1)}, f32[64,256]{1,0:T(8,128)S(1)}) custom-call(f32[8,128]{1,0:T(8,128)S(1)} %get-tuple-element.44.mask_ref, f32[128,128]{1,0:T(8,128)S(1)} %collective-permute-done.3.got_ref, bf16[64,256]{1,0:T(8,128)(2,1)S(1)} %bitcast.21, bf16[64,256]{1,0:T(8,128)(2,1)S(1)} %collective-permute-done.1.other_ref.k_other_ref, ...), custom_call_target="tpu_custom_call" | custom-call | flops 1000000000 | bytes 1048576 | tf_op jit(solution)/shard_map/pallas_call | solution.py:335
  16.6 0.5 %collective-permute-start.5 = (f32[64,256]{1,0:T(8,128)S(1)}, f32[64,256]{1,0:T(8,128)S(1)}, u32[]{:S(2)}, u32[]{:S(2)}) collective-permute-start(f32[64,256]{1,0:T(8,128)S(1)} %get-tuple-element.81), channel_id=1, source_target_pairs={{0,1},{1,0},{2,3},{3,2},{4,5},{5,4},{6,7},{7,6},{8,9},{9,8},{10,11... | collective-permute-start | bytes 196616 | tf_op jit(solution)/shard_map/ppermute | solution.py:348
  17.1 1.1 %shard_map.108 = (f32[256,128]{1,0:T(8,128)}, f32[1,256]{1,0:T(1,128)}, f32[64,256]{1,0:T(8,128)}) custom-call(f32[8,128]{1,0:T(8,128)S(1)} %get-tuple-element.44.mask_ref, f32[128,128]{1,0:T(8,128)S(1)} %collective-permute-done.3.got_ref, bf16[384,128]{1,0:T(8,128)(2,1)S(1)} %get-tuple-element.60.ph_ref, bf16[384,128]{1,0:T(8,128)(2,1)S(1)} %get-tuple-element.61.pl_ref, ...), custom_call_target="tpu_custom_call" | custom-call | flops 1000000000 | bytes 1048576 | tf_op jit(solution)/shard_map/pallas_call | solution.py:335
  18.2 2.8 %collective-permute-done.5.got_ref = f32[64,256]{1,0:T(8,128)S(1)} collective-permute-done((f32[64,256]{1,0:T(8,128)S(1)}, f32[64,256]{1,0:T(8,128)S(1)}, u32[]{:S(2)}, u32[]{:S(2)}) %collective-permute-start.5) | collective-permute-done | bytes 65568 | tf_op jit(solution)/shard_map/ppermute | solution.py:348
  20.9 0.6 %shard_map.110 = f32[64,256]{1,0:T(8,128)} custom-call(f32[64,256]{1,0:T(8,128)S(1)} %get-tuple-element.80.keep_ref, f32[64,256]{1,0:T(8,128)S(1)} %collective-permute-done.5.got_ref), custom_call_target="tpu_custom_call" | custom-call | flops 1000000000 | bytes 1048576 | tf_op jit(solution)/shard_map/pallas_call | solution.py:335
  (13 shorter events, 0.0 us)
Async XLA Ops:
  0.6 5.1 %collective-permute-start.1 = (bf16[64,256]{1,0:T(8,128)(2,1)}, bf16[64,256]{1,0:T(8,128)(2,1)S(1)}, u32[]{:S(2)}, u32[]{:S(2)}) collective-permute-start(bf16[64,256]{1,0:T(8,128)(2,1)} %bitcast.15), channel_id=1, source_target_pairs={{0,1},{1,0},{2,3},{3,2},{4,5},{5,4},{6,7},{7,6},{8,9},{9,8},{10,11... | collective-permute-start | bytes 98312 | tf_op jit(solution)/shard_map/ppermute | solution.py:348
  3.7 4.1 %collective-permute-start = (bf16[64,256]{1,0:T(8,128)(2,1)}, bf16[64,256]{1,0:T(8,128)(2,1)S(1)}, u32[]{:S(2)}, u32[]{:S(2)}) collective-permute-start(bf16[64,256]{1,0:T(8,128)(2,1)} %bitcast.10), channel_id=1, source_target_pairs={{0,1},{1,0},{2,3},{3,2},{4,5},{5,4},{6,7},{7,6},{8,9},{9,8},{10,11... | collective-permute-start | bytes 98312 | tf_op jit(solution)/shard_map/ppermute | solution.py:348
  3.7 0.7 %copy-start.6 = (f32[1,256]{1,0:T(1,128)S(1)}, f32[1,256]{1,0:T(1,128)}, u32[]{:S(2)}) copy-start(f32[1,256]{1,0:T(1,128)} %rate_ref.1) | copy-start | bytes 3076
  3.7 0.8 %copy-start.4 = (bf16[256,64]{0,1:T(8,128)(2,1)S(1)}, bf16[256,64]{0,1:T(8,128)(2,1)}, u32[]{:S(2)}) copy-start(bf16[256,64]{0,1:T(8,128)(2,1)} %param.8) | copy-start | bytes 98308
  3.7 0.8 %copy-start.3 = (bf16[256,64]{0,1:T(8,128)(2,1)S(1)}, bf16[256,64]{0,1:T(8,128)(2,1)}, u32[]{:S(2)}) copy-start(bf16[256,64]{0,1:T(8,128)(2,1)} %param.7) | copy-start | bytes 98308
  3.8 0.7 %copy-start.5 = (f32[1,256]{1,0:T(1,128)S(1)}, f32[1,256]{1,0:T(1,128)}, u32[]{:S(2)}) copy-start(f32[1,256]{1,0:T(1,128)} %decay_ref.1) | copy-start | bytes 3076
  5.8 2.0 %copy-start.2 = (bf16[256,128]{1,0:T(8,128)(2,1)S(1)}, bf16[256,128]{1,0:T(8,128)(2,1)}, u32[]{:S(2)}) copy-start(bf16[256,128]{1,0:T(8,128)(2,1)} %g_ref.5) | copy-start | bytes 196612
  7.8 0.8 %copy-start = (bf16[256,128]{1,0:T(8,128)(2,1)S(1)}, bf16[256,128]{1,0:T(8,128)(2,1)}, u32[]{:S(2)}) copy-start(bf16[256,128]{1,0:T(8,128)(2,1)} %v_ref.1) | copy-start | bytes 196612
  7.8 0.9 %copy-start.1 = (f32[1,1,128,128]{3,2,1,0:T(8,128)S(1)}, f32[1,1,128,128]{3,2,1,0:T(8,128)}, u32[]{:S(2)}) copy-start(f32[1,1,128,128]{3,2,1,0:T(8,128)} %param.12) | copy-start | bytes 196612
  8.4 2.9 %collective-permute-start.2 = (f32[256,128]{1,0:T(8,128)S(1)}, f32[256,128]{1,0:T(8,128)S(1)}, u32[]{:S(2)}, u32[]{:S(2)}) collective-permute-start(f32[256,128]{1,0:T(8,128)S(1)} %get-tuple-element.53.own_ref), channel_id=1, source_target_pairs={{0,8},{8,0},{16,24},{24,16},{1,9},{9,1},{17,25},{25,17},{2,10},{10... | collective-permute-start | bytes 393224 | tf_op jit(solution)/shard_map/ppermute | solution.py:348
  9.6 7.5 %collective-permute-start.4 = (f32[64,256]{1,0:T(8,128)S(1)}, f32[64,256]{1,0:T(8,128)S(1)}, u32[]{:S(2)}, u32[]{:S(2)}) collective-permute-start(f32[64,256]{1,0:T(8,128)S(1)} %get-tuple-element.66), channel_id=1, source_target_pairs={{0,1},{1,0},{2,3},{3,2},{4,5},{5,4},{6,7},{7,6},{8,9},{9,8},{10,11... | collective-permute-start | bytes 196616 | tf_op jit(solution)/shard_map/ppermute | solution.py:348
  11.5 4.3 %collective-permute-start.3 = (f32[128,128]{1,0:T(8,128)S(1)}, f32[128,128]{1,0:T(8,128)S(1)}, u32[]{:S(2)}, u32[]{:S(2)}) collective-permute-start(f32[128,128]{1,0:T(8,128)S(1)} %shard_map.105.after_ref), channel_id=1, source_target_pairs={{0,16},{8,24},{16,0},{24,8},{1,17},{9,25},{17,1},{25,9},{2,18},{10... | collective-permute-start | bytes 196616 | tf_op jit(solution)/shard_map/ppermute | solution.py:348
  16.6 4.3 %collective-permute-start.5 = (f32[64,256]{1,0:T(8,128)S(1)}, f32[64,256]{1,0:T(8,128)S(1)}, u32[]{:S(2)}, u32[]{:S(2)}) collective-permute-start(f32[64,256]{1,0:T(8,128)S(1)} %get-tuple-element.81), channel_id=1, source_target_pairs={{0,1},{1,0},{2,3},{3,2},{4,5},{5,4},{6,7},{7,6},{8,9},{9,8},{10,11... | collective-permute-start | bytes 196616 | tf_op jit(solution)/shard_map/ppermute | solution.py:348

commit v6 on v5

v6 whole, which is shorter than its diff:
```python
import jax
import jax.numpy as jnp
from jax import lax
from jax.experimental import pallas as pl
from jax.experimental.pallas import tpu as pltpu
from jax.sharding import PartitionSpec as P

F32 = jnp.float32
BF16 = jnp.bfloat16
BASE = 32
PACK = 128
NN = (((1,), (0,)), ((), ()))
NT = (((1,), (1,)), ((), ()))


def split(x):
    high = x.astype(BF16)
    return (high, (x - high.astype(F32)).astype(BF16))


def mm(left, right, dims=NN):
    left = left if isinstance(left, tuple) else (left if left.dtype == BF16 else split(left))
    right = right if isinstance(right, tuple) else (right if right.dtype == BF16 else split(right))
    deep, out = (0, 1) if dims is NN else (1, 0)

    def one(a, b):
        return lax.dot_general(a, b, dims, preferred_element_type=F32)

    def join(parts, axis):
        return jnp.concatenate(parts, axis)

    pair_left, pair_right = isinstance(left, tuple), isinstance(right, tuple)
    shape = (right[0] if pair_right else right).shape
    shallow, thin = shape[deep] == PACK, shape[out] == PACK
    rows = (left[0] if pair_left else left).shape[0]
    if pair_left and pair_right:
        high, low = right
        if shallow and thin:
            block = join([join([high, low], out), join([high, jnp.zeros_like(low)], out)], deep)
            both = one(join(left, 1), block)
            return both[:, :PACK] + both[:, PACK:]
        if shallow:
            return one(join(left, 1), join([high, high], deep)) + one(left[0], low)
        if thin:
            both = one(join(left, 0), join(right, out))
            return both[:rows, :PACK] + (both[:rows, PACK:] + both[rows:, :PACK])
        both = one(join(left, 0), high)
        return both[:rows] + (both[rows:] + one(left[0], low))
    if pair_left:
        if shallow:
            return one(join(left, 1), join([right, right], deep))
        both = one(join(left, 0), right)
        return both[:rows] + both[rows:]
    if pair_right:
        if shallow:
            return one(join([left, left], 1), join(right, deep))
        if thin:
            both = one(left, join(right, out))
            return both[:, :PACK] + both[:, PACK:]
        return one(left, right[0]) + one(left, right[1])
    return one(left, right)


def ids(shape):
    return lax.broadcasted_iota(jnp.int32, shape, 0), lax.broadcasted_iota(jnp.int32, shape, 1)


def to_col(row, eye):
    return jnp.sum(jnp.where(eye, row, 0.0), 1, keepdims=True)


def to_row(col, eye):
    return jnp.sum(jnp.where(eye, col, 0.0), 0, keepdims=True)


def base_inverse(nil, base):
    size = nil.shape[0]
    count = size // base
    _, lane = ids((base, size))
    block = lane // base
    packed = jnp.zeros((base, size), F32)
    for b in range(count):
        packed = jnp.where(block == b, nil[b * base : (b + 1) * base, :], packed)
    row, lane = ids((8, size))
    first = lane // base * base
    tiles = range(base // 8)
    parts = [packed[8 * t : 8 * t + 8, :] for t in tiles]
    solved = [jnp.where(row + 8 * t == lane - first, 1.0, 0.0) for t in tiles]
    for j in range(base - 1):
        source = solved[j // 8][j % 8 : j % 8 + 1, :]
        for t in tiles[(j + 1) // 8 :]:
            factor = jnp.take_along_axis(parts[t], first + j, axis=1)
            if t == j // 8:
                factor = jnp.where(row + 8 * t > j, factor, 0.0)
            solved[t] = solved[t] + factor * source
    solved = jnp.concatenate(solved, 0)
    return jnp.concatenate([jnp.where(block == b, solved, 0.0) for b in range(count)], 0)


def inverses(nils):
    size = nils[0].shape[0]
    row, lane = ids((size, size))
    found = [base_inverse(nil, BASE) for nil in nils]
    width = BASE
    while width < size:
        factor = 4 if size >= 4 * width else 2
        wide = width * factor
        off = (row // wide == lane // wide) & (row // width != lane // width)
        known = [split(inv) for inv in found]
        steps = [split(mm(inv, jnp.where(off, nil, 0.0))) for inv, nil in zip(known, nils)]
        found = [inv + mm(step, pair) for inv, step, pair in zip(found, steps, known)]
        if factor == 4:
            steps = [mm(step, step) for step in steps]
            found = [inv + mm(step, inv) for inv, step in zip(found, steps)]
        width = wide
    return found


def head_terms(decay_row, rate_row, row, lane):
    cum_col = jnp.sum(jnp.where(lane <= row, decay_row, 0.0), 1, keepdims=True)
    eye = row == lane
    cum_row = to_row(cum_col, eye)
    rate_col = to_col(rate_row, eye)
    apart = cum_col - cum_row
    spread = jnp.exp(jnp.where(lane <= row, apart, -1e30))
    spread_t = jnp.exp(jnp.where(lane >= row, -apart, -1e30))
    damp = jnp.where(lane < row, spread, 0.0) * -rate_col
    tail = jnp.exp(cum_row[:, cum_row.shape[1] - 1 :] - cum_row)
    rows = jnp.concatenate([jnp.exp(cum_row), tail, rate_row, cum_row], 0)
    return spread, spread_t, damp, rows


def parts_of(x):
    high = x.astype(BF16).astype(F32)
    middle = (x - high).astype(BF16).astype(F32)
    return [high, middle, x - high - middle]


def pack_kernel(q_ref, k_ref, g_ref, decay_ref, rate_ref, out_ref):
    half, length = q_ref.shape
    mid = length // 2
    rows = parts_of(decay_ref[...]) + parts_of(rate_ref[...])
    out_ref[0:half, :] = k_ref[...]
    out_ref[half : 2 * half, :] = q_ref[...]
    out_ref[2 * half : 2 * half + mid, :] = jnp.concatenate([g_ref[0:mid, :], g_ref[mid:, :]], 1)
    out_ref[2 * half + mid :, :] = jnp.concatenate(rows + [jnp.zeros((10, length), F32)], 0).astype(BF16)


def unpack(pack_ref, half):
    length = pack_ref.shape[1]
    mid = length // 2
    grad = pack_ref[2 * half : 2 * half + mid, :]
    rows = pack_ref[2 * half + mid :, :].astype(F32)
    decay_row = rows[0:1, :] + rows[1:2, :] + rows[2:3, :]
    rate_row = rows[3:4, :] + rows[4:5, :] + rows[5:6, :]
    return jnp.concatenate([grad[:, 0:mid], grad[:, mid:]], 0), decay_row, rate_row


def prep_kernel(
    flag_ref, q_ref, k_ref, decay_ref, rate_ref, spread_ref, spread_t_ref, damp_ref, kk_ref, kq_ref, rows_ref, mask_ref,
):
    length = q_ref.shape[1]
    row, lane = ids((length, length))
    spread_ref[...], spread_t_ref[...], damp_ref[...], rows_ref[...] = head_terms(
        decay_ref[...], rate_ref[...], row, lane
    )
    k_rows = k_ref[...].astype(F32).T.astype(BF16)
    kk_ref[...] = mm(k_rows, k_ref[...])
    kq_ref[...] = mm(k_rows, q_ref[...])
    mask_ref[...] = jnp.concatenate([jnp.full((1, mask_ref.shape[1]), flag_ref[i], F32) for i in range(8)], 0)


def map_kernel(
    q_ref, k_ref, pack_ref, g_ref, kk_own_ref, kq_own_ref, damp_ref, spread_t_ref, rows_ref,
    section_ref, inv_ref, inv_b_ref, score_g_ref, score_g_b_ref, kk_ref, damp_b_ref, spread_b_ref, rows_b_ref, scale_ref,
):
    half, length = q_ref.shape
    mid = length // 2
    row, lane = ids((length, length))
    k_other, q_other = pack_ref[0:half, :], pack_ref[half : 2 * half, :]
    grad_b, decay_b, rate_b = unpack(pack_ref, half)
    k_t = jnp.concatenate([k_ref[...], k_other], 0)
    q_t = jnp.concatenate([q_ref[...], q_other], 0)
    width = 2 * half
    k_f, q_f = k_t.astype(F32), q_t.astype(F32)
    other_rows = k_other.astype(F32).T.astype(BF16)
    kk = kk_own_ref[...] + mm(other_rows, k_other)
    spread_b, spread_t_b, damp_b, rows_b = head_terms(decay_b, rate_b, row, lane)
    square = jnp.sum(k_f * k_f, 0, keepdims=True) + 1e-6
    k_scale = 1.0 / jnp.sqrt(square)
    q_scale = width ** (-0.5) / jnp.sqrt(jnp.sum(q_f * q_f, 0, keepdims=True) + 1e-6)
    scaled = kk * (k_scale * k_scale)
    nils = [damp_ref[...] * scaled, damp_b * scaled]
    rows = [rows_ref[...], rows_b]
    kq = (kq_own_ref[...] + mm(other_rows, q_other)) * q_scale
    grads = [g_ref[...], grad_b]
    score_g = [mm(spread * kq, grad) for spread, grad in zip((spread_t_ref[...], spread_t_b), grads)]
    direct = [mm(q_f * (q_scale * r[0:1, :]), grad) for r, grad in zip(rows, grads)]
    found = inverses([block for nil in nils for block in (nil[:mid, :mid], nil[mid:, mid:])])
    uppers, lowers = [split(x) for x in found[0::2]], [split(x) for x in found[1::2]]
    corners = [split(nil[mid:, :mid]) for nil in nils]
    keys = [k_f * (r[2:3, :] * r[0:1, :]) for r in rows]
    first = [mm(key[:, :mid], upper, NT) for key, upper in zip(keys, uppers)]
    below = [mm(lower, corner) for lower, corner in zip(lowers, corners)]
    second = [mm(f, corner, NT) + key[:, mid:] for f, corner, key in zip(first, corners, keys)]
    second = [mm(s, lower, NT) for s, lower in zip(second, lowers)]
    below = [mm(b, upper) for b, upper in zip(below, uppers)]
    w_t = [jnp.concatenate([f, s], 1) * (k_scale * k_scale) for f, s in zip(first, second)]
    eye = jnp.equal(*ids((width, width)))
    for i in range(2):
        ends = jnp.where(eye, rows[i][0:1, length - 1 :], 0.0)
        section_ref[2 * i * width : (2 * i + 1) * width, :] = ends - mm(w_t[i] * rows[i][1:2, :], k_t, NT)
        section_ref[(2 * i + 1) * width : (2 * i + 2) * width, :] = direct[i] - mm(w_t[i], score_g[i])
    for ref, upper, b, lower in zip((inv_ref, inv_b_ref), found[0::2], below, found[1::2]):
        ref[0:mid, :] = jnp.concatenate([upper, jnp.zeros_like(upper)], 1)
        ref[mid:, :] = jnp.concatenate([b, lower], 1)
    score_g_ref[...], score_g_b_ref[...] = score_g
    kk_ref[...] = kk
    damp_b_ref[...], spread_b_ref[...], rows_b_ref[...] = damp_b, spread_b, rows_b
    scale_ref[...] = jnp.concatenate([k_scale, square * k_scale, q_scale, q_scale], 0)


def join_kernel(mask_ref, own_ref, got_ref, total_ref):
    width = own_ref.shape[1]
    low = mask_ref[0:1, :] > 0.0
    for i in range(2):
        a, b = pl.ds(2 * i * width, width), pl.ds((2 * i + 1) * width, width)
        own, got = own_ref[b, :], got_ref[b, :]
        first = jnp.where(low, own_ref[a, :], got_ref[a, :])
        total_ref[pl.ds(i * width, width), :] = mm(first, jnp.where(low, got, own)) + jnp.where(low, own, got)


def update_kernel(
    mask_ref, k_ref, pack_ref, v_ref, v_b_ref, start_ref, start_b_ref, inv_ref, inv_b_ref, rows_ref, rows_b_ref, scale_ref,
    base_ref, u_ref, u_b_ref, psi_ref, psi_b_ref, start_t_ref, start_t_b_ref,
):
    half, length = k_ref.shape
    k_t = jnp.concatenate([k_ref[...], pack_ref[0:half, :]], 0)
    eye = jnp.equal(*ids((length, length)))
    k_scale, k_norm = scale_ref[0:1, :], scale_ref[1:2, :]
    scale_col, norm_col = to_col(k_scale, eye), to_col(k_norm, eye)
    k_rows = k_t.astype(F32).T.astype(BF16)
    rows = [rows_ref[...], rows_b_ref[...]]
    grow, tail, rate = ([to_col(r[i : i + 1, :], eye) for r in rows] for i in range(3))
    even = mask_ref[2:3, :] > 0.0
    starts = [jnp.where(even, ref[...], pltpu.roll(ref[...], half, 1)) for ref in (start_ref, start_b_ref)]
    values = [v_ref[...], v_b_ref[...]]
    invs = [inv_ref[...], inv_b_ref[...]]
    bases = [v.astype(F32) - g * scale_col * mm(k_rows, st, NT) for v, g, st in zip(values, grow, starts)]
    psis = [mm(k_t, inv * (t * scale_col * scale_col)) * k_norm for inv, t in zip(invs, tail)]
    us = [scale_col * mm(inv, norm_col * r * base) for inv, r, base in zip(invs, rate, bases)]
    start_t_ref[...], start_t_b_ref[...] = (st.T for st in starts)
    psi_ref[...], psi_b_ref[...] = psis
    base_ref[...] = bases[0]
    u_ref[...], u_b_ref[...] = us


def local_kernel(
    mask_ref, q_ref, k_ref, pack_ref, g_ref, inv_ref, inv_b_ref, score_g_ref, score_g_b_ref, kk_ref, damp_ref, damp_b_ref,
    spread_ref, spread_b_ref, rows_ref, rows_b_ref, scale_ref, base_ref, u_ref, u_b_ref, psi_ref, psi_b_ref, start_t_ref,
    start_t_b_ref, ahead_ref, after_ref,
    kh_ref, kl_ref, uth_ref, utl_ref, uh_ref, ul_ref, ph_ref, pl_ref, pth_ref, ptl_ref, gh_ref, gl_ref,
    uth_b_ref, utl_b_ref, uh_b_ref, ul_b_ref, ph_b_ref, pl_b_ref, pth_b_ref, ptl_b_ref, gh_b_ref, gl_b_ref,
    sym_ref, sym_b_ref, y_ref, write_ref, dk_ref, q_grad_ref,
):
    half, length = q_ref.shape
    k_t = jnp.concatenate([k_ref[...], pack_ref[0:half, :]], 0)
    q_f = jnp.concatenate([q_ref[...], pack_ref[half : 2 * half, :]], 0).astype(F32)
    width = 2 * half
    row, lane = ids((length, length))
    eye = row == lane
    k_scale, k_norm, q_scale = (scale_ref[i : i + 1, :] for i in range(3))
    rows = [rows_ref[...], rows_b_ref[...]]
    grow, tail, rate = ([r[i : i + 1, :] for r in rows] for i in range(3))
    low = mask_ref[0:1, :] > 0.0
    w_eye = jnp.where(jnp.equal(*ids((width, width))), 1.0, 0.0)
    maps = [split(jnp.where(low, ahead_ref[pl.ds(2 * i * width, width), :], w_eye)) for i in range(2)]
    ahead = [jnp.where(low, ahead_ref[pl.ds((2 * i + 1) * width, width), :], 0.0) for i in range(2)]
    grads = [g_ref[...], unpack(pack_ref, half)[0]]
    grads_t = [g.astype(F32).T.astype(BF16) for g in grads]
    us = [u_ref[...], u_b_ref[...]]
    us_t = [split(u.T) for u in us]
    psis_t = [psi_ref[...], psi_b_ref[...]]
    psis = [split(p.T) for p in psis_t]
    starts = [split(start_t_ref[...]), split(start_t_b_ref[...])]
    damps = [damp_ref[...], damp_b_ref[...]]
    sides = [sg.T * (k_scale * k_scale) for sg in (score_g_ref[...], score_g_b_ref[...])]
    ys_t = [mm(side, inv) * k_norm for side, inv in zip(sides, (inv_ref[...], inv_b_ref[...]))]
    score_grads = [mm(g, u) * spread for g, u, spread in zip(grads, us_t, (spread_ref[...], spread_b_ref[...]))]
    ys_t = [y + mm(a.T, p) for y, a, p in zip(ys_t, ahead, psis_t)]
    psi_far = [mm(p, m) for p, m in zip(psis, maps)]
    uz_t = [mm(a, u) for a, u in zip(ahead, us_t)]
    ys = [y.T for y in ys_t]
    inner = [d * mm(y, u) for d, y, u in zip(damps, ys, us_t)]
    score_grad = score_grads[0] + score_grads[1]
    dq = mm(k_t, score_grad * k_scale, NT)
    dq = dq + grow[0] * mm(starts[0], grads_t[0]) + grow[1] * mm(starts[1], grads_t[1])
    k_s = split(k_t.astype(F32) * k_scale)
    dk = mm(q_f * q_scale, score_grad)
    for i in range(2):
        dk = dk - mm(starts[i], ys_t[i] * (grow[i] * rate[i])) + tail[i] * uz_t[i]
    inner = inner[0] + inner[1]
    dk_ref[...] = dk + mm(k_s, inner + inner.T)
    unit = q_f * (q_scale * width**0.5)
    dq = q_scale * (dq - unit * jnp.sum(unit * dq, 0, keepdims=True))
    q_grad_ref[...] = dq[0:half, :]
    strict = jnp.where(lane < row, spread_ref[...] * kk_ref[...], 0.0) * (to_col(k_scale, eye) * k_scale)
    write_ref[...] = base_ref[...] - mm(strict, us[0])
    y_ref[...] = ys[0]
    kh_ref[...], kl_ref[...] = k_s
    outs = (
        (uth_ref, utl_ref, uh_ref, ul_ref, ph_ref, pl_ref, pth_ref, ptl_ref, gh_ref, gl_ref, sym_ref),
        (uth_b_ref, utl_b_ref, uh_b_ref, ul_b_ref, ph_b_ref, pl_b_ref, pth_b_ref, ptl_b_ref, gh_b_ref, gl_b_ref, sym_b_ref),
    )
    for i, refs in enumerate(outs):
        refs[0][...], refs[1][...] = us_t[i]
        refs[2][0:length, :], refs[3][0:length, :] = split(us[i])
        refs[2][length:, :], refs[3][length:, :] = starts[i]
        refs[4][0:length, :], refs[5][0:length, :] = split(psi_far[i])
        refs[4][length:, :], refs[5][length:, :] = maps[i]
        psi_far_t = psi_far[i].T
        refs[6][...], refs[7][...] = split(psi_far_t)
        refs[8][...], refs[9][...] = split(psi_far_t * (grow[i] * rate[i]))
        refs[10][...] = damps[i] + damps[i].T


def far_kernel(
    mask_ref, got_ref, k_ref, pack_ref, rows_ref, rows_b_ref, scale_ref,
    kh_ref, kl_ref, uth_ref, utl_ref, uh_ref, ul_ref, ph_ref, pl_ref, pth_ref, ptl_ref, gh_ref, gl_ref,
    uth_b_ref, utl_b_ref, uh_b_ref, ul_b_ref, ph_b_ref, pl_b_ref, pth_b_ref, ptl_b_ref, gh_b_ref, gl_b_ref,
    sym_ref, sym_b_ref, y_ref, write_ref, dk_ref,
    k_grad_ref, value_ref, rate_out_ref,
):
    half, length = k_ref.shape
    width = 2 * half
    row, lane = ids((length, length))
    eye = row == lane
    k_scale = scale_ref[0:1, :]
    on = mask_ref[1:2, :] > 0.0
    got = [split(jnp.where(on, got_ref[pl.ds(i * width, width), :], 0.0)) for i in range(2)]
    right_of = [(uth_ref[...], utl_ref[...]), (uth_b_ref[...], utl_b_ref[...])]
    rows_of = [(uh_ref[...], ul_ref[...]), (uh_b_ref[...], ul_b_ref[...])]
    psi_of = [(ph_ref[...], pl_ref[...]), (ph_b_ref[...], pl_b_ref[...])]
    psi_t_of = [(pth_ref[...], ptl_ref[...]), (pth_b_ref[...], ptl_b_ref[...])]
    far_of = [(gh_ref[...], gl_ref[...]), (gh_b_ref[...], gl_b_ref[...])]
    gu = [split(mm(z, u)) for z, u in zip(got, right_of)]
    right = [mm(u, z, NT) for u, z in zip(rows_of, got)]
    left = [mm(p, u) for p, u in zip(psi_of, gu)]
    upper = [mm(r[0:length, :], p) for r, p in zip(right, psi_t_of)]
    inner = sym_ref[...] * jnp.where(lane < row, left[0][0:length, :], upper[0])
    inner = inner + sym_b_ref[...] * jnp.where(lane < row, left[1][0:length, :], upper[1])
    dk = dk_ref[...]
    for i, r in enumerate((rows_ref, rows_b_ref)):
        dk = dk + r[1:2, :] * left[i][length:, :] - mm(right[i][length:, :], far_of[i])
    dk = dk + mm((kh_ref[...], kl_ref[...]), inner)
    y = y_ref[...] + mm((ph_ref[0:length, :], pl_ref[0:length, :]), got[0])
    unit = jnp.concatenate([k_ref[...], pack_ref[0:half, :]], 0).astype(F32) * k_scale
    dk = k_scale * (dk - unit * jnp.sum(unit * dk, 0, keepdims=True))
    k_grad_ref[...] = dk[0:half, :]
    value_ref[...] = to_col(rows_ref[2:3, :], eye) * y
    rate_out_ref[...] = to_row(jnp.sum(y * write_ref[...], 1, keepdims=True), eye)


def call(kernel, outs, *args, smem=(), cost=1.0):
    shapes = [out if isinstance(out[0], tuple) else (out, F32) for out in outs]
    return pl.pallas_call(
        kernel,
        out_shape=tuple(jax.ShapeDtypeStruct(shape, kind) for shape, kind in shapes),
        in_specs=[
            pl.BlockSpec(memory_space=pltpu.SMEM if i in smem else pltpu.VMEM) for i in range(len(args))
        ],
        out_specs=tuple(pl.BlockSpec(memory_space=pltpu.VMEM) for _ in outs),
        cost_estimate=pl.CostEstimate(flops=int(cost * 1e9), bytes_accessed=1 << 20, transcendentals=0),
        compiler_params=pltpu.CompilerParams(vmem_limit_bytes=24 << 20),
    )(*args)


def swap(x, axis, apart):
    return lax.ppermute(x, axis, [(i, i ^ 1 << apart) for i in range(lax.axis_size(axis))])


def far_scan(section, count, place):
    def dot(left, right):
        return jnp.dot(left, right, precision=lax.Precision.HIGHEST)

    width = section.shape[1]
    own_map, own = section[:width], section[width:]
    ahead_map, ahead = jnp.eye(width, dtype=F32), jnp.zeros_like(own)
    for bit in range(count.bit_length() - 2):
        got = swap(jnp.concatenate([own_map, own], 0), "seq", bit)
        got_map, got = got[:width], got[width:]
        low = (place >> bit) % 2 == 0
        ahead = jnp.where(low, dot(ahead_map, got) + ahead, ahead)
        ahead_map = jnp.where(low, dot(ahead_map, got_map), ahead_map)
        low_map, high_map = jnp.where(low, own_map, got_map), jnp.where(low, got_map, own_map)
        own = dot(low_map, jnp.where(low, got, own)) + jnp.where(low, own, got)
        own_map = dot(low_map, high_map)
    return own, jnp.concatenate([ahead_map, ahead], 0)


def per_device(queries, key_rows, values, log_decay, beta_rate, start_states, output_grad):
    count = lax.axis_size("seq")
    stages = count.bit_length() - 1
    assert count == 1 << stages and stages >= 2
    place = lax.axis_index("seq")
    parity = lax.axis_index("head") % 2
    q_t, k_t = queries.T, key_rows.T
    half, length = q_t.shape
    width = 2 * half
    depth = values.shape[1]
    start = start_states[0, 0]
    square, tall, wide = (length, length), (length, depth), (width, length)
    state = (width, depth)
    (pack,) = call(
        pack_kernel, [((width + length // 2 + 16, length), BF16)], q_t, k_t, output_grad, log_decay, beta_rate
    )
    pack = swap(pack, "head", 0)
    start_b = swap(start, "head", 0)
    values_b = swap(values, "head", 0)
    low_first = 1 - place % 2 if stages == 2 else place * 0 + 1
    low_last = 1 - (place >> (stages - 1)) % 2
    flags = jnp.stack([low_first, low_last, 1 - parity] + [parity] * 5).astype(F32)
    spread, spread_t, damp, kk_own, kq_own, rows, mask = call(
        prep_kernel, [square, square, square, square, square, (4, length), (8, depth)],
        flags, q_t, k_t, log_decay, beta_rate, smem=(0,),
    )
    section, inv, inv_b, score_g, score_g_b, kk, damp_b, spread_b, rows_b, scale = call(
        map_kernel,
        [(4 * width, depth), square, square, tall, tall, square, square, square, (4, length), (4, length)],
        q_t, k_t, pack, output_grad, kk_own, kq_own, damp, spread_t, rows,
    )
    if stages == 2:
        ahead = swap(section, "seq", 0)
        (total,) = call(join_kernel, [(2 * width, depth)], mask, section, ahead)
    else:
        scans = [far_scan(part, count, place) for part in (section[: 2 * width], section[2 * width :])]
        total, ahead = (jnp.concatenate(both, 0) for both in zip(*scans))
    arrived = swap(total, "seq", stages - 1)
    base, u, u_b, psi, psi_b, start_t, start_t_b = call(
        update_kernel, [tall, tall, tall, wide, wide, state, state],
        mask, k_t, pack, values, values_b, start, start_b, inv, inv_b, rows, rows_b, scale,
    )
    shapes = [(depth, length), (length + width, depth), (length + width, width), wide, wide]
    packs = [(shape, BF16) for shape in [wide] + shapes + shapes for _ in range(2)]
    *packs, query_grad = call(
        local_kernel, packs + [square, square, tall, tall, wide, (half, length)],
        mask, q_t, k_t, pack, output_grad, inv, inv_b, score_g, score_g_b, kk, damp, damp_b, spread, spread_b, rows, rows_b,
        scale, base, u, u_b, psi, psi_b, start_t, start_t_b, ahead, total,
    )
    key_grad, value_grad, rate_grad = call(
        far_kernel, [(half, length), tall, (1, length)], mask, arrived, k_t, pack, rows, rows_b, scale, *packs
    )
    return (query_grad.T, key_grad.T, value_grad, rate_grad)


def solution(mesh):
    in_specs = (
        P("seq", "head"),
        P("seq", "head"),
        P("seq", "head"),
        P("head", "seq"),
        P("head", "seq"),
        P("seq", "head", None, None),
        P("seq", "head"),
    )
    out_specs = (P("seq", "head"), P("seq", "head"), P("seq", "head"), P("head", "seq"))

    return jax.shard_map(per_device, mesh=mesh, in_specs=in_specs, out_specs=out_specs, check_vma=False)
```

time: 21.8 us -> 23.8 us (1.092)
  local copies, waits for them, and re-layouts: 0.93 us -> 3.81 us
  waiting for transfers between devices: 5.1 us -> 3.98 us
    unnamed x14 -> x20, local copies, waits for them, and re-layouts: 0.84 us -> 3.72 us
    ppermute x6 -> x5, waiting for transfers between devices: 5.1 us -> 3.98 us  [swap(): lax.ppermute(x, axis, [(i, i ^ 1 << apart) for i in range(lax.axis_size(a...]
    ppermute x6 -> x5, starting transfers between devices: 6.95 us -> 7.02 us  [swap(): lax.ppermute(x, axis, [(i, i ^ 1 << apart) for i in range(lax.axis_size(a...]
    pallas_call x9 -> x7, Pallas kernels: 7.88 us -> 7.85 us  [call(): pl.pallas_call(kernel, out_shape=tuple((jax.ShapeDtypeStruct(shape, kind)...]
  transfers between devices with their start and end apart: 6 -> 5, of which waited for: 4 -> 3; matrix products, arithmetic and copies ran while one was open for 0% -> 0% of each run, Pallas kernels for 31% -> 15%
where the time goes in v6:
time: 23.8 us; the launch traced here: 23.4 us
  Pallas kernels  7.85 us (33%)
  starting transfers between devices  7.02 us (29%)
  waiting for transfers between devices  3.98 us (17%)
  local copies, waits for them, and re-layouts  3.81 us (16%)
  between operations  0.71 us (3%)
    pallas_call x7, Pallas kernels, call(): pl.pallas_call(kernel, out_shape=tuple((jax.ShapeDtypeStruct(shape, kind)...  7.85 us
    ppermute x5, starting transfers between devices, swap(): lax.ppermute(x, axis, [(i, i ^ 1 << apart) for i in range(lax.axis_size(a...  7.02 us
    ppermute x5, waiting for transfers between devices, swap(): lax.ppermute(x, axis, [(i, i ^ 1 << apart) for i in range(lax.axis_size(a...  3.98 us
    unnamed x20, local copies, waits for them, and re-layouts  3.72 us
  transfers between devices with their start and end apart: 5, of which 3 were waited for; matrix products, arithmetic and copies ran while one was open for 0% of the time, Pallas kernels for 15%

profile of v6, /device:TPU:0, one launch (start us, length us, event | category | flops | bytes accessed | tf_op | source)
XLA Modules:
  0.0 23.4 jit_solution(10228691772326355941)
XLA Ops:
  0.7 0.7 %copy-done.9 = f32[1,256]{1,0:T(1,128)S(1)} copy-done((f32[1,256]{1,0:T(1,128)S(1)}, f32[1,256]{1,0:T(1,128)}, u32[]{:S(2)}) %copy-start.9) | copy-done | bytes 1048
  1.3 0.0 copy-done.8
  1.3 0.8 %copy-done.2 = bf16[256,128]{1,0:T(8,128)(2,1)S(1)} copy-done((bf16[256,128]{1,0:T(8,128)(2,1)S(1)}, bf16[256,128]{1,0:T(8,128)(2,1)}, u32[]{:S(2)}) %copy-start.2) | copy-done | bytes 65560
  2.2 0.8 %copy-done.4 = bf16[256,64]{0,1:T(8,128)(2,1)S(1)} copy-done((bf16[256,64]{0,1:T(8,128)(2,1)S(1)}, bf16[256,64]{0,1:T(8,128)(2,1)}, u32[]{:S(2)}) %copy-start.4) | copy-done | bytes 32792
  2.9 0.8 %copy-done.6 = bf16[256,64]{0,1:T(8,128)(2,1)S(1)} copy-done((bf16[256,64]{0,1:T(8,128)(2,1)S(1)}, bf16[256,64]{0,1:T(8,128)(2,1)}, u32[]{:S(2)}) %copy-start.6) | copy-done | bytes 32792
  3.7 3.0 %collective-permute-start = (bf16[272,256]{1,0:T(8,128)(2,1)S(1)}, bf16[272,256]{1,0:T(8,128)(2,1)S(1)}, u32[]{:S(2)}, u32[]{:S(2)}) collective-permute-start(bf16[272,256]{1,0:T(8,128)(2,1)S(1)} %shard_map.103), channel_id=1, source_target_pairs={{0,1},{1,0},{2,3},{3,2},{4,5},{5,4},{6,7},{7,6},{8,9},{9,8},{10,11... | collective-permute-start | bytes 417800 | tf_op jit(solution)/shard_map/ppermute | solution.py:379
  6.8 0.1 stack.23
  6.8 0.7 %copy-done.7 = bf16[256,64]{0,1:T(8,128)(2,1)S(1)} copy-done((bf16[256,64]{0,1:T(8,128)(2,1)S(1)}, bf16[256,64]{0,1:T(8,128)(2,1)}, u32[]{:S(2)}) %copy-start.7) | copy-done | bytes 32792
  7.5 0.0 copy-done.5
  7.5 0.8 %shard_map.102 = (f32[256,256]{1,0:T(8,128)S(1)}, f32[256,256]{1,0:T(8,128)S(1)}, f32[256,256]{1,0:T(8,128)S(1)}, f32[256,256]{1,0:T(8,128)S(1)}, f32[256,256]{1...) custom-call(f32[8]{0:T(128)S(1)} %convert_element_type.3.flag_ref, bf16[64,256]{1,0:T(8,128)(2,1)S(1)} %bitcast.12, ...), custom_call_target="tpu_custom_call" | custom-call | flops 1000000000 | bytes 1048576 | tf_op jit(solution)/shard_map/pallas_call | solution.py:366
  8.4 2.0 %collective-permute-done.pack_ref = bf16[272,256]{1,0:T(8,128)(2,1)S(1)} collective-permute-done((bf16[272,256]{1,0:T(8,128)(2,1)S(1)}, bf16[272,256]{1,0:T(8,128)(2,1)S(1)}, u32[]{:S(2)}, u32[]{:S(2)}) %collective-permute-start) | collective-permute-done | bytes 139296 | tf_op jit(solution)/shard_map/ppermute | solution.py:379
  10.4 2.5 %shard_map.104 = (f32[512,128]{1,0:T(8,128)S(1)}, f32[256,256]{1,0:T(8,128)S(1)}, f32[256,256]{1,0:T(8,128)S(1)}, f32[256,128]{1,0:T(8,128)S(1)}, f32[256,128]{1...) custom-call(bf16[64,256]{1,0:T(8,128)(2,1)S(1)} %bitcast.13, ...), custom_call_target="tpu_custom_call" | custom-call | flops 1000000000 | bytes 1048576 | tf_op jit(solution)/shard_map/pallas_call | solution.py:366
  12.9 0.1 collective-permute-start.3
  13.0 1.8 %collective-permute-start.2 = (f32[128,128]{1,0:T(8,128)S(1)}, f32[128,128]{1,0:T(8,128)S(1)}, u32[]{:S(2)}, u32[]{:S(2)}) collective-permute-start(f32[128,128]{1,0:T(8,128)S(1)} %bitcast.9), channel_id=1, source_target_pairs={{0,1},{1,0},{2,3},{3,2},{4,5},{5,4},{6,7},{7,6},{8,9},{9,8},{10,11... | collective-permute-start | bytes 196616 | tf_op jit(solution)/shard_map/ppermute | solution.py:379
  14.8 0.3 %collective-permute-start.1 = (bf16[256,128]{1,0:T(8,128)(2,1)S(1)}, bf16[256,128]{1,0:T(8,128)(2,1)S(1)}, u32[]{:S(2)}, u32[]{:S(2)}) collective-permute-start(bf16[256,128]{1,0:T(8,128)(2,1)S(1)} %copy-done), channel_id=1, source_target_pairs={{0,1},{1,0},{2,3},{3,2},{4,5},{5,4},{6,7},{7,6},{8,9},{9,8},{10,11... | collective-permute-start | bytes 196616 | tf_op jit(solution)/shard_map/ppermute | solution.py:379
  15.1 0.0 collective-permute-done.3.got_ref.ahead_ref
  15.1 0.2 shard_map.106.after_ref
  15.3 1.8 %collective-permute-start.4 = (f32[256,128]{1,0:T(8,128)S(1)}, f32[256,128]{1,0:T(8,128)S(1)}, u32[]{:S(2)}, u32[]{:S(2)}) collective-permute-start(f32[256,128]{1,0:T(8,128)S(1)} %shard_map.106.after_ref), channel_id=1, source_target_pairs={{0,16},{8,24},{16,0},{24,8},{1,17},{9,25},{17,1},{25,9},{2,18},{10... | collective-permute-start | bytes 393224 | tf_op jit(solution)/shard_map/ppermute | solution.py:379
  17.2 0.4 %collective-permute-done.2.start_b_ref = f32[128,128]{1,0:T(8,128)S(1)} collective-permute-done((f32[128,128]{1,0:T(8,128)S(1)}, f32[128,128]{1,0:T(8,128)S(1)}, u32[]{:S(2)}, u32[]{:S(2)}) %collective-permute-start.2) | collective-permute-done | bytes 65568 | tf_op jit(solution)/shard_map/ppermute | solution.py:379
  17.5 1.6 %collective-permute-done.1.v_b_ref = bf16[256,128]{1,0:T(8,128)(2,1)S(1)} collective-permute-done((bf16[256,128]{1,0:T(8,128)(2,1)S(1)}, bf16[256,128]{1,0:T(8,128)(2,1)S(1)}, u32[]{:S(2)}, u32[]{:S(2)}) %collective-permute-start.1) | collective-permute-done | bytes 65568 | tf_op jit(solution)/shard_map/ppermute | solution.py:379
  19.1 0.8 %shard_map.105 = (f32[256,128]{1,0:T(8,128)S(1)}, f32[256,128]{1,0:T(8,128)S(1)}, f32[256,128]{1,0:T(8,128)S(1)}, f32[128,256]{1,0:T(8,128)S(1)}, f32[128,256]{1...) custom-call(f32[8,128]{1,0:T(8,128)S(1)} %get-tuple-element.59.mask_ref, bf16[64,256]{1,0:T(8,128)(2,1)S(1)} %bitcast.18, ...), custom_call_target="tpu_custom_call" | custom-call | flops 1000000000 | bytes 1048576 | tf_op jit(solution)/shard_map/pallas_call | solution.py:366
  19.9 1.8 %shard_map.107 = (bf16[128,256]{1,0:T(8,128)(2,1)S(1)}, bf16[128,256]{1,0:T(8,128)(2,1)S(1)}, bf16[128,256]{1,0:T(8,128)(2,1)S(1)}, bf16[128,256]{1,0:T(8,128)(2...) custom-call(f32[8,128]{1,0:T(8,128)S(1)} %get-tuple-element.59.mask_, ...), custom_call_target="tpu_custom_call" | custom-call | flops 1000000000 | bytes 1048576 | tf_op jit(solution)/shard_map/pallas_call | solution.py:366
  21.7 0.0 collective-permute-done.4.got_ref
  21.7 1.7 %shard_map.108 = (f32[64,256]{1,0:T(8,128)}, f32[256,128]{1,0:T(8,128)}, f32[1,256]{1,0:T(1,128)}) custom-call(f32[8,128]{1,0:T(8,128)S(1)} %get-tuple-element.59.mask_ref, f32[256,128]{1,0:T(8,128)S(1)} %collective-permute-done.4.got_ref, bf16[64,256]{1,0:T(8,128)(2,1)S(1)} %bitcast.20, bf16[272,256]{1,0:T(8,128)(2,1)S(1)} %collective-permute-done.pack_ref, ...), custom_call_target="tpu_custom_call" | custom-call | flops 1000000000 | bytes 1048576 | tf_op jit(solution)/shard_map/pallas_call | solution.py:366
  (15 shorter events, 0.1 us)
Async XLA Ops:
  0.6 0.7 %copy-start.9 = (f32[1,256]{1,0:T(1,128)S(1)}, f32[1,256]{1,0:T(1,128)}, u32[]{:S(2)}) copy-start(f32[1,256]{1,0:T(1,128)} %rate_ref.3) | copy-start | bytes 3076
  0.6 0.7 %copy-start.8 = (f32[1,256]{1,0:T(1,128)S(1)}, f32[1,256]{1,0:T(1,128)}, u32[]{:S(2)}) copy-start(f32[1,256]{1,0:T(1,128)} %decay_ref.3) | copy-start | bytes 3076
  1.3 0.8 %copy-start.2 = (bf16[256,128]{1,0:T(8,128)(2,1)S(1)}, bf16[256,128]{1,0:T(8,128)(2,1)}, u32[]{:S(2)}) copy-start(bf16[256,128]{1,0:T(8,128)(2,1)} %g_ref.5) | copy-start | bytes 196612
  2.2 0.8 %copy-start.4 = (bf16[256,64]{0,1:T(8,128)(2,1)S(1)}, bf16[256,64]{0,1:T(8,128)(2,1)}, u32[]{:S(2)}) copy-start(bf16[256,64]{0,1:T(8,128)(2,1)} %param.7) | copy-start | bytes 98308
  2.9 0.8 %copy-start.6 = (bf16[256,64]{0,1:T(8,128)(2,1)S(1)}, bf16[256,64]{0,1:T(8,128)(2,1)}, u32[]{:S(2)}) copy-start(bf16[256,64]{0,1:T(8,128)(2,1)} %param.8) | copy-start | bytes 98308
  3.7 6.7 %collective-permute-start = (bf16[272,256]{1,0:T(8,128)(2,1)S(1)}, bf16[272,256]{1,0:T(8,128)(2,1)S(1)}, u32[]{:S(2)}, u32[]{:S(2)}) collective-permute-start(bf16[272,256]{1,0:T(8,128)(2,1)S(1)} %shard_map.103), channel_id=1, source_target_pairs={{0,1},{1,0},{2,3},{3,2},{4,5},{5,4},{6,7},{7,6},{8,9},{9,8},{10,11... | collective-permute-start | bytes 417800 | tf_op jit(solution)/shard_map/ppermute | solution.py:379
  6.8 0.8 %copy-start.7 = (bf16[256,64]{0,1:T(8,128)(2,1)S(1)}, bf16[256,64]{0,1:T(8,128)(2,1)}, u32[]{:S(2)}) copy-start(bf16[256,64]{0,1:T(8,128)(2,1)} %param.8) | copy-start | bytes 98308
  6.8 0.8 %copy-start.5 = (bf16[256,64]{0,1:T(8,128)(2,1)S(1)}, bf16[256,64]{0,1:T(8,128)(2,1)}, u32[]{:S(2)}) copy-start(bf16[256,64]{0,1:T(8,128)(2,1)} %param.7) | copy-start | bytes 98308
  7.5 2.9 %copy-start.3 = (bf16[256,128]{1,0:T(8,128)(2,1)S(1)}, bf16[256,128]{1,0:T(8,128)(2,1)}, u32[]{:S(2)}) copy-start(bf16[256,128]{1,0:T(8,128)(2,1)} %g_ref.5) | copy-start | bytes 196612
  10.4 2.6 %copy-start.1 = (f32[1,1,128,128]{3,2,1,0:T(8,128)S(1)}, f32[1,1,128,128]{3,2,1,0:T(8,128)}, u32[]{:S(2)}) copy-start(f32[1,1,128,128]{3,2,1,0:T(8,128)} %param.12) | copy-start | bytes 196612
  10.4 4.4 %copy-start = (bf16[256,128]{1,0:T(8,128)(2,1)S(1)}, bf16[256,128]{1,0:T(8,128)(2,1)}, u32[]{:S(2)}) copy-start(bf16[256,128]{1,0:T(8,128)(2,1)} %v_ref.1) | copy-start | bytes 196612
  12.9 2.2 %collective-permute-start.3 = (f32[512,128]{1,0:T(8,128)S(1)}, f32[512,128]{1,0:T(8,128)S(1)}, u32[]{:S(2)}, u32[]{:S(2)}) collective-permute-start(f32[512,128]{1,0:T(8,128)S(1)} %get-tuple-element.82.own_ref), channel_id=1, source_target_pairs={{0,8},{8,0},{16,24},{24,16},{1,9},{9,1},{17,25},{25,17},{2,10},{10... | collective-permute-start | bytes 786440 | tf_op jit(solution)/shard_map/ppermute | solution.py:379
  13.0 4.5 %collective-permute-start.2 = (f32[128,128]{1,0:T(8,128)S(1)}, f32[128,128]{1,0:T(8,128)S(1)}, u32[]{:S(2)}, u32[]{:S(2)}) collective-permute-start(f32[128,128]{1,0:T(8,128)S(1)} %bitcast.9), channel_id=1, source_target_pairs={{0,1},{1,0},{2,3},{3,2},{4,5},{5,4},{6,7},{7,6},{8,9},{9,8},{10,11... | collective-permute-start | bytes 196616 | tf_op jit(solution)/shard_map/ppermute | solution.py:379
  14.8 4.3 %collective-permute-start.1 = (bf16[256,128]{1,0:T(8,128)(2,1)S(1)}, bf16[256,128]{1,0:T(8,128)(2,1)S(1)}, u32[]{:S(2)}, u32[]{:S(2)}) collective-permute-start(bf16[256,128]{1,0:T(8,128)(2,1)S(1)} %copy-done), channel_id=1, source_target_pairs={{0,1},{1,0},{2,3},{3,2},{4,5},{5,4},{6,7},{7,6},{8,9},{9,8},{10,11... | collective-permute-start | bytes 196616 | tf_op jit(solution)/shard_map/ppermute | solution.py:379
  15.3 6.3 %collective-permute-start.4 = (f32[256,128]{1,0:T(8,128)S(1)}, f32[256,128]{1,0:T(8,128)S(1)}, u32[]{:S(2)}, u32[]{:S(2)}) collective-permute-start(f32[256,128]{1,0:T(8,128)S(1)} %shard_map.106.after_ref), channel_id=1, source_target_pairs={{0,16},{8,24},{16,0},{24,8},{1,17},{9,25},{17,1},{25,9},{2,18},{10... | collective-permute-start | bytes 393224 | tf_op jit(solution)/shard_map/ppermute | solution.py:379

commit v7 on v5

--- a/solution.py
+++ b/solution.py
@@ -97,23 +97,32 @@
     return jnp.concatenate([jnp.where(block == b, solved, 0.0) for b in range(count)], 0)
 
 
-def inverses(nils):
+def inverses(nils, keys, corner):
     size = nils[0].shape[0]
     row, lane = ids((size, size))
     found = [base_inverse(nil, BASE) for nil in nils]
     width = BASE
-    while width < size:
+    while True:
         factor = 4 if size >= 4 * width else 2
         wide = width * factor
         off = (row // wide == lane // wide) & (row // width != lane // width)
         known = [split(inv) for inv in found]
         steps = [split(mm(inv, jnp.where(off, nil, 0.0))) for inv, nil in zip(known, nils)]
+        if wide == size:
+            moved = [mm(key, inv, NT) for key, inv in zip(keys, known)]
+            below = mm(known[1], corner)
+            moved = [m + mm(m, step, NT) for m, step in zip(moved, steps)]
+            below = below + mm(steps[1], below)
         found = [inv + mm(step, pair) for inv, step, pair in zip(found, steps, known)]
         if factor == 4:
-            steps = [mm(step, step) for step in steps]
+            steps = [split(mm(step, step)) for step in steps]
+            if wide == size:
+                moved = [m + mm(m, step, NT) for m, step in zip(moved, steps)]
+                below = below + mm(steps[1], below)
             found = [inv + mm(step, inv) for inv, step in zip(found, steps)]
+        if wide == size:
+            return found, moved, below
         width = wide
-    return found
 
 
 def decays(decay_row, row, lane):
@@ -122,18 +131,21 @@
 
 
 def prep_kernel(
-    flag_ref, q_ref, k_ref, decay_ref, rate_ref, spread_ref, damp_ref, kk_ref, qk_ref, rows_ref, mask_ref,
+    flag_ref, q_ref, k_ref, decay_ref, rate_ref, spread_ref, spread_t_ref, damp_ref, kk_ref, kq_ref, rows_ref, mask_ref,
 ):
     length = q_ref.shape[1]
     row, lane = ids((length, length))
     cum_col, cum_row = decays(decay_ref[...], row, lane)
     rate_row = rate_ref[...]
-    spread = jnp.exp(jnp.where(lane <= row, cum_col - cum_row, -1e30))
+    apart = cum_col - cum_row
+    spread = jnp.exp(jnp.where(lane <= row, apart, -1e30))
     spread_ref[...] = spread
+    spread_t_ref[...] = jnp.exp(jnp.where(lane >= row, -apart, -1e30))
     damp_ref[...] = jnp.where(lane < row, spread, 0.0) * -to_col(rate_row, row == lane)
     k_f, q_f = k_ref[...].astype(F32), q_ref[...].astype(F32)
-    kk_ref[...] = mm(k_f.T.astype(BF16), k_ref[...])
-    qk_ref[...] = mm(q_f.T.astype(BF16), k_ref[...])
+    k_rows = k_f.T.astype(BF16)
+    kk_ref[...] = mm(k_rows, k_ref[...])
+    kq_ref[...] = mm(k_rows, q_ref[...])
     grow = jnp.exp(cum_row)
     tail = jnp.exp(cum_row[:, length - 1 :] - cum_row)
     k_sum = jnp.sum(k_f * k_f, 0, keepdims=True)
@@ -142,57 +154,53 @@
     mask_ref[...] = jnp.concatenate([jnp.full((1, mask_ref.shape[1]), flag_ref[i], F32) for i in range(8)], 0)
 
 
-def inverse_kernel(k_ref, other_ref, kk_in_ref, damp_ref, rows_ref, inv_ref, w_ref, kk_ref, scale_ref):
+def inverse_kernel(k_ref, other_ref, kk_in_ref, damp_ref, rows_ref, inv_ref, w_ref, kk_ref, scale_ref, other_rows_ref):
     other = other_ref[...]
     other_f = other.astype(F32)
+    other_rows = other_f.T.astype(BF16)
+    kk = kk_in_ref[...] + mm(other_rows, other)
     k_t = jnp.concatenate([k_ref[...], other], 0)
     mid = k_t.shape[1] // 2
     grow, rate_row, k_sum = (rows_ref[i : i + 1, :] for i in (1, 3, 4))
     square = k_sum + jnp.sum(other_f * other_f, 0, keepdims=True) + 1e-6
     k_scale = 1.0 / jnp.sqrt(square)
-    kk = kk_in_ref[...] + mm(other_f.T.astype(BF16), other)
     nil = damp_ref[...] * (kk * (k_scale * k_scale))
-    upper, lower = inverses([nil[:mid, :mid], nil[mid:, mid:]])
     keys = k_t.astype(F32) * (rate_row * grow)
-    corner = nil[mid:, :mid]
-    first = mm(keys[:, :mid], upper, NT)
-    second = mm(mm(first, corner, NT) + keys[:, mid:], lower, NT)
-    w_ref[...] = jnp.concatenate([first, second], 1) * k_scale
-    inv_ref[...] = jnp.concatenate(
-        [jnp.concatenate([upper, jnp.zeros_like(upper)], 1), jnp.concatenate([corner, lower], 1)], 0
-    )
+    (upper, lower), (first, second), below = inverses(
+        [nil[:mid, :mid], nil[mid:, mid:]], [keys[:, :mid], keys[:, mid:]], nil[mid:, :mid]
+    )
+    below = split(below)
+    second = second + mm(first, below, NT)
+    w_ref[...] = jnp.concatenate([first, second], 1) * (k_scale * k_scale)
+    inv_ref[0:mid, :] = jnp.concatenate([upper, jnp.zeros_like(upper)], 1)
+    inv_ref[mid:, :] = jnp.concatenate([mm(below, upper), lower], 1)
     kk_ref[...] = kk
     scale_ref[...] = jnp.concatenate([k_scale, square * k_scale], 0)
+    other_rows_ref[...] = other_rows
 
 
 def shift_kernel(
-    q_ref, other_ref, k_ref, k_other_ref, g_ref, qk_ref, spread_ref, rows_ref, scale_ref, w_ref, inv_in_ref,
-    map_ref, score_ref, q_scale_ref, inv_ref,
+    q_ref, other_ref, k_ref, k_other_ref, k_rows_ref, g_ref, kq_ref, spread_t_ref, rows_ref, w_ref,
+    map_ref, score_g_ref, q_scale_ref,
 ):
     other = other_ref[...]
+    kq = kq_ref[...] + mm(k_rows_ref[...], other)
     other_f = other.astype(F32)
     k_t = jnp.concatenate([k_ref[...], k_other_ref[...]], 0)
     q_f = jnp.concatenate([q_ref[...].astype(F32), other_f], 0)
     width, length = k_t.shape
-    mid = length // 2
-    k_scale, grow, tail = scale_ref[0:1, :], rows_ref[1:2, :], rows_ref[2:3, :]
-    score = spread_ref[...] * (qk_ref[...] + mm(other_f.T.astype(BF16), k_other_ref[...]))
-    lower = split(inv_in_ref[mid:, mid:])
-    corner = mm(lower, inv_in_ref[mid:, :mid])
-    w_t = w_ref[...] * k_scale
-    w_row, w_lane = ids((width, width))
-    side = mm(w_t, score, NT)
+    grow, tail = rows_ref[1:2, :], rows_ref[2:3, :]
     q_sum = rows_ref[5:6, :] + jnp.sum(other_f * other_f, 0, keepdims=True)
     q_scale = width ** (-0.5) / jnp.sqrt(q_sum + 1e-6)
-    own_map = jnp.where(w_row == w_lane, grow[:, length - 1 :], 0.0) - mm(w_t * tail, k_t, NT)
-    corner = mm(corner, inv_in_ref[:mid, :mid])
-    side = q_scale * (q_f * grow - side)
-    map_ref[width:, :] = mm(side, g_ref[...])
-    map_ref[0:width, :] = own_map
-    score_ref[...] = score
+    grad = g_ref[...]
+    score_g = mm(spread_t_ref[...] * (kq * q_scale), grad)
+    w_t = w_ref[...]
+    w_row, w_lane = ids((width, width))
+    direct = mm(q_f * (q_scale * grow), grad)
+    map_ref[0:width, :] = jnp.where(w_row == w_lane, grow[:, length - 1 :], 0.0) - mm(w_t * tail, k_t, NT)
+    map_ref[width:, :] = direct - mm(w_t, score_g)
+    score_g_ref[...] = score_g
     q_scale_ref[...] = q_scale
-    inv_ref[0:mid, :] = inv_in_ref[0:mid, :]
-    inv_ref[mid:, :] = jnp.concatenate([corner, inv_in_ref[mid:, mid:]], 1)
 
 
 def join_kernel(mask_ref, own_ref, got_ref, total_ref):
@@ -237,7 +245,7 @@
 
 
 def local_kernel(
-    mask_ref, q_ref, q_other_ref, k_ref, k_other_ref, g_ref, start_t_ref, inv_ref, score_ref, damp_ref, rows_ref, scale_ref,
+    mask_ref, q_ref, q_other_ref, k_ref, k_other_ref, start_t_ref, inv_ref, score_g_ref, damp_ref, rows_ref, scale_ref,
     q_scale_ref, u_ref, score_grad_ref, ahead_ref, after_ref,
     uth_ref, utl_ref, uh_ref, ul_ref, ph_ref, pl_ref, pth_ref, ptl_ref, gh_ref, gl_ref, kh_ref, kl_ref, sym_ref, y_ref, dk_ref,
 ):
@@ -251,14 +259,12 @@
     low = mask_ref[0:1, :] > 0.0
     ahead_map = jnp.where(low, ahead_ref[0:width, :], jnp.where(jnp.equal(*ids((width, width))), 1.0, 0.0))
     ahead = jnp.where(low, ahead_ref[width:, :], 0.0)
-    grad_t = g_ref[...].astype(F32).T.astype(BF16)
-    score = score_ref[...] * to_col(q_scale_ref[...], eye)
     u = u_ref[...]
     u_ts = split(u.T)
     inv = inv_ref[...]
     damp = damp_ref[...]
     psi_t = mm(k_t, inv * to_col(tail * k_scale * k_scale, eye)) * k_norm
-    du_t = mm(grad_t, score) * (k_scale * k_scale)
+    du_t = score_g_ref[...].T * (k_scale * k_scale)
     psi_s = split(psi_t.T)
     y_t = mm(du_t, inv) * k_norm
     sym = damp + damp.T
@@ -384,16 +390,16 @@
     low_first = 1 - place % 2 if stages == 2 else place * 0 + 1
     low_last = 1 - (place >> (stages - 1)) % 2
     flags = jnp.stack([low_first, low_last, 1 - parity] + [parity] * 5).astype(F32)
-    spread, damp, kk_own, qk_own, rows, mask = call(
-        prep_kernel, [square, square, square, square, (8, length), (8, depth)],
+    spread, spread_t, damp, kk_own, kq_own, rows, mask = call(
+        prep_kernel, [square, square, square, square, square, (8, length), (8, depth)],
         flags, q_t, k_t, log_decay, beta_rate, smem=(0,),
     )
-    halves, w_t, kk, scale = call(
-        inverse_kernel, [square, wide, square, (2, length)], k_t, k_other, kk_own, damp, rows
-    )
-    section, score, q_scale, inv = call(
-        shift_kernel, [(2 * width, depth), square, thin, square],
-        q_t, q_other, k_t, k_other, output_grad, qk_own, spread, rows, scale, w_t, halves,
+    inv, w_t, kk, scale, k_rows = call(
+        inverse_kernel, [square, wide, square, (2, length), ((length, half), BF16)], k_t, k_other, kk_own, damp, rows
+    )
+    section, score_g, q_scale = call(
+        shift_kernel, [(2 * width, depth), tall, thin],
+        q_t, q_other, k_t, k_other, k_rows, output_grad, kq_own, spread_t, rows, w_t,
     )
     if stages == 2:
         ahead = swap(section, "seq", 0)
@@ -409,7 +415,7 @@
     shapes = [(depth, length), (length + width, depth), (length + width, width), wide, wide, wide]
     *packs, sym, y, dk = call(
         local_kernel, [(shape, BF16) for shape in shapes for _ in range(2)] + [square, tall, wide],
-        mask, q_t, q_other, k_t, k_other, output_grad, start_t, inv, score, damp, rows, scale, q_scale, u, score_grad, ahead,
+        mask, q_t, q_other, k_t, k_other, start_t, inv, score_g, damp, rows, scale, q_scale, u, score_grad, ahead,
         total,
     )
     send, keep = call(

time: 21.8 us -> 21.8 us (level)
  transfers between devices with their start and end apart: 6 -> 6, of which waited for: 4 -> 4; matrix products, arithmetic and copies ran while one was open for 0% -> 0% of each run, Pallas kernels for 31% -> 30%
where the time goes in v7:
time: 21.8 us; the launch traced here: 21.6 us
  Pallas kernels  7.78 us (36%)
  starting transfers between devices  6.92 us (32%)
  waiting for transfers between devices  5.16 us (24%)
  local copies, waits for them, and re-layouts  1.01 us (5%)
  between operations  0.7 us (3%)
    pallas_call x9, Pallas kernels, call(): pl.pallas_call(kernel, out_shape=tuple((jax.ShapeDtypeStruct(shape, kind)...  7.78 us
    ppermute x6, starting transfers between devices, swap(): lax.ppermute(x, axis, [(i, i ^ 1 << apart) for i in range(lax.axis_size(a...  6.92 us
    ppermute x6, waiting for transfers between devices, swap(): lax.ppermute(x, axis, [(i, i ^ 1 << apart) for i in range(lax.axis_size(a...  5.16 us
    unnamed x14, local copies, waits for them, and re-layouts  0.92 us
  transfers between devices with their start and end apart: 6, of which 4 were waited for; matrix products, arithmetic and copies ran while one was open for 0% of the time, Pallas kernels for 30%

profile of v7, /device:TPU:0, one launch (start us, length us, event | category | flops | bytes accessed | tf_op | source)
XLA Modules:
  0.0 21.6 jit_solution(10444103195012416908)
XLA Ops:
  0.6 3.0 %collective-permute-start.1 = (bf16[64,256]{1,0:T(8,128)(2,1)}, bf16[64,256]{1,0:T(8,128)(2,1)S(1)}, u32[]{:S(2)}, u32[]{:S(2)}) collective-permute-start(bf16[64,256]{1,0:T(8,128)(2,1)} %bitcast.15), channel_id=1, source_target_pairs={{0,1},{1,0},{2,3},{3,2},{4,5},{5,4},{6,7},{7,6},{8,9},{9,8},{10,11... | collective-permute-start | bytes 98312 | tf_op jit(solution)/shard_map/ppermute | solution.py:354
  3.7 0.1 collective-permute-start
  3.7 0.1 stack.23
  3.8 0.6 %copy-done.6 = f32[1,256]{1,0:T(1,128)S(1)} copy-done((f32[1,256]{1,0:T(1,128)S(1)}, f32[1,256]{1,0:T(1,128)}, u32[]{:S(2)}) %copy-start.6) | copy-done | bytes 1048
  4.4 0.1 copy-done.4
  4.5 0.8 %shard_map.102 = (f32[256,256]{1,0:T(8,128)S(1)}, f32[256,256]{1,0:T(8,128)S(1)}, f32[256,256]{1,0:T(8,128)S(1)}, f32[256,256]{1,0:T(8,128)S(1)}, f32[256,256]{1...) custom-call(f32[8]{0:T(128)S(1)} %convert_element_type.3.flag_ref, bf16[64,256]{1,0:T(8,128)(2,1)S(1)} %bitcast.11, ...), custom_call_target="tpu_custom_call" | custom-call | flops 1000000000 | bytes 1048576 | tf_op jit(solution)/shard_map/pallas_call | solution.py:341
  5.4 0.4 %collective-permute-done.1.other_ref.k_other_ref = bf16[64,256]{1,0:T(8,128)(2,1)S(1)} collective-permute-done((bf16[64,256]{1,0:T(8,128)(2,1)}, bf16[64,256]{1,0:T(8,128)(2,1)S(1)}, u32[]{:S(2)}, u32[]{:S(2)}) %collective-permute-start.1) | collective-permute-done | bytes 32800 | tf_op jit(solution)/shard_map/ppermute | solution.py:354
  5.8 1.6 %shard_map.103 = (f32[256,256]{1,0:T(8,128)S(1)}, f32[128,256]{1,0:T(8,128)S(1)}, f32[256,256]{1,0:T(8,128)S(1)}, f32[2,256]{1,0:T(2,128)S(1)}, bf16[256,64]{1,0:T(8,128)(2,1)S(1)}) custom-call(bf16[64,256]{1,0:T(8,128)(2,1)S(1)} %bitcast.17, bf16[64,256]{1,0:T(8,128)(2,1)S(1)} %collective-permute-done.1.other_ref.k_other_ref, ...), custom_call_target="tpu_custom_call" | custom-call | flops 1000000000 | bytes 1048576 | tf_op jit(solution)/shard_map/pallas_call | solution.py:341
  7.4 0.4 %collective-permute-done.other_ref.q_other_ref = bf16[64,256]{1,0:T(8,128)(2,1)S(1)} collective-permute-done((bf16[64,256]{1,0:T(8,128)(2,1)}, bf16[64,256]{1,0:T(8,128)(2,1)S(1)}, u32[]{:S(2)}, u32[]{:S(2)}) %collective-permute-start) | collective-permute-done | bytes 32800 | tf_op jit(solution)/shard_map/ppermute | solution.py:354
  7.8 0.6 %shard_map.104 = (f32[256,128]{1,0:T(8,128)S(1)}, f32[256,128]{1,0:T(8,128)S(1)}, f32[1,256]{1,0:T(1,128)S(1)}) custom-call(bf16[64,256]{1,0:T(8,128)(2,1)S(1)} %bitcast.12, bf16[64,256]{1,0:T(8,128)(2,1)S(1)} %collective-permute-done.other_ref.q_other_ref, bf16[64,256]{1,0:T(8,128)(2,1)S(1)} %bitcast.18, ...), custom_call_target="tpu_custom_call" | custom-call | flops 1000000000 | bytes 1048576 | tf_op jit(solution)/shard_map/pallas_call | solution.py:341
  8.4 0.1 collective-permute-start.2
  8.4 0.2 copy-done.1
  8.6 0.0 copy-done.2
  8.7 1.0 %shard_map.106 = (f32[256,128]{1,0:T(8,128)S(1)}, f32[256,128]{1,0:T(8,128)S(1)}, f32[256,256]{1,0:T(8,128)S(1)}, f32[128,128]{1,0:T(8,128)S(1)}, f32[64,256]{1,0:T(8,128)S(1)}, /*index=5*/f32[64,256]{1,0:T(8,128)S(1)}) custom-call(f32[8,128]{1,0:T(8,128)S(1)} %get-tuple-element.45.mask_ref, bf16[64,256]{1,0:T(8,128)(2,1)S(1)} %bitcast.13, ...), custom_call_target="tpu_custom_call" | custom-call | flops 1000000000 | bytes 1048576 | tf_op jit(solution)/shard_map/pallas_call | solution.py:341
  9.6 1.7 %collective-permute-start.4 = (f32[64,256]{1,0:T(8,128)S(1)}, f32[64,256]{1,0:T(8,128)S(1)}, u32[]{:S(2)}, u32[]{:S(2)}) collective-permute-start(f32[64,256]{1,0:T(8,128)S(1)} %get-tuple-element.68), channel_id=1, source_target_pairs={{0,1},{1,0},{2,3},{3,2},{4,5},{5,4},{6,7},{7,6},{8,9},{9,8},{10,11... | collective-permute-start | bytes 196616 | tf_op jit(solution)/shard_map/ppermute | solution.py:354
  11.3 0.2 shard_map.105.after_ref
  11.5 1.6 %collective-permute-start.3 = (f32[128,128]{1,0:T(8,128)S(1)}, f32[128,128]{1,0:T(8,128)S(1)}, u32[]{:S(2)}, u32[]{:S(2)}) collective-permute-start(f32[128,128]{1,0:T(8,128)S(1)} %shard_map.105.after_ref), channel_id=1, source_target_pairs={{0,16},{8,24},{16,0},{24,8},{1,17},{9,25},{17,1},{25,9},{2,18},{10... | collective-permute-start | bytes 196616 | tf_op jit(solution)/shard_map/ppermute | solution.py:354
  13.1 1.2 %shard_map.107 = (bf16[128,256]{1,0:T(8,128)(2,1)S(1)}, bf16[128,256]{1,0:T(8,128)(2,1)S(1)}, bf16[384,128]{1,0:T(8,128)(2,1)S(1)}, bf16[384,128]{1,0:T(8,128)(2...) custom-call(f32[8,128]{1,0:T(8,128)S(1)} %get-tuple-element.45.mask_, ...), custom_call_target="tpu_custom_call" | custom-call | flops 1000000000 | bytes 1048576 | tf_op jit(solution)/shard_map/pallas_call | solution.py:341
  14.3 1.6 %collective-permute-done.3.got_ref = f32[128,128]{1,0:T(8,128)S(1)} collective-permute-done((f32[128,128]{1,0:T(8,128)S(1)}, f32[128,128]{1,0:T(8,128)S(1)}, u32[]{:S(2)}, u32[]{:S(2)}) %collective-permute-start.3) | collective-permute-done | bytes 65568 | tf_op jit(solution)/shard_map/ppermute | solution.py:354
  15.8 0.7 %shard_map.109 = (f32[64,256]{1,0:T(8,128)S(1)}, f32[64,256]{1,0:T(8,128)S(1)}) custom-call(f32[8,128]{1,0:T(8,128)S(1)} %get-tuple-element.45.mask_ref, f32[128,128]{1,0:T(8,128)S(1)} %collective-permute-done.3.got_ref, bf16[64,256]{1,0:T(8,128)(2,1)S(1)} %bitcast.21, bf16[64,256]{1,0:T(8,128)(2,1)S(1)} %collective-permute-done.1.other_ref.k_other_ref, ...), custom_call_target="tpu_custom_call" | custom-call | flops 1000000000 | bytes 1048576 | tf_op jit(solution)/shard_map/pallas_call | solution.py:341
  16.6 0.4 %collective-permute-start.5 = (f32[64,256]{1,0:T(8,128)S(1)}, f32[64,256]{1,0:T(8,128)S(1)}, u32[]{:S(2)}, u32[]{:S(2)}) collective-permute-start(f32[64,256]{1,0:T(8,128)S(1)} %get-tuple-element.83), channel_id=1, source_target_pairs={{0,1},{1,0},{2,3},{3,2},{4,5},{5,4},{6,7},{7,6},{8,9},{9,8},{10,11... | collective-permute-start | bytes 196616 | tf_op jit(solution)/shard_map/ppermute | solution.py:354
  17.1 1.1 %shard_map.108 = (f32[256,128]{1,0:T(8,128)}, f32[1,256]{1,0:T(1,128)}, f32[64,256]{1,0:T(8,128)}) custom-call(f32[8,128]{1,0:T(8,128)S(1)} %get-tuple-element.45.mask_ref, f32[128,128]{1,0:T(8,128)S(1)} %collective-permute-done.3.got_ref, bf16[384,128]{1,0:T(8,128)(2,1)S(1)} %get-tuple-element.62.ph_ref, bf16[384,128]{1,0:T(8,128)(2,1)S(1)} %get-tuple-element.63.pl_ref, ...), custom_call_target="tpu_custom_call" | custom-call | flops 1000000000 | bytes 1048576 | tf_op jit(solution)/shard_map/pallas_call | solution.py:341
  18.1 2.8 %collective-permute-done.5.got_ref = f32[64,256]{1,0:T(8,128)S(1)} collective-permute-done((f32[64,256]{1,0:T(8,128)S(1)}, f32[64,256]{1,0:T(8,128)S(1)}, u32[]{:S(2)}, u32[]{:S(2)}) %collective-permute-start.5) | collective-permute-done | bytes 65568 | tf_op jit(solution)/shard_map/ppermute | solution.py:354
  20.9 0.6 %shard_map.110 = f32[64,256]{1,0:T(8,128)} custom-call(f32[64,256]{1,0:T(8,128)S(1)} %get-tuple-element.82.keep_ref, f32[64,256]{1,0:T(8,128)S(1)} %collective-permute-done.5.got_ref), custom_call_target="tpu_custom_call" | custom-call | flops 1000000000 | bytes 1048576 | tf_op jit(solution)/shard_map/pallas_call | solution.py:341
  (13 shorter events, 0.0 us)
Async XLA Ops:
  0.6 5.1 %collective-permute-start.1 = (bf16[64,256]{1,0:T(8,128)(2,1)}, bf16[64,256]{1,0:T(8,128)(2,1)S(1)}, u32[]{:S(2)}, u32[]{:S(2)}) collective-permute-start(bf16[64,256]{1,0:T(8,128)(2,1)} %bitcast.15), channel_id=1, source_target_pairs={{0,1},{1,0},{2,3},{3,2},{4,5},{5,4},{6,7},{7,6},{8,9},{9,8},{10,11... | collective-permute-start | bytes 98312 | tf_op jit(solution)/shard_map/ppermute | solution.py:354
  3.7 4.1 %collective-permute-start = (bf16[64,256]{1,0:T(8,128)(2,1)}, bf16[64,256]{1,0:T(8,128)(2,1)S(1)}, u32[]{:S(2)}, u32[]{:S(2)}) collective-permute-start(bf16[64,256]{1,0:T(8,128)(2,1)} %bitcast.10), channel_id=1, source_target_pairs={{0,1},{1,0},{2,3},{3,2},{4,5},{5,4},{6,7},{7,6},{8,9},{9,8},{10,11... | collective-permute-start | bytes 98312 | tf_op jit(solution)/shard_map/ppermute | solution.py:354
  3.7 0.7 %copy-start.6 = (f32[1,256]{1,0:T(1,128)S(1)}, f32[1,256]{1,0:T(1,128)}, u32[]{:S(2)}) copy-start(f32[1,256]{1,0:T(1,128)} %rate_ref.1) | copy-start | bytes 3076
  3.7 0.8 %copy-start.4 = (bf16[256,64]{0,1:T(8,128)(2,1)S(1)}, bf16[256,64]{0,1:T(8,128)(2,1)}, u32[]{:S(2)}) copy-start(bf16[256,64]{0,1:T(8,128)(2,1)} %param.8) | copy-start | bytes 98308
  3.7 0.8 %copy-start.3 = (bf16[256,64]{0,1:T(8,128)(2,1)S(1)}, bf16[256,64]{0,1:T(8,128)(2,1)}, u32[]{:S(2)}) copy-start(bf16[256,64]{0,1:T(8,128)(2,1)} %param.7) | copy-start | bytes 98308
  3.8 0.7 %copy-start.5 = (f32[1,256]{1,0:T(1,128)S(1)}, f32[1,256]{1,0:T(1,128)}, u32[]{:S(2)}) copy-start(f32[1,256]{1,0:T(1,128)} %decay_ref.1) | copy-start | bytes 3076
  5.8 2.0 %copy-start = (bf16[256,128]{1,0:T(8,128)(2,1)S(1)}, bf16[256,128]{1,0:T(8,128)(2,1)}, u32[]{:S(2)}) copy-start(bf16[256,128]{1,0:T(8,128)(2,1)} %g_ref.3) | copy-start | bytes 196612
  7.8 0.8 %copy-start.1 = (bf16[256,128]{1,0:T(8,128)(2,1)S(1)}, bf16[256,128]{1,0:T(8,128)(2,1)}, u32[]{:S(2)}) copy-start(bf16[256,128]{1,0:T(8,128)(2,1)} %v_ref.1) | copy-start | bytes 196612
  7.8 0.9 %copy-start.2 = (f32[1,1,128,128]{3,2,1,0:T(8,128)S(1)}, f32[1,1,128,128]{3,2,1,0:T(8,128)}, u32[]{:S(2)}) copy-start(f32[1,1,128,128]{3,2,1,0:T(8,128)} %param.12) | copy-start | bytes 196612
  8.4 3.0 %collective-permute-start.2 = (f32[256,128]{1,0:T(8,128)S(1)}, f32[256,128]{1,0:T(8,128)S(1)}, u32[]{:S(2)}, u32[]{:S(2)}) collective-permute-start(f32[256,128]{1,0:T(8,128)S(1)} %get-tuple-element.53.own_ref), channel_id=1, source_target_pairs={{0,8},{8,0},{16,24},{24,16},{1,9},{9,1},{17,25},{25,17},{2,10},{10... | collective-permute-start | bytes 393224 | tf_op jit(solution)/shard_map/ppermute | solution.py:354
  9.6 7.4 %collective-permute-start.4 = (f32[64,256]{1,0:T(8,128)S(1)}, f32[64,256]{1,0:T(8,128)S(1)}, u32[]{:S(2)}, u32[]{:S(2)}) collective-permute-start(f32[64,256]{1,0:T(8,128)S(1)} %get-tuple-element.68), channel_id=1, source_target_pairs={{0,1},{1,0},{2,3},{3,2},{4,5},{5,4},{6,7},{7,6},{8,9},{9,8},{10,11... | collective-permute-start | bytes 196616 | tf_op jit(solution)/shard_map/ppermute | solution.py:354
  11.5 4.3 %collective-permute-start.3 = (f32[128,128]{1,0:T(8,128)S(1)}, f32[128,128]{1,0:T(8,128)S(1)}, u32[]{:S(2)}, u32[]{:S(2)}) collective-permute-start(f32[128,128]{1,0:T(8,128)S(1)} %shard_map.105.after_ref), channel_id=1, source_target_pairs={{0,16},{8,24},{16,0},{24,8},{1,17},{9,25},{17,1},{25,9},{2,18},{10... | collective-permute-start | bytes 196616 | tf_op jit(solution)/shard_map/ppermute | solution.py:354
  16.6 4.3 %collective-permute-start.5 = (f32[64,256]{1,0:T(8,128)S(1)}, f32[64,256]{1,0:T(8,128)S(1)}, u32[]{:S(2)}, u32[]{:S(2)}) collective-permute-start(f32[64,256]{1,0:T(8,128)S(1)} %get-tuple-element.83), channel_id=1, source_target_pairs={{0,1},{1,0},{2,3},{3,2},{4,5},{5,4},{6,7},{7,6},{8,9},{9,8},{10,11... | collective-permute-start | bytes 196616 | tf_op jit(solution)/shard_map/ppermute | solution.py:354

commit v8 on v7

--- a/solution.py
+++ b/solution.py
@@ -73,34 +73,38 @@
     return jnp.sum(jnp.where(eye, col, 0.0), 0, keepdims=True)
 
 
-def base_inverse(nil, base):
-    size = nil.shape[0]
+def base_inverses(nils, base):
+    size = nils[0].shape[0]
     count = size // base
     _, lane = ids((base, size))
     block = lane // base
-    packed = jnp.zeros((base, size), F32)
-    for b in range(count):
-        packed = jnp.where(block == b, nil[b * base : (b + 1) * base, :], packed)
     row, lane = ids((8, size))
     first = lane // base * base
     tiles = range(base // 8)
-    parts = [packed[8 * t : 8 * t + 8, :] for t in tiles]
-    solved = [jnp.where(row + 8 * t == lane - first, 1.0, 0.0) for t in tiles]
+    parts, solved = [], []
+    for nil in nils:
+        packed = jnp.where(block == 0, nil[0:base, :], 0.0)
+        for b in range(1, count):
+            packed = jnp.where(block == b, nil[b * base : (b + 1) * base, :], packed)
+        parts.append([packed[8 * t : 8 * t + 8, :] for t in tiles])
+        solved.append([jnp.where(row + 8 * t == lane - first, 1.0, 0.0) for t in tiles])
     for j in range(base - 1):
-        source = solved[j // 8][j % 8 : j % 8 + 1, :]
-        for t in tiles[(j + 1) // 8 :]:
-            factor = jnp.take_along_axis(parts[t], first + j, axis=1)
-            if t == j // 8:
-                factor = jnp.where(row + 8 * t > j, factor, 0.0)
-            solved[t] = solved[t] + factor * source
-    solved = jnp.concatenate(solved, 0)
-    return jnp.concatenate([jnp.where(block == b, solved, 0.0) for b in range(count)], 0)
+        at = first + j
+        for part, done in zip(parts, solved):
+            source = done[j // 8][j % 8 : j % 8 + 1, :]
+            for t in tiles[(j + 1) // 8 :]:
+                factor = jnp.take_along_axis(part[t], at, axis=1)
+                if t == j // 8:
+                    factor = jnp.where(row + 8 * t > j, factor, 0.0)
+                done[t] = done[t] + factor * source
+    solved = [jnp.concatenate(done, 0) for done in solved]
+    return [jnp.concatenate([jnp.where(block == b, done, 0.0) for b in range(count)], 0) for done in solved]
 
 
 def inverses(nils, keys, corner):
     size = nils[0].shape[0]
     row, lane = ids((size, size))
-    found = [base_inverse(nil, BASE) for nil in nils]
+    found = base_inverses(nils, BASE)
     width = BASE
     while True:
         factor = 4 if size >= 4 * width else 2
@@ -108,19 +112,24 @@
         off = (row // wide == lane // wide) & (row // width != lane // width)
         known = [split(inv) for inv in found]
         steps = [split(mm(inv, jnp.where(off, nil, 0.0))) for inv, nil in zip(known, nils)]
-        if wide == size:
+        last = wide == size
+        if last:
             moved = [mm(key, inv, NT) for key, inv in zip(keys, known)]
             below = mm(known[1], corner)
+        twice = [split(mm(step, step)) for step in steps] if factor == 4 else []
+        if last:
+            below = below + mm(steps[1], below)
             moved = [m + mm(m, step, NT) for m, step in zip(moved, steps)]
-            below = below + mm(steps[1], below)
         found = [inv + mm(step, pair) for inv, step, pair in zip(found, steps, known)]
-        if factor == 4:
-            steps = [split(mm(step, step)) for step in steps]
-            if wide == size:
-                moved = [m + mm(m, step, NT) for m, step in zip(moved, steps)]
-                below = below + mm(steps[1], below)
-            found = [inv + mm(step, inv) for inv, step in zip(found, steps)]
-        if wide == size:
+        if last and twice:
+            below = below + mm(twice[1], below)
+            moved = [m + mm(m, step, NT) for m, step in zip(moved, twice)]
+        if last:
+            below = split(below)
+            moved[1] = moved[1] + mm(moved[0], below, NT)
+        if twice:
+            found = [inv + mm(step, inv) for inv, step in zip(found, twice)]
+        if last:
             return found, moved, below
         width = wide
 
@@ -158,23 +167,26 @@
     other = other_ref[...]
     other_f = other.astype(F32)
     other_rows = other_f.T.astype(BF16)
-    kk = kk_in_ref[...] + mm(other_rows, other)
     k_t = jnp.concatenate([k_ref[...], other], 0)
     mid = k_t.shape[1] // 2
     grow, rate_row, k_sum = (rows_ref[i : i + 1, :] for i in (1, 3, 4))
     square = k_sum + jnp.sum(other_f * other_f, 0, keepdims=True) + 1e-6
     k_scale = 1.0 / jnp.sqrt(square)
-    nil = damp_ref[...] * (kk * (k_scale * k_scale))
+    both = k_scale * k_scale
+    upper = kk_in_ref[0:mid, 0:mid] + mm(other_rows[0:mid, :], other[:, 0:mid])
+    lower = kk_in_ref[mid:, :] + mm(other_rows[mid:, :], other)
+    kk_ref[0:mid, 0:mid] = upper
+    kk_ref[0:mid, mid:] = jnp.zeros_like(upper)
+    kk_ref[mid:, :] = lower
+    upper = damp_ref[0:mid, 0:mid] * (upper * both[:, 0:mid])
+    lower = damp_ref[mid:, :] * (lower * both)
     keys = k_t.astype(F32) * (rate_row * grow)
-    (upper, lower), (first, second), below = inverses(
-        [nil[:mid, :mid], nil[mid:, mid:]], [keys[:, :mid], keys[:, mid:]], nil[mid:, :mid]
-    )
-    below = split(below)
-    second = second + mm(first, below, NT)
-    w_ref[...] = jnp.concatenate([first, second], 1) * (k_scale * k_scale)
+    (upper, lower), moved, below = inverses(
+        [upper, lower[:, mid:]], [keys[:, :mid], keys[:, mid:]], lower[:, :mid]
+    )
+    w_ref[...] = jnp.concatenate(moved, 1) * both
     inv_ref[0:mid, :] = jnp.concatenate([upper, jnp.zeros_like(upper)], 1)
     inv_ref[mid:, :] = jnp.concatenate([mm(below, upper), lower], 1)
-    kk_ref[...] = kk
     scale_ref[...] = jnp.concatenate([k_scale, square * k_scale], 0)
     other_rows_ref[...] = other_rows
 

time: 21.8 us -> 21.8 us (level)
  no operation moved by 1% of the time
where the time goes in v8:
time: 21.8 us; the launch traced here: 21.6 us
  Pallas kernels  7.76 us (36%)
  starting transfers between devices  6.92 us (32%)
  waiting for transfers between devices  5.16 us (24%)
  local copies, waits for them, and re-layouts  1.01 us (5%)
  between operations  0.7 us (3%)
    pallas_call x9, Pallas kernels, call(): pl.pallas_call(kernel, out_shape=tuple((jax.ShapeDtypeStruct(shape, kind)...  7.76 us
    ppermute x6, starting transfers between devices, swap(): lax.ppermute(x, axis, [(i, i ^ 1 << apart) for i in range(lax.axis_size(a...  6.92 us
    ppermute x6, waiting for transfers between devices, swap(): lax.ppermute(x, axis, [(i, i ^ 1 << apart) for i in range(lax.axis_size(a...  5.16 us
    unnamed x14, local copies, waits for them, and re-layouts  0.92 us
  transfers between devices with their start and end apart: 6, of which 4 were waited for; matrix products, arithmetic and copies ran while one was open for 0% of the time, Pallas kernels for 30%

profile of v8, /device:TPU:0, one launch (start us, length us, event | category | flops | bytes accessed | tf_op | source)
XLA Modules:
  0.0 21.6 jit_solution(7975991202751074946)
XLA Ops:
  0.6 3.0 %collective-permute-start.1 = (bf16[64,256]{1,0:T(8,128)(2,1)}, bf16[64,256]{1,0:T(8,128)(2,1)S(1)}, u32[]{:S(2)}, u32[]{:S(2)}) collective-permute-start(bf16[64,256]{1,0:T(8,128)(2,1)} %bitcast.15), channel_id=1, source_target_pairs={{0,1},{1,0},{2,3},{3,2},{4,5},{5,4},{6,7},{7,6},{8,9},{9,8},{10,11... | collective-permute-start | bytes 98312 | tf_op jit(solution)/shard_map/ppermute | solution.py:366
  3.7 0.1 collective-permute-start
  3.7 0.1 stack.23
  3.8 0.6 %copy-done.6 = f32[1,256]{1,0:T(1,128)S(1)} copy-done((f32[1,256]{1,0:T(1,128)S(1)}, f32[1,256]{1,0:T(1,128)}, u32[]{:S(2)}) %copy-start.6) | copy-done | bytes 1048
  4.4 0.1 copy-done.4
  4.5 0.8 %shard_map.102 = (f32[256,256]{1,0:T(8,128)S(1)}, f32[256,256]{1,0:T(8,128)S(1)}, f32[256,256]{1,0:T(8,128)S(1)}, f32[256,256]{1,0:T(8,128)S(1)}, f32[256,256]{1...) custom-call(f32[8]{0:T(128)S(1)} %convert_element_type.3.flag_ref, bf16[64,256]{1,0:T(8,128)(2,1)S(1)} %bitcast.11, ...), custom_call_target="tpu_custom_call" | custom-call | flops 1000000000 | bytes 1048576 | tf_op jit(solution)/shard_map/pallas_call | solution.py:353
  5.4 0.4 %collective-permute-done.1.other_ref.k_other_ref = bf16[64,256]{1,0:T(8,128)(2,1)S(1)} collective-permute-done((bf16[64,256]{1,0:T(8,128)(2,1)}, bf16[64,256]{1,0:T(8,128)(2,1)S(1)}, u32[]{:S(2)}, u32[]{:S(2)}) %collective-permute-start.1) | collective-permute-done | bytes 32800 | tf_op jit(solution)/shard_map/ppermute | solution.py:366
  5.8 1.6 %shard_map.103 = (f32[256,256]{1,0:T(8,128)S(1)}, f32[128,256]{1,0:T(8,128)S(1)}, f32[256,256]{1,0:T(8,128)S(1)}, f32[2,256]{1,0:T(2,128)S(1)}, bf16[256,64]{1,0:T(8,128)(2,1)S(1)}) custom-call(bf16[64,256]{1,0:T(8,128)(2,1)S(1)} %bitcast.17, bf16[64,256]{1,0:T(8,128)(2,1)S(1)} %collective-permute-done.1.other_ref.k_other_ref, ...), custom_call_target="tpu_custom_call" | custom-call | flops 1000000000 | bytes 1048576 | tf_op jit(solution)/shard_map/pallas_call | solution.py:353
  7.4 0.4 %collective-permute-done.other_ref.q_other_ref = bf16[64,256]{1,0:T(8,128)(2,1)S(1)} collective-permute-done((bf16[64,256]{1,0:T(8,128)(2,1)}, bf16[64,256]{1,0:T(8,128)(2,1)S(1)}, u32[]{:S(2)}, u32[]{:S(2)}) %collective-permute-start) | collective-permute-done | bytes 32800 | tf_op jit(solution)/shard_map/ppermute | solution.py:366
  7.8 0.6 %shard_map.104 = (f32[256,128]{1,0:T(8,128)S(1)}, f32[256,128]{1,0:T(8,128)S(1)}, f32[1,256]{1,0:T(1,128)S(1)}) custom-call(bf16[64,256]{1,0:T(8,128)(2,1)S(1)} %bitcast.12, bf16[64,256]{1,0:T(8,128)(2,1)S(1)} %collective-permute-done.other_ref.q_other_ref, bf16[64,256]{1,0:T(8,128)(2,1)S(1)} %bitcast.18, ...), custom_call_target="tpu_custom_call" | custom-call | flops 1000000000 | bytes 1048576 | tf_op jit(solution)/shard_map/pallas_call | solution.py:353
  8.4 0.1 collective-permute-start.2
  8.4 0.2 copy-done.1
  8.6 0.0 copy-done.2
  8.7 1.0 %shard_map.106 = (f32[256,128]{1,0:T(8,128)S(1)}, f32[256,128]{1,0:T(8,128)S(1)}, f32[256,256]{1,0:T(8,128)S(1)}, f32[128,128]{1,0:T(8,128)S(1)}, f32[64,256]{1,0:T(8,128)S(1)}, /*index=5*/f32[64,256]{1,0:T(8,128)S(1)}) custom-call(f32[8,128]{1,0:T(8,128)S(1)} %get-tuple-element.45.mask_ref, bf16[64,256]{1,0:T(8,128)(2,1)S(1)} %bitcast.13, ...), custom_call_target="tpu_custom_call" | custom-call | flops 1000000000 | bytes 1048576 | tf_op jit(solution)/shard_map/pallas_call | solution.py:353
  9.6 1.7 %collective-permute-start.4 = (f32[64,256]{1,0:T(8,128)S(1)}, f32[64,256]{1,0:T(8,128)S(1)}, u32[]{:S(2)}, u32[]{:S(2)}) collective-permute-start(f32[64,256]{1,0:T(8,128)S(1)} %get-tuple-element.68), channel_id=1, source_target_pairs={{0,1},{1,0},{2,3},{3,2},{4,5},{5,4},{6,7},{7,6},{8,9},{9,8},{10,11... | collective-permute-start | bytes 196616 | tf_op jit(solution)/shard_map/ppermute | solution.py:366
  11.3 0.2 shard_map.105.after_ref
  11.5 1.6 %collective-permute-start.3 = (f32[128,128]{1,0:T(8,128)S(1)}, f32[128,128]{1,0:T(8,128)S(1)}, u32[]{:S(2)}, u32[]{:S(2)}) collective-permute-start(f32[128,128]{1,0:T(8,128)S(1)} %shard_map.105.after_ref), channel_id=1, source_target_pairs={{0,16},{8,24},{16,0},{24,8},{1,17},{9,25},{17,1},{25,9},{2,18},{10... | collective-permute-start | bytes 196616 | tf_op jit(solution)/shard_map/ppermute | solution.py:366
  13.1 1.2 %shard_map.107 = (bf16[128,256]{1,0:T(8,128)(2,1)S(1)}, bf16[128,256]{1,0:T(8,128)(2,1)S(1)}, bf16[384,128]{1,0:T(8,128)(2,1)S(1)}, bf16[384,128]{1,0:T(8,128)(2...) custom-call(f32[8,128]{1,0:T(8,128)S(1)} %get-tuple-element.45.mask_, ...), custom_call_target="tpu_custom_call" | custom-call | flops 1000000000 | bytes 1048576 | tf_op jit(solution)/shard_map/pallas_call | solution.py:353
  14.3 1.6 %collective-permute-done.3.got_ref = f32[128,128]{1,0:T(8,128)S(1)} collective-permute-done((f32[128,128]{1,0:T(8,128)S(1)}, f32[128,128]{1,0:T(8,128)S(1)}, u32[]{:S(2)}, u32[]{:S(2)}) %collective-permute-start.3) | collective-permute-done | bytes 65568 | tf_op jit(solution)/shard_map/ppermute | solution.py:366
  15.8 0.7 %shard_map.109 = (f32[64,256]{1,0:T(8,128)S(1)}, f32[64,256]{1,0:T(8,128)S(1)}) custom-call(f32[8,128]{1,0:T(8,128)S(1)} %get-tuple-element.45.mask_ref, f32[128,128]{1,0:T(8,128)S(1)} %collective-permute-done.3.got_ref, bf16[64,256]{1,0:T(8,128)(2,1)S(1)} %bitcast.21, bf16[64,256]{1,0:T(8,128)(2,1)S(1)} %collective-permute-done.1.other_ref.k_other_ref, ...), custom_call_target="tpu_custom_call" | custom-call | flops 1000000000 | bytes 1048576 | tf_op jit(solution)/shard_map/pallas_call | solution.py:353
  16.6 0.5 %collective-permute-start.5 = (f32[64,256]{1,0:T(8,128)S(1)}, f32[64,256]{1,0:T(8,128)S(1)}, u32[]{:S(2)}, u32[]{:S(2)}) collective-permute-start(f32[64,256]{1,0:T(8,128)S(1)} %get-tuple-element.83), channel_id=1, source_target_pairs={{0,1},{1,0},{2,3},{3,2},{4,5},{5,4},{6,7},{7,6},{8,9},{9,8},{10,11... | collective-permute-start | bytes 196616 | tf_op jit(solution)/shard_map/ppermute | solution.py:366
  17.1 1.1 %shard_map.108 = (f32[256,128]{1,0:T(8,128)}, f32[1,256]{1,0:T(1,128)}, f32[64,256]{1,0:T(8,128)}) custom-call(f32[8,128]{1,0:T(8,128)S(1)} %get-tuple-element.45.mask_ref, f32[128,128]{1,0:T(8,128)S(1)} %collective-permute-done.3.got_ref, bf16[384,128]{1,0:T(8,128)(2,1)S(1)} %get-tuple-element.62.ph_ref, bf16[384,128]{1,0:T(8,128)(2,1)S(1)} %get-tuple-element.63.pl_ref, ...), custom_call_target="tpu_custom_call" | custom-call | flops 1000000000 | bytes 1048576 | tf_op jit(solution)/shard_map/pallas_call | solution.py:353
  18.1 2.8 %collective-permute-done.5.got_ref = f32[64,256]{1,0:T(8,128)S(1)} collective-permute-done((f32[64,256]{1,0:T(8,128)S(1)}, f32[64,256]{1,0:T(8,128)S(1)}, u32[]{:S(2)}, u32[]{:S(2)}) %collective-permute-start.5) | collective-permute-done | bytes 65568 | tf_op jit(solution)/shard_map/ppermute | solution.py:366
  20.9 0.6 %shard_map.110 = f32[64,256]{1,0:T(8,128)} custom-call(f32[64,256]{1,0:T(8,128)S(1)} %get-tuple-element.82.keep_ref, f32[64,256]{1,0:T(8,128)S(1)} %collective-permute-done.5.got_ref), custom_call_target="tpu_custom_call" | custom-call | flops 1000000000 | bytes 1048576 | tf_op jit(solution)/shard_map/pallas_call | solution.py:353
  (13 shorter events, 0.0 us)
Async XLA Ops:
  0.6 5.1 %collective-permute-start.1 = (bf16[64,256]{1,0:T(8,128)(2,1)}, bf16[64,256]{1,0:T(8,128)(2,1)S(1)}, u32[]{:S(2)}, u32[]{:S(2)}) collective-permute-start(bf16[64,256]{1,0:T(8,128)(2,1)} %bitcast.15), channel_id=1, source_target_pairs={{0,1},{1,0},{2,3},{3,2},{4,5},{5,4},{6,7},{7,6},{8,9},{9,8},{10,11... | collective-permute-start | bytes 98312 | tf_op jit(solution)/shard_map/ppermute | solution.py:366
  3.7 4.1 %collective-permute-start = (bf16[64,256]{1,0:T(8,128)(2,1)}, bf16[64,256]{1,0:T(8,128)(2,1)S(1)}, u32[]{:S(2)}, u32[]{:S(2)}) collective-permute-start(bf16[64,256]{1,0:T(8,128)(2,1)} %bitcast.10), channel_id=1, source_target_pairs={{0,1},{1,0},{2,3},{3,2},{4,5},{5,4},{6,7},{7,6},{8,9},{9,8},{10,11... | collective-permute-start | bytes 98312 | tf_op jit(solution)/shard_map/ppermute | solution.py:366
  3.7 0.7 %copy-start.6 = (f32[1,256]{1,0:T(1,128)S(1)}, f32[1,256]{1,0:T(1,128)}, u32[]{:S(2)}) copy-start(f32[1,256]{1,0:T(1,128)} %rate_ref.1) | copy-start | bytes 3076
  3.7 0.8 %copy-start.4 = (bf16[256,64]{0,1:T(8,128)(2,1)S(1)}, bf16[256,64]{0,1:T(8,128)(2,1)}, u32[]{:S(2)}) copy-start(bf16[256,64]{0,1:T(8,128)(2,1)} %param.8) | copy-start | bytes 98308
  3.7 0.8 %copy-start.3 = (bf16[256,64]{0,1:T(8,128)(2,1)S(1)}, bf16[256,64]{0,1:T(8,128)(2,1)}, u32[]{:S(2)}) copy-start(bf16[256,64]{0,1:T(8,128)(2,1)} %param.7) | copy-start | bytes 98308
  3.8 0.7 %copy-start.5 = (f32[1,256]{1,0:T(1,128)S(1)}, f32[1,256]{1,0:T(1,128)}, u32[]{:S(2)}) copy-start(f32[1,256]{1,0:T(1,128)} %decay_ref.1) | copy-start | bytes 3076
  5.8 2.0 %copy-start = (bf16[256,128]{1,0:T(8,128)(2,1)S(1)}, bf16[256,128]{1,0:T(8,128)(2,1)}, u32[]{:S(2)}) copy-start(bf16[256,128]{1,0:T(8,128)(2,1)} %g_ref.3) | copy-start | bytes 196612
  7.8 0.8 %copy-start.1 = (bf16[256,128]{1,0:T(8,128)(2,1)S(1)}, bf16[256,128]{1,0:T(8,128)(2,1)}, u32[]{:S(2)}) copy-start(bf16[256,128]{1,0:T(8,128)(2,1)} %v_ref.1) | copy-start | bytes 196612
  7.8 0.9 %copy-start.2 = (f32[1,1,128,128]{3,2,1,0:T(8,128)S(1)}, f32[1,1,128,128]{3,2,1,0:T(8,128)}, u32[]{:S(2)}) copy-start(f32[1,1,128,128]{3,2,1,0:T(8,128)} %param.12) | copy-start | bytes 196612
  8.4 3.0 %collective-permute-start.2 = (f32[256,128]{1,0:T(8,128)S(1)}, f32[256,128]{1,0:T(8,128)S(1)}, u32[]{:S(2)}, u32[]{:S(2)}) collective-permute-start(f32[256,128]{1,0:T(8,128)S(1)} %get-tuple-element.53.own_ref), channel_id=1, source_target_pairs={{0,8},{8,0},{16,24},{24,16},{1,9},{9,1},{17,25},{25,17},{2,10},{10... | collective-permute-start | bytes 393224 | tf_op jit(solution)/shard_map/ppermute | solution.py:366
  9.6 7.4 %collective-permute-start.4 = (f32[64,256]{1,0:T(8,128)S(1)}, f32[64,256]{1,0:T(8,128)S(1)}, u32[]{:S(2)}, u32[]{:S(2)}) collective-permute-start(f32[64,256]{1,0:T(8,128)S(1)} %get-tuple-element.68), channel_id=1, source_target_pairs={{0,1},{1,0},{2,3},{3,2},{4,5},{5,4},{6,7},{7,6},{8,9},{9,8},{10,11... | collective-permute-start | bytes 196616 | tf_op jit(solution)/shard_map/ppermute | solution.py:366
  11.5 4.3 %collective-permute-start.3 = (f32[128,128]{1,0:T(8,128)S(1)}, f32[128,128]{1,0:T(8,128)S(1)}, u32[]{:S(2)}, u32[]{:S(2)}) collective-permute-start(f32[128,128]{1,0:T(8,128)S(1)} %shard_map.105.after_ref), channel_id=1, source_target_pairs={{0,16},{8,24},{16,0},{24,8},{1,17},{9,25},{17,1},{25,9},{2,18},{10... | collective-permute-start | bytes 196616 | tf_op jit(solution)/shard_map/ppermute | solution.py:366
  16.6 4.3 %collective-permute-start.5 = (f32[64,256]{1,0:T(8,128)S(1)}, f32[64,256]{1,0:T(8,128)S(1)}, u32[]{:S(2)}, u32[]{:S(2)}) collective-permute-start(f32[64,256]{1,0:T(8,128)S(1)} %get-tuple-element.83), channel_id=1, source_target_pairs={{0,1},{1,0},{2,3},{3,2},{4,5},{5,4},{6,7},{7,6},{8,9},{9,8},{10,11... | collective-permute-start | bytes 196616 | tf_op jit(solution)/shard_map/ppermute | solution.py:366

commit v9 on v8

--- a/solution.py
+++ b/solution.py
@@ -7,10 +7,11 @@
 
 F32 = jnp.float32
 BF16 = jnp.bfloat16
-BASE = 32
+BASE = 16
 PACK = 128
 NN = (((1,), (0,)), ((), ()))
 NT = (((1,), (1,)), ((), ()))
+TN = (((0,), (0,)), ((), ()))
 
 
 def split(x):
@@ -125,7 +126,6 @@
             below = below + mm(twice[1], below)
             moved = [m + mm(m, step, NT) for m, step in zip(moved, twice)]
         if last:
-            below = split(below)
             moved[1] = moved[1] + mm(moved[0], below, NT)
         if twice:
             found = [inv + mm(step, inv) for inv, step in zip(found, twice)]
@@ -163,21 +163,21 @@
     mask_ref[...] = jnp.concatenate([jnp.full((1, mask_ref.shape[1]), flag_ref[i], F32) for i in range(8)], 0)
 
 
-def inverse_kernel(k_ref, other_ref, kk_in_ref, damp_ref, rows_ref, inv_ref, w_ref, kk_ref, scale_ref, other_rows_ref):
+def gram(left, right):
+    return lax.dot_general(left, right, TN, preferred_element_type=F32)
+
+
+def inverse_kernel(k_ref, other_ref, kk_ref, damp_ref, rows_ref, half_ref, w_ref, scale_ref):
     other = other_ref[...]
-    other_f = other.astype(F32)
-    other_rows = other_f.T.astype(BF16)
     k_t = jnp.concatenate([k_ref[...], other], 0)
     mid = k_t.shape[1] // 2
+    upper = kk_ref[0:mid, 0:mid] + gram(other[:, 0:mid], other[:, 0:mid])
+    lower = kk_ref[mid:, :] + gram(other[:, mid:], other)
     grow, rate_row, k_sum = (rows_ref[i : i + 1, :] for i in (1, 3, 4))
+    other_f = other.astype(F32)
     square = k_sum + jnp.sum(other_f * other_f, 0, keepdims=True) + 1e-6
     k_scale = 1.0 / jnp.sqrt(square)
     both = k_scale * k_scale
-    upper = kk_in_ref[0:mid, 0:mid] + mm(other_rows[0:mid, :], other[:, 0:mid])
-    lower = kk_in_ref[mid:, :] + mm(other_rows[mid:, :], other)
-    kk_ref[0:mid, 0:mid] = upper
-    kk_ref[0:mid, mid:] = jnp.zeros_like(upper)
-    kk_ref[mid:, :] = lower
     upper = damp_ref[0:mid, 0:mid] * (upper * both[:, 0:mid])
     lower = damp_ref[mid:, :] * (lower * both)
     keys = k_t.astype(F32) * (rate_row * grow)
@@ -185,18 +185,18 @@
         [upper, lower[:, mid:]], [keys[:, :mid], keys[:, mid:]], lower[:, :mid]
     )
     w_ref[...] = jnp.concatenate(moved, 1) * both
-    inv_ref[0:mid, :] = jnp.concatenate([upper, jnp.zeros_like(upper)], 1)
-    inv_ref[mid:, :] = jnp.concatenate([mm(below, upper), lower], 1)
+    half_ref[0:mid, :] = upper
+    half_ref[mid : 2 * mid, :] = lower
+    half_ref[2 * mid :, :] = below
     scale_ref[...] = jnp.concatenate([k_scale, square * k_scale], 0)
-    other_rows_ref[...] = other_rows
 
 
 def shift_kernel(
-    q_ref, other_ref, k_ref, k_other_ref, k_rows_ref, g_ref, kq_ref, spread_t_ref, rows_ref, w_ref,
+    q_ref, other_ref, k_ref, k_other_ref, g_ref, kq_ref, spread_t_ref, rows_ref, w_ref,
     map_ref, score_g_ref, q_scale_ref,
 ):
     other = other_ref[...]
-    kq = kq_ref[...] + mm(k_rows_ref[...], other)
+    kq = kq_ref[...] + gram(k_other_ref[...], other)
     other_f = other.astype(F32)
     k_t = jnp.concatenate([k_ref[...], k_other_ref[...]], 0)
     q_f = jnp.concatenate([q_ref[...].astype(F32), other_f], 0)
@@ -224,7 +224,7 @@
 
 
 def update_kernel(
-    mask_ref, q_ref, q_other_ref, k_ref, k_other_ref, v_ref, g_ref, start_ref, inv_ref, spread_ref, rows_ref, scale_ref,
+    mask_ref, q_ref, q_other_ref, k_ref, k_other_ref, v_ref, g_ref, start_ref, half_ref, spread_ref, rows_ref, scale_ref,
     q_scale_ref, u_ref, base_ref, score_grad_ref, start_t_ref, keep_ref, send_ref,
 ):
     half, length = q_ref.shape
@@ -242,7 +242,11 @@
     grad_t = grad.astype(F32).T.astype(BF16)
     k_rows = k_t.astype(F32).T.astype(BF16)
     base = v_ref[...].astype(F32) - to_col(grow * k_scale, eye) * mm(k_rows, start, NT)
-    u = to_col(k_scale, eye) * mm(inv_ref[...], to_col(k_norm * rate_row, eye) * base)
+    mid = length // 2
+    write = to_col(k_norm * rate_row, eye) * base
+    first = mm(half_ref[0:mid, :], write[0:mid, :])
+    second = mm(half_ref[mid : 2 * mid, :], write[mid:, :]) + mm(half_ref[2 * mid :, :], first)
+    u = to_col(k_scale, eye) * jnp.concatenate([first, second], 0)
     score_grad = mm(grad, u, NT) * spread_ref[...]
     q_scale = q_scale_ref[...]
     dq = mm(k_t, score_grad * k_scale, NT) + grow * mm(start_t, grad_t)
@@ -257,7 +261,7 @@
 
 
 def local_kernel(
-    mask_ref, q_ref, q_other_ref, k_ref, k_other_ref, start_t_ref, inv_ref, score_g_ref, damp_ref, rows_ref, scale_ref,
+    mask_ref, q_ref, q_other_ref, k_ref, k_other_ref, start_t_ref, half_ref, score_g_ref, damp_ref, rows_ref, scale_ref,
     q_scale_ref, u_ref, score_grad_ref, ahead_ref, after_ref,
     uth_ref, utl_ref, uh_ref, ul_ref, ph_ref, pl_ref, pth_ref, ptl_ref, gh_ref, gl_ref, kh_ref, kl_ref, sym_ref, y_ref, dk_ref,
 ):
@@ -273,12 +277,17 @@
     ahead = jnp.where(low, ahead_ref[width:, :], 0.0)
     u = u_ref[...]
     u_ts = split(u.T)
-    inv = inv_ref[...]
     damp = damp_ref[...]
-    psi_t = mm(k_t, inv * to_col(tail * k_scale * k_scale, eye)) * k_norm
-    du_t = score_g_ref[...].T * (k_scale * k_scale)
+    mid = length // 2
+    solve = jnp.concatenate([score_g_ref[...].T, k_t.astype(F32) * tail], 0) * (k_scale * k_scale)
+    second = split(solve[:, mid:])
+    first = solve[:, 0:mid] + mm(second, half_ref[2 * mid :, :])
+    second = mm(second, half_ref[mid : 2 * mid, :])
+    first = mm(first, half_ref[0:mid, :])
+    solve = jnp.concatenate([first, second], 1) * k_norm
+    depth = solve.shape[0] - width
+    y_t, psi_t = solve[0:depth, :], solve[depth:, :]
     psi_s = split(psi_t.T)
-    y_t = mm(du_t, inv) * k_norm
     sym = damp + damp.T
     sym_ref[...] = sym
     y_t = y_t + mm(ahead.T, psi_t)
@@ -328,7 +337,7 @@
 
 
 def value_kernel(
-    mask_ref, got_ref, ph_ref, pl_ref, y_ref, base_ref, kk_ref, spread_ref, scale_ref, rows_ref, u_ref, keep_ref, got_q_ref,
+    mask_ref, got_ref, k_ref, k_other_ref, ph_ref, pl_ref, y_ref, base_ref, spread_ref, scale_ref, rows_ref, u_ref, keep_ref, got_q_ref,
     value_ref, rate_out_ref, q_ref,
 ):
     length = y_ref.shape[0]
@@ -336,7 +345,8 @@
     eye = row == lane
     k_scale = scale_ref[0:1, :]
     got = jnp.where(mask_ref[1:2, :] > 0.0, got_ref[...], 0.0)
-    low = jnp.where(lane < row, spread_ref[...] * kk_ref[...], 0.0) * (to_col(k_scale, eye) * k_scale)
+    k_t = jnp.concatenate([k_ref[...], k_other_ref[...]], 0)
+    low = jnp.where(lane < row, spread_ref[...] * gram(k_t, k_t), 0.0) * (to_col(k_scale, eye) * k_scale)
     y = y_ref[...] + mm((ph_ref[0:length, :], pl_ref[0:length, :]), got)
     write = base_ref[...] - mm(low, u_ref[...])
     value_ref[...] = to_col(rows_ref[3:4, :], eye) * y
@@ -406,12 +416,12 @@
         prep_kernel, [square, square, square, square, square, (8, length), (8, depth)],
         flags, q_t, k_t, log_decay, beta_rate, smem=(0,),
     )
-    inv, w_t, kk, scale, k_rows = call(
-        inverse_kernel, [square, wide, square, (2, length), ((length, half), BF16)], k_t, k_other, kk_own, damp, rows
+    halves, w_t, scale = call(
+        inverse_kernel, [(length + length // 2, length // 2), wide, (2, length)], k_t, k_other, kk_own, damp, rows
     )
     section, score_g, q_scale = call(
         shift_kernel, [(2 * width, depth), tall, thin],
-        q_t, q_other, k_t, k_other, k_rows, output_grad, kq_own, spread_t, rows, w_t,
+        q_t, q_other, k_t, k_other, output_grad, kq_own, spread_t, rows, w_t,
     )
     if stages == 2:
         ahead = swap(section, "seq", 0)
@@ -421,13 +431,13 @@
     arrived = swap(total, "seq", stages - 1)
     u, base, score_grad, start_t, keep_q, send_q = call(
         update_kernel, [tall, tall, square, (width, depth), (half, length), (half, length)],
-        mask, q_t, q_other, k_t, k_other, values, output_grad, start, inv, spread, rows, scale, q_scale,
+        mask, q_t, q_other, k_t, k_other, values, output_grad, start, halves, spread, rows, scale, q_scale,
     )
     got_q = swap(send_q, "head", 0)
     shapes = [(depth, length), (length + width, depth), (length + width, width), wide, wide, wide]
     *packs, sym, y, dk = call(
         local_kernel, [(shape, BF16) for shape in shapes for _ in range(2)] + [square, tall, wide],
-        mask, q_t, q_other, k_t, k_other, start_t, inv, score_g, damp, rows, scale, q_scale, u, score_grad, ahead,
+        mask, q_t, q_other, k_t, k_other, start_t, halves, score_g, damp, rows, scale, q_scale, u, score_grad, ahead,
         total,
     )
     send, keep = call(
@@ -437,7 +447,7 @@
     got_k = swap(send, "head", 0)
     value_grad, rate_grad, query_grad = call(
         value_kernel, [tall, thin, (half, length)],
-        mask, arrived, packs[4], packs[5], y, base, kk, spread, scale, rows, u, keep_q, got_q,
+        mask, arrived, k_t, k_other, packs[4], packs[5], y, base, spread, scale, rows, u, keep_q, got_q,
     )
     (key_grad,) = call(add_kernel, [(half, length)], keep, got_k)
     return (query_grad.T, key_grad.T, value_grad, rate_grad)

time: 21.8 us -> 21.8 us (level)
  transfers between devices with their start and end apart: 6 -> 6, of which waited for: 4 -> 4; matrix products, arithmetic and copies ran while one was open for 0% -> 0% of each run, Pallas kernels for 30% -> 31%
where the time goes in v9:
time: 21.8 us; the launch traced here: 21.5 us
  Pallas kernels  7.93 us (36%)
  starting transfers between devices  6.92 us (32%)
  waiting for transfers between devices  5.02 us (23%)
  local copies, waits for them, and re-layouts  0.96 us (4%)
  between operations  0.7 us (3%)
    pallas_call x9, Pallas kernels, call(): pl.pallas_call(kernel, out_shape=tuple((jax.ShapeDtypeStruct(shape, kind)...  7.93 us
    ppermute x6, starting transfers between devices, swap(): lax.ppermute(x, axis, [(i, i ^ 1 << apart) for i in range(lax.axis_size(a...  6.92 us
    ppermute x6, waiting for transfers between devices, swap(): lax.ppermute(x, axis, [(i, i ^ 1 << apart) for i in range(lax.axis_size(a...  5.02 us
    unnamed x14, local copies, waits for them, and re-layouts  0.88 us
  transfers between devices with their start and end apart: 6, of which 4 were waited for; matrix products, arithmetic and copies ran while one was open for 0% of the time, Pallas kernels for 31%

profile of v9, /device:TPU:0, one launch (start us, length us, event | category | flops | bytes accessed | tf_op | source)
XLA Modules:
  0.0 21.5 jit_solution(17372784178118505649)
XLA Ops:
  0.6 3.0 %collective-permute-start.1 = (bf16[64,256]{1,0:T(8,128)(2,1)}, bf16[64,256]{1,0:T(8,128)(2,1)S(1)}, u32[]{:S(2)}, u32[]{:S(2)}) collective-permute-start(bf16[64,256]{1,0:T(8,128)(2,1)} %bitcast.15), channel_id=1, source_target_pairs={{0,1},{1,0},{2,3},{3,2},{4,5},{5,4},{6,7},{7,6},{8,9},{9,8},{10,11... | collective-permute-start | bytes 98312 | tf_op jit(solution)/shard_map/ppermute | solution.py:376
  3.7 0.1 collective-permute-start
  3.7 0.1 stack.23
  3.8 0.6 %copy-done.6 = f32[1,256]{1,0:T(1,128)S(1)} copy-done((f32[1,256]{1,0:T(1,128)S(1)}, f32[1,256]{1,0:T(1,128)}, u32[]{:S(2)}) %copy-start.6) | copy-done | bytes 1048
  4.4 0.1 copy-done.4
  4.5 0.8 %shard_map.102 = (f32[256,256]{1,0:T(8,128)S(1)}, f32[256,256]{1,0:T(8,128)S(1)}, f32[256,256]{1,0:T(8,128)S(1)}, f32[256,256]{1,0:T(8,128)S(1)}, f32[256,256]{1...) custom-call(f32[8]{0:T(128)S(1)} %convert_element_type.3.flag_ref, bf16[64,256]{1,0:T(8,128)(2,1)S(1)} %bitcast.11, ...), custom_call_target="tpu_custom_call" | custom-call | flops 1000000000 | bytes 1048576 | tf_op jit(solution)/shard_map/pallas_call | solution.py:363
  5.4 0.4 %collective-permute-done.1.other_ref.k_other_ref = bf16[64,256]{1,0:T(8,128)(2,1)S(1)} collective-permute-done((bf16[64,256]{1,0:T(8,128)(2,1)}, bf16[64,256]{1,0:T(8,128)(2,1)S(1)}, u32[]{:S(2)}, u32[]{:S(2)}) %collective-permute-start.1) | collective-permute-done | bytes 32800 | tf_op jit(solution)/shard_map/ppermute | solution.py:376
  5.8 1.5 %shard_map.103 = (f32[384,128]{1,0:T(8,128)S(1)}, f32[128,256]{1,0:T(8,128)S(1)}, f32[2,256]{1,0:T(2,128)S(1)}) custom-call(bf16[64,256]{1,0:T(8,128)(2,1)S(1)} %bitcast.17, bf16[64,256]{1,0:T(8,128)(2,1)S(1)} %collective-permute-done.1.other_ref.k_other_ref, f32[256,256]{1,0:T(8,128)S(1)} %get-tuple-element.47.kk_ref, ...), custom_call_target="tpu_custom_call" | custom-call | flops 1000000000 | bytes 1048576 | tf_op jit(solution)/shard_map/pallas_call | solution.py:363
  7.3 0.5 %collective-permute-done.other_ref.q_other_ref = bf16[64,256]{1,0:T(8,128)(2,1)S(1)} collective-permute-done((bf16[64,256]{1,0:T(8,128)(2,1)}, bf16[64,256]{1,0:T(8,128)(2,1)S(1)}, u32[]{:S(2)}, u32[]{:S(2)}) %collective-permute-start) | collective-permute-done | bytes 32800 | tf_op jit(solution)/shard_map/ppermute | solution.py:376
  7.8 0.6 %shard_map.104 = (f32[256,128]{1,0:T(8,128)S(1)}, f32[256,128]{1,0:T(8,128)S(1)}, f32[1,256]{1,0:T(1,128)S(1)}) custom-call(bf16[64,256]{1,0:T(8,128)(2,1)S(1)} %bitcast.12, bf16[64,256]{1,0:T(8,128)(2,1)S(1)} %collective-permute-done.other_ref.q_other_ref, bf16[64,256]{1,0:T(8,128)(2,1)S(1)} %bitcast.18, ...), custom_call_target="tpu_custom_call" | custom-call | flops 1000000000 | bytes 1048576 | tf_op jit(solution)/shard_map/pallas_call | solution.py:363
  8.4 0.1 collective-permute-start.2
  8.5 0.1 copy-done.1
  8.6 0.0 copy-done.2
  8.7 1.1 %shard_map.106 = (f32[256,128]{1,0:T(8,128)S(1)}, f32[256,128]{1,0:T(8,128)S(1)}, f32[256,256]{1,0:T(8,128)S(1)}, f32[128,128]{1,0:T(8,128)S(1)}, f32[64,256]{1,0:T(8,128)S(1)}, /*index=5*/f32[64,256]{1,0:T(8,128)S(1)}) custom-call(f32[8,128]{1,0:T(8,128)S(1)} %get-tuple-element.43.mask_ref, bf16[64,256]{1,0:T(8,128)(2,1)S(1)} %bitcast.13, ...), custom_call_target="tpu_custom_call" | custom-call | flops 1000000000 | bytes 1048576 | tf_op jit(solution)/shard_map/pallas_call | solution.py:363
  9.7 1.6 %collective-permute-start.4 = (f32[64,256]{1,0:T(8,128)S(1)}, f32[64,256]{1,0:T(8,128)S(1)}, u32[]{:S(2)}, u32[]{:S(2)}) collective-permute-start(f32[64,256]{1,0:T(8,128)S(1)} %get-tuple-element.64), channel_id=1, source_target_pairs={{0,1},{1,0},{2,3},{3,2},{4,5},{5,4},{6,7},{7,6},{8,9},{9,8},{10,11... | collective-permute-start | bytes 196616 | tf_op jit(solution)/shard_map/ppermute | solution.py:376
  11.3 0.2 shard_map.105.after_ref
  11.5 1.6 %collective-permute-start.3 = (f32[128,128]{1,0:T(8,128)S(1)}, f32[128,128]{1,0:T(8,128)S(1)}, u32[]{:S(2)}, u32[]{:S(2)}) collective-permute-start(f32[128,128]{1,0:T(8,128)S(1)} %shard_map.105.after_ref), channel_id=1, source_target_pairs={{0,16},{8,24},{16,0},{24,8},{1,17},{9,25},{17,1},{25,9},{2,18},{10... | collective-permute-start | bytes 196616 | tf_op jit(solution)/shard_map/ppermute | solution.py:376
  13.1 1.2 %shard_map.107 = (bf16[128,256]{1,0:T(8,128)(2,1)S(1)}, bf16[128,256]{1,0:T(8,128)(2,1)S(1)}, bf16[384,128]{1,0:T(8,128)(2,1)S(1)}, bf16[384,128]{1,0:T(8,128)(2...) custom-call(f32[8,128]{1,0:T(8,128)S(1)} %get-tuple-element.43.mask_, ...), custom_call_target="tpu_custom_call" | custom-call | flops 1000000000 | bytes 1048576 | tf_op jit(solution)/shard_map/pallas_call | solution.py:363
  14.3 1.5 %collective-permute-done.3.got_ref = f32[128,128]{1,0:T(8,128)S(1)} collective-permute-done((f32[128,128]{1,0:T(8,128)S(1)}, f32[128,128]{1,0:T(8,128)S(1)}, u32[]{:S(2)}, u32[]{:S(2)}) %collective-permute-start.3) | collective-permute-done | bytes 65568 | tf_op jit(solution)/shard_map/ppermute | solution.py:376
  15.8 0.8 %shard_map.109 = (f32[64,256]{1,0:T(8,128)S(1)}, f32[64,256]{1,0:T(8,128)S(1)}) custom-call(f32[8,128]{1,0:T(8,128)S(1)} %get-tuple-element.43.mask_ref, f32[128,128]{1,0:T(8,128)S(1)} %collective-permute-done.3.got_ref, bf16[64,256]{1,0:T(8,128)(2,1)S(1)} %bitcast.21, bf16[64,256]{1,0:T(8,128)(2,1)S(1)} %collective-permute-done.1.other_ref.k_other_ref, ...), custom_call_target="tpu_custom_call" | custom-call | flops 1000000000 | bytes 1048576 | tf_op jit(solution)/shard_map/pallas_call | solution.py:363
  16.6 0.6 %collective-permute-start.5 = (f32[64,256]{1,0:T(8,128)S(1)}, f32[64,256]{1,0:T(8,128)S(1)}, u32[]{:S(2)}, u32[]{:S(2)}) collective-permute-start(f32[64,256]{1,0:T(8,128)S(1)} %get-tuple-element.79), channel_id=1, source_target_pairs={{0,1},{1,0},{2,3},{3,2},{4,5},{5,4},{6,7},{7,6},{8,9},{9,8},{10,11... | collective-permute-start | bytes 196616 | tf_op jit(solution)/shard_map/ppermute | solution.py:376
  17.2 1.2 %shard_map.108 = (f32[256,128]{1,0:T(8,128)}, f32[1,256]{1,0:T(1,128)}, f32[64,256]{1,0:T(8,128)}) custom-call(f32[8,128]{1,0:T(8,128)S(1)} %get-tuple-element.43.mask_ref, f32[128,128]{1,0:T(8,128)S(1)} %collective-permute-done.3.got_ref, bf16[64,256]{1,0:T(8,128)(2,1)S(1)} %bitcast.22, bf16[64,256]{1,0:T(8,128)(2,1)S(1)} %collective-permute-done.1.other_ref.k_other_ref, ...), custom_call_target="tpu_custom_call" | custom-call | flops 1000000000 | bytes 1048576 | tf_op jit(solution)/shard_map/pallas_call | solution.py:363
  18.3 2.6 %collective-permute-done.5.got_ref = f32[64,256]{1,0:T(8,128)S(1)} collective-permute-done((f32[64,256]{1,0:T(8,128)S(1)}, f32[64,256]{1,0:T(8,128)S(1)}, u32[]{:S(2)}, u32[]{:S(2)}) %collective-permute-start.5) | collective-permute-done | bytes 65568 | tf_op jit(solution)/shard_map/ppermute | solution.py:376
  20.9 0.6 %shard_map.110 = f32[64,256]{1,0:T(8,128)} custom-call(f32[64,256]{1,0:T(8,128)S(1)} %get-tuple-element.78.keep_ref, f32[64,256]{1,0:T(8,128)S(1)} %collective-permute-done.5.got_ref), custom_call_target="tpu_custom_call" | custom-call | flops 1000000000 | bytes 1048576 | tf_op jit(solution)/shard_map/pallas_call | solution.py:363
  (13 shorter events, 0.0 us)
Async XLA Ops:
  0.6 5.1 %collective-permute-start.1 = (bf16[64,256]{1,0:T(8,128)(2,1)}, bf16[64,256]{1,0:T(8,128)(2,1)S(1)}, u32[]{:S(2)}, u32[]{:S(2)}) collective-permute-start(bf16[64,256]{1,0:T(8,128)(2,1)} %bitcast.15), channel_id=1, source_target_pairs={{0,1},{1,0},{2,3},{3,2},{4,5},{5,4},{6,7},{7,6},{8,9},{9,8},{10,11... | collective-permute-start | bytes 98312 | tf_op jit(solution)/shard_map/ppermute | solution.py:376
  3.7 4.1 %collective-permute-start = (bf16[64,256]{1,0:T(8,128)(2,1)}, bf16[64,256]{1,0:T(8,128)(2,1)S(1)}, u32[]{:S(2)}, u32[]{:S(2)}) collective-permute-start(bf16[64,256]{1,0:T(8,128)(2,1)} %bitcast.10), channel_id=1, source_target_pairs={{0,1},{1,0},{2,3},{3,2},{4,5},{5,4},{6,7},{7,6},{8,9},{9,8},{10,11... | collective-permute-start | bytes 98312 | tf_op jit(solution)/shard_map/ppermute | solution.py:376
  3.7 0.7 %copy-start.6 = (f32[1,256]{1,0:T(1,128)S(1)}, f32[1,256]{1,0:T(1,128)}, u32[]{:S(2)}) copy-start(f32[1,256]{1,0:T(1,128)} %rate_ref.1) | copy-start | bytes 3076
  3.7 0.8 %copy-start.4 = (bf16[256,64]{0,1:T(8,128)(2,1)S(1)}, bf16[256,64]{0,1:T(8,128)(2,1)}, u32[]{:S(2)}) copy-start(bf16[256,64]{0,1:T(8,128)(2,1)} %param.8) | copy-start | bytes 98308
  3.7 0.8 %copy-start.3 = (bf16[256,64]{0,1:T(8,128)(2,1)S(1)}, bf16[256,64]{0,1:T(8,128)(2,1)}, u32[]{:S(2)}) copy-start(bf16[256,64]{0,1:T(8,128)(2,1)} %param.7) | copy-start | bytes 98308
  3.8 0.7 %copy-start.5 = (f32[1,256]{1,0:T(1,128)S(1)}, f32[1,256]{1,0:T(1,128)}, u32[]{:S(2)}) copy-start(f32[1,256]{1,0:T(1,128)} %decay_ref.1) | copy-start | bytes 3076
  5.8 2.0 %copy-start = (bf16[256,128]{1,0:T(8,128)(2,1)S(1)}, bf16[256,128]{1,0:T(8,128)(2,1)}, u32[]{:S(2)}) copy-start(bf16[256,128]{1,0:T(8,128)(2,1)} %g_ref.3) | copy-start | bytes 196612
  7.8 0.8 %copy-start.1 = (bf16[256,128]{1,0:T(8,128)(2,1)S(1)}, bf16[256,128]{1,0:T(8,128)(2,1)}, u32[]{:S(2)}) copy-start(bf16[256,128]{1,0:T(8,128)(2,1)} %v_ref.1) | copy-start | bytes 196612
  7.8 0.9 %copy-start.2 = (f32[1,1,128,128]{3,2,1,0:T(8,128)S(1)}, f32[1,1,128,128]{3,2,1,0:T(8,128)}, u32[]{:S(2)}) copy-start(f32[1,1,128,128]{3,2,1,0:T(8,128)} %param.12) | copy-start | bytes 196612
  8.4 2.9 %collective-permute-start.2 = (f32[256,128]{1,0:T(8,128)S(1)}, f32[256,128]{1,0:T(8,128)S(1)}, u32[]{:S(2)}, u32[]{:S(2)}) collective-permute-start(f32[256,128]{1,0:T(8,128)S(1)} %get-tuple-element.50.own_ref), channel_id=1, source_target_pairs={{0,8},{8,0},{16,24},{24,16},{1,9},{9,1},{17,25},{25,17},{2,10},{10... | collective-permute-start | bytes 393224 | tf_op jit(solution)/shard_map/ppermute | solution.py:376
  9.7 7.4 %collective-permute-start.4 = (f32[64,256]{1,0:T(8,128)S(1)}, f32[64,256]{1,0:T(8,128)S(1)}, u32[]{:S(2)}, u32[]{:S(2)}) collective-permute-start(f32[64,256]{1,0:T(8,128)S(1)} %get-tuple-element.64), channel_id=1, source_target_pairs={{0,1},{1,0},{2,3},{3,2},{4,5},{5,4},{6,7},{7,6},{8,9},{9,8},{10,11... | collective-permute-start | bytes 196616 | tf_op jit(solution)/shard_map/ppermute | solution.py:376
  11.5 4.3 %collective-permute-start.3 = (f32[128,128]{1,0:T(8,128)S(1)}, f32[128,128]{1,0:T(8,128)S(1)}, u32[]{:S(2)}, u32[]{:S(2)}) collective-permute-start(f32[128,128]{1,0:T(8,128)S(1)} %shard_map.105.after_ref), channel_id=1, source_target_pairs={{0,16},{8,24},{16,0},{24,8},{1,17},{9,25},{17,1},{25,9},{2,18},{10... | collective-permute-start | bytes 196616 | tf_op jit(solution)/shard_map/ppermute | solution.py:376
  16.6 4.3 %collective-permute-start.5 = (f32[64,256]{1,0:T(8,128)S(1)}, f32[64,256]{1,0:T(8,128)S(1)}, u32[]{:S(2)}, u32[]{:S(2)}) collective-permute-start(f32[64,256]{1,0:T(8,128)S(1)} %get-tuple-element.79), channel_id=1, source_target_pairs={{0,1},{1,0},{2,3},{3,2},{4,5},{5,4},{6,7},{7,6},{8,9},{9,8},{10,11... | collective-permute-start | bytes 196616 | tf_op jit(solution)/shard_map/ppermute | solution.py:376

commit v10 on v9

--- a/solution.py
+++ b/solution.py
@@ -167,7 +167,9 @@
     return lax.dot_general(left, right, TN, preferred_element_type=F32)
 
 
-def inverse_kernel(k_ref, other_ref, kk_ref, damp_ref, rows_ref, half_ref, w_ref, scale_ref):
+def inverse_kernel(
+    k_ref, other_ref, kk_ref, damp_ref, rows_ref, half_ref, w_ref, scale_ref, other_rows_ref,
+):
     other = other_ref[...]
     k_t = jnp.concatenate([k_ref[...], other], 0)
     mid = k_t.shape[1] // 2
@@ -184,7 +186,9 @@
     (upper, lower), moved, below = inverses(
         [upper, lower[:, mid:]], [keys[:, :mid], keys[:, mid:]], lower[:, :mid]
     )
-    w_ref[...] = jnp.concatenate(moved, 1) * both
+    w_t = jnp.concatenate(moved, 1) * both
+    w_ref[...] = w_t
+    other_rows_ref[...] = other_f.T.astype(BF16)
     half_ref[0:mid, :] = upper
     half_ref[mid : 2 * mid, :] = lower
     half_ref[2 * mid :, :] = below
@@ -192,25 +196,28 @@
 
 
 def shift_kernel(
-    q_ref, other_ref, k_ref, k_other_ref, g_ref, kq_ref, spread_t_ref, rows_ref, w_ref,
+    q_ref, other_ref, k_ref, k_other_ref, k_rows_ref, g_ref, kq_ref, spread_t_ref, rows_ref, w_ref,
     map_ref, score_g_ref, q_scale_ref,
 ):
     other = other_ref[...]
-    kq = kq_ref[...] + gram(k_other_ref[...], other)
+    mid = other.shape[1] // 2
+    top = kq_ref[0:mid, :] + mm(k_rows_ref[0:mid, :], other)
+    bottom = kq_ref[mid:, mid:] + mm(k_rows_ref[mid:, :], other[:, mid:])
     other_f = other.astype(F32)
+    q_sum = rows_ref[5:6, :] + jnp.sum(other_f * other_f, 0, keepdims=True)
+    width = w_ref.shape[0]
     k_t = jnp.concatenate([k_ref[...], k_other_ref[...]], 0)
-    q_f = jnp.concatenate([q_ref[...].astype(F32), other_f], 0)
-    width, length = k_t.shape
-    grow, tail = rows_ref[1:2, :], rows_ref[2:3, :]
-    q_sum = rows_ref[5:6, :] + jnp.sum(other_f * other_f, 0, keepdims=True)
+    ends = jnp.where(jnp.equal(*ids((width, width))), rows_ref[1:2, 2 * mid - 1 :], 0.0)
+    own_map = ends - mm(w_ref[...] * rows_ref[2:3, :], k_t, NT)
     q_scale = width ** (-0.5) / jnp.sqrt(q_sum + 1e-6)
     grad = g_ref[...]
-    score_g = mm(spread_t_ref[...] * (kq * q_scale), grad)
-    w_t = w_ref[...]
-    w_row, w_lane = ids((width, width))
-    direct = mm(q_f * (q_scale * grow), grad)
-    map_ref[0:width, :] = jnp.where(w_row == w_lane, grow[:, length - 1 :], 0.0) - mm(w_t * tail, k_t, NT)
-    map_ref[width:, :] = direct - mm(w_t, score_g)
+    top = mm(spread_t_ref[0:mid, :] * (top * q_scale), grad)
+    bottom = mm(spread_t_ref[mid:, mid:] * (bottom * q_scale[:, mid:]), grad[mid:, :])
+    score_g = jnp.concatenate([top, bottom], 0)
+    q_f = jnp.concatenate([q_ref[...].astype(F32), other_f], 0)
+    direct = mm(q_f * (q_scale * rows_ref[1:2, :]), grad)
+    map_ref[width:, :] = direct - mm(w_ref[...], score_g)
+    map_ref[0:width, :] = own_map
     score_g_ref[...] = score_g
     q_scale_ref[...] = q_scale
 
@@ -325,10 +332,22 @@
     got_s = split(jnp.where(mask_ref[1:2, :] > 0.0, got_ref[...], 0.0))
     gu_s = split(mm(got_s, (uth_ref[...], utl_ref[...])))
     right = mm((uh_ref[...], ul_ref[...]), got_s, NT)
-    upper = mm(right[0:length, :], (pth_ref[...], ptl_ref[...]))
-    left = mm((ph_ref[...], pl_ref[...]), gu_s)
-    inner = sym_ref[...] * jnp.where(lane < row, left[0:length, :], upper)
-    dk = dk_ref[...] + rows_ref[2:3, :] * left[length:, :] - mm(right[length:, :], (gh_ref[...], gl_ref[...]))
+    mid = length // 2
+    low = lane[:mid, :mid] < row[:mid, :mid]
+    gu_left = (gu_s[0][:, :mid], gu_s[1][:, :mid])
+    left_top = mm((ph_ref[0:mid, :], pl_ref[0:mid, :]), gu_left)
+    left = mm((ph_ref[mid:, :], pl_ref[mid:, :]), gu_s)
+    upper = mm(right[0:mid, :], (pth_ref[...], ptl_ref[...]))
+    upper_low = mm(right[mid:length, :], (pth_ref[:, mid:], ptl_ref[:, mid:]))
+    inner = jnp.concatenate(
+        [
+            jnp.concatenate([jnp.where(low, left_top, upper[:, :mid]), upper[:, mid:]], 1),
+            jnp.concatenate([left[0:mid, :mid], jnp.where(low, left[0:mid, mid:], upper_low)], 1),
+        ],
+        0,
+    )
+    inner = sym_ref[...] * inner
+    dk = dk_ref[...] + rows_ref[2:3, :] * left[mid:, :] - mm(right[length:, :], (gh_ref[...], gl_ref[...]))
     dk = dk + mm((kh_ref[...], kl_ref[...]), inner)
     unit = jnp.concatenate([k_ref[...], k_other_ref[...]], 0).astype(F32) * k_scale
     dk = k_scale * (dk - unit * jnp.sum(unit * dk, 0, keepdims=True))
@@ -416,12 +435,14 @@
         prep_kernel, [square, square, square, square, square, (8, length), (8, depth)],
         flags, q_t, k_t, log_decay, beta_rate, smem=(0,),
     )
-    halves, w_t, scale = call(
-        inverse_kernel, [(length + length // 2, length // 2), wide, (2, length)], k_t, k_other, kk_own, damp, rows
+    halves, w_t, scale, k_rows = call(
+        inverse_kernel,
+        [(length + length // 2, length // 2), wide, (2, length), ((length, half), BF16)],
+        k_t, k_other, kk_own, damp, rows,
     )
     section, score_g, q_scale = call(
         shift_kernel, [(2 * width, depth), tall, thin],
-        q_t, q_other, k_t, k_other, output_grad, kq_own, spread_t, rows, w_t,
+        q_t, q_other, k_t, k_other, k_rows, output_grad, kq_own, spread_t, rows, w_t,
     )
     if stages == 2:
         ahead = swap(section, "seq", 0)

time: 21.8 us -> 21.7 us (level)
  no operation moved by 1% of the time
where the time goes in v10:
time: 21.7 us; the launch traced here: 21.5 us
  Pallas kernels  7.84 us (36%)
  starting transfers between devices  6.92 us (32%)
  waiting for transfers between devices  5.01 us (23%)
  local copies, waits for them, and re-layouts  1.02 us (5%)
  between operations  0.7 us (3%)
    pallas_call x9, Pallas kernels, call(): pl.pallas_call(kernel, out_shape=tuple((jax.ShapeDtypeStruct(shape, kind)...  7.84 us
    ppermute x6, starting transfers between devices, swap(): lax.ppermute(x, axis, [(i, i ^ 1 << apart) for i in range(lax.axis_size(a...  6.92 us
    ppermute x6, waiting for transfers between devices, swap(): lax.ppermute(x, axis, [(i, i ^ 1 << apart) for i in range(lax.axis_size(a...  5.01 us
    unnamed x14, local copies, waits for them, and re-layouts  0.94 us
  transfers between devices with their start and end apart: 6, of which 4 were waited for; matrix products, arithmetic and copies ran while one was open for 0% of the time, Pallas kernels for 31%

profile of v10, /device:TPU:0, one launch (start us, length us, event | category | flops | bytes accessed | tf_op | source)
XLA Modules:
  0.0 21.5 jit_solution(8499694089692561620)
XLA Ops:
  0.6 3.0 %collective-permute-start.1 = (bf16[64,256]{1,0:T(8,128)(2,1)}, bf16[64,256]{1,0:T(8,128)(2,1)S(1)}, u32[]{:S(2)}, u32[]{:S(2)}) collective-permute-start(bf16[64,256]{1,0:T(8,128)(2,1)} %bitcast.15), channel_id=1, source_target_pairs={{0,1},{1,0},{2,3},{3,2},{4,5},{5,4},{6,7},{7,6},{8,9},{9,8},{10,11... | collective-permute-start | bytes 98312 | tf_op jit(solution)/shard_map/ppermute | solution.py:395
  3.7 0.1 collective-permute-start
  3.7 0.1 stack.23
  3.8 0.6 %copy-done.6 = f32[1,256]{1,0:T(1,128)S(1)} copy-done((f32[1,256]{1,0:T(1,128)S(1)}, f32[1,256]{1,0:T(1,128)}, u32[]{:S(2)}) %copy-start.6) | copy-done | bytes 1048
  4.4 0.1 copy-done.4
  4.5 0.8 %shard_map.102 = (f32[256,256]{1,0:T(8,128)S(1)}, f32[256,256]{1,0:T(8,128)S(1)}, f32[256,256]{1,0:T(8,128)S(1)}, f32[256,256]{1,0:T(8,128)S(1)}, f32[256,256]{1...) custom-call(f32[8]{0:T(128)S(1)} %convert_element_type.3.flag_ref, bf16[64,256]{1,0:T(8,128)(2,1)S(1)} %bitcast.11, ...), custom_call_target="tpu_custom_call" | custom-call | flops 1000000000 | bytes 1048576 | tf_op jit(solution)/shard_map/pallas_call | solution.py:382
  5.4 0.4 %collective-permute-done.1.other_ref.k_other_ref = bf16[64,256]{1,0:T(8,128)(2,1)S(1)} collective-permute-done((bf16[64,256]{1,0:T(8,128)(2,1)}, bf16[64,256]{1,0:T(8,128)(2,1)S(1)}, u32[]{:S(2)}, u32[]{:S(2)}) %collective-permute-start.1) | collective-permute-done | bytes 32800 | tf_op jit(solution)/shard_map/ppermute | solution.py:395
  5.8 1.5 %shard_map.103 = (f32[384,128]{1,0:T(8,128)S(1)}, f32[128,256]{1,0:T(8,128)S(1)}, f32[2,256]{1,0:T(2,128)S(1)}, bf16[256,64]{1,0:T(8,128)(2,1)S(1)}) custom-call(bf16[64,256]{1,0:T(8,128)(2,1)S(1)} %bitcast.17, bf16[64,256]{1,0:T(8,128)(2,1)S(1)} %collective-permute-done.1.other_ref.k_other_ref, f32[256,256]{1,0:T(8,128)S(1)} %get-tuple-element.45.kk_ref, ...), custom_call_target="tpu_custom_call" | custom-call | flops 1000000000 | bytes 1048576 | tf_op jit(solution)/shard_map/pallas_call | solution.py:382
  7.3 0.5 %collective-permute-done.other_ref.q_other_ref = bf16[64,256]{1,0:T(8,128)(2,1)S(1)} collective-permute-done((bf16[64,256]{1,0:T(8,128)(2,1)}, bf16[64,256]{1,0:T(8,128)(2,1)S(1)}, u32[]{:S(2)}, u32[]{:S(2)}) %collective-permute-start) | collective-permute-done | bytes 32800 | tf_op jit(solution)/shard_map/ppermute | solution.py:395
  7.8 0.6 %shard_map.104 = (f32[256,128]{1,0:T(8,128)S(1)}, f32[256,128]{1,0:T(8,128)S(1)}, f32[1,256]{1,0:T(1,128)S(1)}) custom-call(bf16[64,256]{1,0:T(8,128)(2,1)S(1)} %bitcast.12, bf16[64,256]{1,0:T(8,128)(2,1)S(1)} %collective-permute-done.other_ref.q_other_ref, bf16[64,256]{1,0:T(8,128)(2,1)S(1)} %bitcast.18, ...), custom_call_target="tpu_custom_call" | custom-call | flops 1000000000 | bytes 1048576 | tf_op jit(solution)/shard_map/pallas_call | solution.py:382
  8.4 0.1 collective-permute-start.2
  8.4 0.2 copy-done.1
  8.6 0.0 copy-done.2
  8.7 1.1 %shard_map.106 = (f32[256,128]{1,0:T(8,128)S(1)}, f32[256,128]{1,0:T(8,128)S(1)}, f32[256,256]{1,0:T(8,128)S(1)}, f32[128,128]{1,0:T(8,128)S(1)}, f32[64,256]{1,0:T(8,128)S(1)}, /*index=5*/f32[64,256]{1,0:T(8,128)S(1)}) custom-call(f32[8,128]{1,0:T(8,128)S(1)} %get-tuple-element.44.mask_ref, bf16[64,256]{1,0:T(8,128)(2,1)S(1)} %bitcast.13, ...), custom_call_target="tpu_custom_call" | custom-call | flops 1000000000 | bytes 1048576 | tf_op jit(solution)/shard_map/pallas_call | solution.py:382
  9.7 1.6 %collective-permute-start.4 = (f32[64,256]{1,0:T(8,128)S(1)}, f32[64,256]{1,0:T(8,128)S(1)}, u32[]{:S(2)}, u32[]{:S(2)}) collective-permute-start(f32[64,256]{1,0:T(8,128)S(1)} %get-tuple-element.66), channel_id=1, source_target_pairs={{0,1},{1,0},{2,3},{3,2},{4,5},{5,4},{6,7},{7,6},{8,9},{9,8},{10,11... | collective-permute-start | bytes 196616 | tf_op jit(solution)/shard_map/ppermute | solution.py:395
  11.3 0.2 shard_map.105.after_ref
  11.5 1.6 %collective-permute-start.3 = (f32[128,128]{1,0:T(8,128)S(1)}, f32[128,128]{1,0:T(8,128)S(1)}, u32[]{:S(2)}, u32[]{:S(2)}) collective-permute-start(f32[128,128]{1,0:T(8,128)S(1)} %shard_map.105.after_ref), channel_id=1, source_target_pairs={{0,16},{8,24},{16,0},{24,8},{1,17},{9,25},{17,1},{25,9},{2,18},{10... | collective-permute-start | bytes 196616 | tf_op jit(solution)/shard_map/ppermute | solution.py:395
  13.1 1.2 %shard_map.107 = (bf16[128,256]{1,0:T(8,128)(2,1)S(1)}, bf16[128,256]{1,0:T(8,128)(2,1)S(1)}, bf16[384,128]{1,0:T(8,128)(2,1)S(1)}, bf16[384,128]{1,0:T(8,128)(2...) custom-call(f32[8,128]{1,0:T(8,128)S(1)} %get-tuple-element.44.mask_, ...), custom_call_target="tpu_custom_call" | custom-call | flops 1000000000 | bytes 1048576 | tf_op jit(solution)/shard_map/pallas_call | solution.py:382
  14.3 1.5 %collective-permute-done.3.got_ref = f32[128,128]{1,0:T(8,128)S(1)} collective-permute-done((f32[128,128]{1,0:T(8,128)S(1)}, f32[128,128]{1,0:T(8,128)S(1)}, u32[]{:S(2)}, u32[]{:S(2)}) %collective-permute-start.3) | collective-permute-done | bytes 65568 | tf_op jit(solution)/shard_map/ppermute | solution.py:395
  15.8 0.7 %shard_map.109 = (f32[64,256]{1,0:T(8,128)S(1)}, f32[64,256]{1,0:T(8,128)S(1)}) custom-call(f32[8,128]{1,0:T(8,128)S(1)} %get-tuple-element.44.mask_ref, f32[128,128]{1,0:T(8,128)S(1)} %collective-permute-done.3.got_ref, bf16[64,256]{1,0:T(8,128)(2,1)S(1)} %bitcast.21, bf16[64,256]{1,0:T(8,128)(2,1)S(1)} %collective-permute-done.1.other_ref.k_other_ref, ...), custom_call_target="tpu_custom_call" | custom-call | flops 1000000000 | bytes 1048576 | tf_op jit(solution)/shard_map/pallas_call | solution.py:382
  16.5 0.6 %collective-permute-start.5 = (f32[64,256]{1,0:T(8,128)S(1)}, f32[64,256]{1,0:T(8,128)S(1)}, u32[]{:S(2)}, u32[]{:S(2)}) collective-permute-start(f32[64,256]{1,0:T(8,128)S(1)} %get-tuple-element.81), channel_id=1, source_target_pairs={{0,1},{1,0},{2,3},{3,2},{4,5},{5,4},{6,7},{7,6},{8,9},{9,8},{10,11... | collective-permute-start | bytes 196616 | tf_op jit(solution)/shard_map/ppermute | solution.py:395
  17.1 1.2 %shard_map.108 = (f32[256,128]{1,0:T(8,128)}, f32[1,256]{1,0:T(1,128)}, f32[64,256]{1,0:T(8,128)}) custom-call(f32[8,128]{1,0:T(8,128)S(1)} %get-tuple-element.44.mask_ref, f32[128,128]{1,0:T(8,128)S(1)} %collective-permute-done.3.got_ref, bf16[64,256]{1,0:T(8,128)(2,1)S(1)} %bitcast.22, bf16[64,256]{1,0:T(8,128)(2,1)S(1)} %collective-permute-done.1.other_ref.k_other_ref, ...), custom_call_target="tpu_custom_call" | custom-call | flops 1000000000 | bytes 1048576 | tf_op jit(solution)/shard_map/pallas_call | solution.py:382
  18.3 2.6 %collective-permute-done.5.got_ref = f32[64,256]{1,0:T(8,128)S(1)} collective-permute-done((f32[64,256]{1,0:T(8,128)S(1)}, f32[64,256]{1,0:T(8,128)S(1)}, u32[]{:S(2)}, u32[]{:S(2)}) %collective-permute-start.5) | collective-permute-done | bytes 65568 | tf_op jit(solution)/shard_map/ppermute | solution.py:395
  20.9 0.6 %shard_map.110 = f32[64,256]{1,0:T(8,128)} custom-call(f32[64,256]{1,0:T(8,128)S(1)} %get-tuple-element.80.keep_ref, f32[64,256]{1,0:T(8,128)S(1)} %collective-permute-done.5.got_ref), custom_call_target="tpu_custom_call" | custom-call | flops 1000000000 | bytes 1048576 | tf_op jit(solution)/shard_map/pallas_call | solution.py:382
  (13 shorter events, 0.0 us)
Async XLA Ops:
  0.6 5.1 %collective-permute-start.1 = (bf16[64,256]{1,0:T(8,128)(2,1)}, bf16[64,256]{1,0:T(8,128)(2,1)S(1)}, u32[]{:S(2)}, u32[]{:S(2)}) collective-permute-start(bf16[64,256]{1,0:T(8,128)(2,1)} %bitcast.15), channel_id=1, source_target_pairs={{0,1},{1,0},{2,3},{3,2},{4,5},{5,4},{6,7},{7,6},{8,9},{9,8},{10,11... | collective-permute-start | bytes 98312 | tf_op jit(solution)/shard_map/ppermute | solution.py:395
  3.7 4.1 %collective-permute-start = (bf16[64,256]{1,0:T(8,128)(2,1)}, bf16[64,256]{1,0:T(8,128)(2,1)S(1)}, u32[]{:S(2)}, u32[]{:S(2)}) collective-permute-start(bf16[64,256]{1,0:T(8,128)(2,1)} %bitcast.10), channel_id=1, source_target_pairs={{0,1},{1,0},{2,3},{3,2},{4,5},{5,4},{6,7},{7,6},{8,9},{9,8},{10,11... | collective-permute-start | bytes 98312 | tf_op jit(solution)/shard_map/ppermute | solution.py:395
  3.7 0.7 %copy-start.6 = (f32[1,256]{1,0:T(1,128)S(1)}, f32[1,256]{1,0:T(1,128)}, u32[]{:S(2)}) copy-start(f32[1,256]{1,0:T(1,128)} %rate_ref.1) | copy-start | bytes 3076
  3.7 0.8 %copy-start.4 = (bf16[256,64]{0,1:T(8,128)(2,1)S(1)}, bf16[256,64]{0,1:T(8,128)(2,1)}, u32[]{:S(2)}) copy-start(bf16[256,64]{0,1:T(8,128)(2,1)} %param.8) | copy-start | bytes 98308
  3.7 0.8 %copy-start.3 = (bf16[256,64]{0,1:T(8,128)(2,1)S(1)}, bf16[256,64]{0,1:T(8,128)(2,1)}, u32[]{:S(2)}) copy-start(bf16[256,64]{0,1:T(8,128)(2,1)} %param.7) | copy-start | bytes 98308
  3.8 0.7 %copy-start.5 = (f32[1,256]{1,0:T(1,128)S(1)}, f32[1,256]{1,0:T(1,128)}, u32[]{:S(2)}) copy-start(f32[1,256]{1,0:T(1,128)} %decay_ref.1) | copy-start | bytes 3076
  5.8 2.0 %copy-start = (bf16[256,128]{1,0:T(8,128)(2,1)S(1)}, bf16[256,128]{1,0:T(8,128)(2,1)}, u32[]{:S(2)}) copy-start(bf16[256,128]{1,0:T(8,128)(2,1)} %g_ref.3) | copy-start | bytes 196612
  7.8 0.8 %copy-start.1 = (bf16[256,128]{1,0:T(8,128)(2,1)S(1)}, bf16[256,128]{1,0:T(8,128)(2,1)}, u32[]{:S(2)}) copy-start(bf16[256,128]{1,0:T(8,128)(2,1)} %v_ref.1) | copy-start | bytes 196612
  7.8 0.9 %copy-start.2 = (f32[1,1,128,128]{3,2,1,0:T(8,128)S(1)}, f32[1,1,128,128]{3,2,1,0:T(8,128)}, u32[]{:S(2)}) copy-start(f32[1,1,128,128]{3,2,1,0:T(8,128)} %param.12) | copy-start | bytes 196612
  8.4 2.9 %collective-permute-start.2 = (f32[256,128]{1,0:T(8,128)S(1)}, f32[256,128]{1,0:T(8,128)S(1)}, u32[]{:S(2)}, u32[]{:S(2)}) collective-permute-start(f32[256,128]{1,0:T(8,128)S(1)} %get-tuple-element.52.own_ref), channel_id=1, source_target_pairs={{0,8},{8,0},{16,24},{24,16},{1,9},{9,1},{17,25},{25,17},{2,10},{10... | collective-permute-start | bytes 393224 | tf_op jit(solution)/shard_map/ppermute | solution.py:395
  9.7 7.4 %collective-permute-start.4 = (f32[64,256]{1,0:T(8,128)S(1)}, f32[64,256]{1,0:T(8,128)S(1)}, u32[]{:S(2)}, u32[]{:S(2)}) collective-permute-start(f32[64,256]{1,0:T(8,128)S(1)} %get-tuple-element.66), channel_id=1, source_target_pairs={{0,1},{1,0},{2,3},{3,2},{4,5},{5,4},{6,7},{7,6},{8,9},{9,8},{10,11... | collective-permute-start | bytes 196616 | tf_op jit(solution)/shard_map/ppermute | solution.py:395
  11.5 4.3 %collective-permute-start.3 = (f32[128,128]{1,0:T(8,128)S(1)}, f32[128,128]{1,0:T(8,128)S(1)}, u32[]{:S(2)}, u32[]{:S(2)}) collective-permute-start(f32[128,128]{1,0:T(8,128)S(1)} %shard_map.105.after_ref), channel_id=1, source_target_pairs={{0,16},{8,24},{16,0},{24,8},{1,17},{9,25},{17,1},{25,9},{2,18},{10... | collective-permute-start | bytes 196616 | tf_op jit(solution)/shard_map/ppermute | solution.py:395
  16.5 4.3 %collective-permute-start.5 = (f32[64,256]{1,0:T(8,128)S(1)}, f32[64,256]{1,0:T(8,128)S(1)}, u32[]{:S(2)}, u32[]{:S(2)}) collective-permute-start(f32[64,256]{1,0:T(8,128)S(1)} %get-tuple-element.81), channel_id=1, source_target_pairs={{0,1},{1,0},{2,3},{3,2},{4,5},{5,4},{6,7},{7,6},{8,9},{9,8},{10,11... | collective-permute-start | bytes 196616 | tf_op jit(solution)/shard_map/ppermute | solution.py:395
